TPU v7x, 32 devices: a whole 2x2x4 slice. The times are simulated.
32 devices in a mesh: fsdp: 8 (over y, x, core), dp: 4 (over z).
Axes of the slice: x: 2, y: 2, z: 4, core: 2. Of those that a mesh axis runs over, the one named last changes fastest.
Arguments:
- tokens: bfloat16 [4096, 1024], P(('fsdp', 'dp')), may hold values from -6 to 6
- segment_ids: int32 [4096], P(('fsdp', 'dp')), may hold values from 0 to 4095, as said below
- cotangent: bfloat16 [4096, 1024], P(('fsdp', 'dp')), may hold values from -6 to 6
- w_in: bfloat16 [1024, 3352], P('fsdp'), may hold values from -0.1875 to 0.1875
- w_q: bfloat16 [1024, 512], P('fsdp'), may hold values from -0.5 to 0.5
- w_k: bfloat16 [1024, 128], P('fsdp'), may hold values from -0.5 to 0.5
- w_v: bfloat16 [1024, 128], P('fsdp'), may hold values from -0.1875 to 0.1875
- w_o: bfloat16 [1024, 512], P('fsdp'), may hold values from -0.5 to 0.5
- w_out: bfloat16 [1024, 1536], P('fsdp'), may hold values from -0.15625 to 0.15625
- w_gate: bfloat16 [1024, 2048], P('fsdp'), may hold values from -0.1875 to 0.1875
- w_up: bfloat16 [1024, 2048], P('fsdp'), may hold values from -0.1875 to 0.1875
- w_down: bfloat16 [1024, 2048], P('fsdp'), may hold values from -0.125 to 0.125
- g_in: float32 [1024], replicated, may hold values from 0.5 to 1.5
- g_ff: float32 [1024], replicated, may hold values from 0.5 to 1.5
- g_mamba: float32 [1536], replicated, may hold values from 0.5 to 1.5
- conv_weight: float32 [4, 1792], replicated, may hold values from -3 to 3
- conv_bias: float32 [1792], replicated, may hold values from -3 to 3
- a_log: float32 [24], replicated, may hold values from 0 to 2.8
- d_skip: float32 [24], replicated, may hold values from 0.5 to 1.5
- dt_bias: float32 [24], replicated, may hold values from -5 to -1
Outputs:
- output: bfloat16 [4096, 1024], P(('fsdp', 'dp'))
- grad_tokens: bfloat16 [4096, 1024], P(('fsdp', 'dp'))
- grad_w_in: float32 [1024, 3352], P('fsdp')
- grad_w_q: float32 [1024, 512], P('fsdp')
- grad_w_k: float32 [1024, 128], P('fsdp')
- grad_w_v: float32 [1024, 128], P('fsdp')
- grad_w_o: float32 [1024, 512], P('fsdp')
- grad_w_out: float32 [1024, 1536], P('fsdp')
- grad_w_gate: float32 [1024, 2048], P('fsdp')
- grad_w_up: float32 [1024, 2048], P('fsdp')
- grad_w_down: float32 [1024, 2048], P('fsdp')
- grad_g_in: float32 [1024], replicated
- grad_g_ff: float32 [1024], replicated
- grad_g_mamba: float32 [1536], replicated
- grad_conv_weight: float32 [4, 1792], replicated
- grad_conv_bias: float32 [1792], replicated
- grad_a_log: float32 [24], replicated
- grad_d_skip: float32 [24], replicated
- grad_dt_bias: float32 [24], replicated
Inputs may be any that keep to these rules, and one draw needn't show every extreme that they name: `segment_ids`: each id is the row of its sequence's first token in the whole array. Within each device's 128 rows the ids do not decrease and the first row starts a sequence, so no sequence crosses the boundary between two devices' rows; the last token of the whole array is a sequence of its own.
All inputs are finite; a program needn't handle non-finite values.
Results may differ from a plain program's by a relative error of at most 0.013.
Values may be sent and summed in bfloat16 or wider, within the bound.
No kernel may reach another device: no remote copies, remote signals or barrier semaphores. Data moves between devices by JAX's collectives and lax.ppermute only.
A program may use at most 256 MiB of HBM per device.

v0:
```python
import jax
import jax.numpy as jnp
from jax import lax
from jax.sharding import PartitionSpec as P

HD = 64
AH = 8
KVH = 2


norm_eps = 1e-05
rope_base = 10000.0
HIGH = lax.Precision.HIGHEST


def rms_norm(values, gain):
    return values * lax.rsqrt(jnp.mean(values * values, -1, keepdims=True) + norm_eps) * gain


def linked_mask(segment_ids):
    count = segment_ids.shape[0]
    row_ids = jnp.arange(count, dtype=jnp.int32)
    return (row_ids[None, :] <= row_ids[:, None]) & (segment_ids[:, None] == segment_ids[None, :])


def seq_position(segment_ids):
    count = segment_ids.shape[0]
    row_ids = jnp.arange(count, dtype=jnp.int32)
    change = jnp.concatenate([jnp.ones((1,), bool), segment_ids[1:] != segment_ids[:-1]])
    starts = lax.cummax(jnp.where(change, row_ids, 0), axis=0)
    return row_ids - starts


def mamba_mix(projected, conv_weight, conv_bias, a_log, d_skip, dt_bias, norm_gain, segment_ids):
    count = projected.shape[0]
    inner_dim = norm_gain.shape[0]
    channels = conv_bias.shape[0]
    state_dim = (channels - inner_dim) // 2
    heads_count = a_log.shape[0]
    head_dim = inner_dim // heads_count
    kernel = conv_weight.shape[0]
    z_part = projected[:, :inner_dim]
    conv_in = projected[:, inner_dim : inner_dim + channels]
    dt_raw = projected[:, inner_dim + channels :]
    conv_out = conv_in * conv_weight[kernel - 1]
    for offset_lag in range(1, kernel):
        shifted = jnp.concatenate(
            [jnp.zeros((offset_lag, channels), jnp.float32), conv_in[:-offset_lag]], 0
        )
        seg_shift = jnp.concatenate(
            [jnp.full((offset_lag,), -1, jnp.int32), segment_ids[:-offset_lag]]
        )
        keep_mask = (seg_shift == segment_ids)[:, None]
        conv_out = (
            conv_out + jnp.where(keep_mask, shifted, 0.0) * conv_weight[kernel - 1 - offset_lag]
        )
    act_conv = jax.nn.silu(conv_out + conv_bias)
    x_heads = act_conv[:, :inner_dim].reshape(count, heads_count, head_dim)
    b_mat = act_conv[:, inner_dim : inner_dim + state_dim]
    c_mat = act_conv[:, inner_dim + state_dim :]
    delta_t = jax.nn.softplus(dt_raw + dt_bias)
    log_decay = -delta_t * jnp.exp(a_log)
    cumulative = jnp.cumsum(log_decay, 0).T
    log_gap = cumulative[:, :, None] - cumulative[:, None, :]
    allowed = linked_mask(segment_ids)[None, :, :]
    decay_w = jnp.where(allowed, jnp.exp(jnp.where(allowed, log_gap, 0.0)), 0.0)
    scores = jnp.dot(c_mat, b_mat.T, precision=HIGH)
    mixer_map = scores[None, :, :] * decay_w * delta_t.T[:, None, :]
    y_heads = (
        jnp.einsum("hts,shd->thd", mixer_map, x_heads, precision=HIGH)
        + d_skip[None, :, None] * x_heads
    )
    gated_out = y_heads.reshape(count, inner_dim) * jax.nn.silu(z_part)
    return rms_norm(gated_out, norm_gain)


def rotate(heads_arr, position):
    half_dim = HD // 2
    frequency = rope_base ** (-jnp.arange(half_dim, dtype=jnp.float32) * 2.0 / HD)
    angles = position.astype(jnp.float32)[:, None] * frequency[None, :]
    cosine = jnp.cos(angles)[:, None, :]
    sine_part = jnp.sin(angles)[:, None, :]
    first = heads_arr[..., :half_dim]
    second = heads_arr[..., half_dim:]
    return jnp.concatenate(
        [first * cosine - second * sine_part, first * sine_part + second * cosine], -1
    )


def attend(q_all, k_all, v_all, segment_ids):
    count = q_all.shape[0]
    position = seq_position(segment_ids)
    q_rot = rotate(q_all.reshape(count, AH, HD), position).reshape(count, KVH, AH // KVH, HD)
    k_rot = rotate(k_all.reshape(count, KVH, HD), position)
    v_heads = v_all.reshape(count, KVH, HD)
    logits = jnp.einsum("tkgd,skd->kgts", q_rot, k_rot, precision=HIGH) * HD ** (-0.5)
    allowed = linked_mask(segment_ids)[None, None, :, :]
    logits = jnp.where(allowed, logits, -1e30)
    top_val = jnp.max(logits, -1, keepdims=True)
    expo = jnp.exp(logits - top_val)
    probs = expo / jnp.sum(expo, -1, keepdims=True)
    return jnp.einsum("kgts,skd->tkgd", probs, v_heads, precision=HIGH).reshape(count, AH * HD)


def mul_t(left, right):
    return lax.dot_general(
        left, right, (((1,), (1,)), ((), ())), preferred_element_type=jnp.float32
    )


def swiglu(gate_in, up_in):
    return jax.nn.silu(gate_in) * up_in


def body(
    tokens,
    segment_ids,
    cotangent,
    w_in,
    w_q,
    w_k,
    w_v,
    w_o,
    w_out,
    w_gate,
    w_up,
    w_down,
    g_in,
    g_ff,
    g_mamba,
    conv_weight,
    conv_bias,
    a_log,
    d_skip,
    dt_bias,
):
    shards = (w_in, w_q, w_k, w_v, w_o, w_out, w_gate, w_up, w_down)
    full_w = (
        lax.all_gather(w_in, "fsdp", axis=0, tiled=True),
        lax.all_gather(w_q, "fsdp", axis=0, tiled=True),
        lax.all_gather(w_k, "fsdp", axis=0, tiled=True),
        lax.all_gather(w_v, "fsdp", axis=0, tiled=True),
        lax.all_gather(w_o, "fsdp", axis=0, tiled=True),
        lax.all_gather(w_out, "fsdp", axis=0, tiled=True),
        lax.all_gather(w_gate, "fsdp", axis=0, tiled=True),
        lax.all_gather(w_up, "fsdp", axis=0, tiled=True),
        lax.all_gather(w_down, "fsdp", axis=0, tiled=True),
    )
    fw_in, fw_q, fw_k, fw_v, fw_o, fw_out, fw_gate, fw_up, fw_down = full_w
    tok32 = tokens.astype(jnp.float32)
    normed32, pull_norm_in = jax.vjp(rms_norm, tok32, g_in)
    normed = normed32.astype(jnp.bfloat16)
    projected = jnp.dot(normed, fw_in, preferred_element_type=jnp.float32)
    queries = jnp.dot(normed, fw_q, preferred_element_type=jnp.float32)
    keys_all = jnp.dot(normed, fw_k, preferred_element_type=jnp.float32)
    values_all = jnp.dot(normed, fw_v, preferred_element_type=jnp.float32)

    def mamba_piece(proj_arg, cw_arg, cb_arg, al_arg, ds_arg, db_arg, gm_arg):
        return mamba_mix(proj_arg, cw_arg, cb_arg, al_arg, ds_arg, db_arg, gm_arg, segment_ids)

    mamba32, pull_mamba = jax.vjp(
        mamba_piece, projected, conv_weight, conv_bias, a_log, d_skip, dt_bias, g_mamba
    )
    mamba_out = mamba32.astype(jnp.bfloat16)

    def attn_piece(q_arg, k_arg, v_arg):
        return attend(q_arg, k_arg, v_arg, segment_ids)

    attn32, pull_attn = jax.vjp(attn_piece, queries, keys_all, values_all)
    attn_out = attn32.astype(jnp.bfloat16)
    mixed = tok32 + mul_t(mamba_out, fw_out) + mul_t(attn_out, fw_o)
    hidden32, pull_norm_ff = jax.vjp(rms_norm, mixed, g_ff)
    hidden_norm = hidden32.astype(jnp.bfloat16)
    gate_pre = jnp.dot(hidden_norm, fw_gate, preferred_element_type=jnp.float32)
    up_pre = jnp.dot(hidden_norm, fw_up, preferred_element_type=jnp.float32)
    act32, pull_ffn = jax.vjp(swiglu, gate_pre, up_pre)
    act_ff = act32.astype(jnp.bfloat16)
    output = (mixed + mul_t(act_ff, fw_down)).astype(jnp.bfloat16)
    bw_in, bw_q, bw_k, bw_v, bw_o, bw_out, bw_gate, bw_up, bw_down = full_w
    d_act = jnp.dot(cotangent, bw_down, preferred_element_type=jnp.float32)
    d_gate32, d_up32 = pull_ffn(d_act)
    d_gate = d_gate32.astype(jnp.bfloat16)
    d_up = d_up32.astype(jnp.bfloat16)
    d_hidden = mul_t(d_gate, bw_gate) + mul_t(d_up, bw_up)
    d_mixed_n, grad_g_ff = pull_norm_ff(d_hidden)
    d_mixed = cotangent.astype(jnp.float32) + d_mixed_n
    d_mixed_b = d_mixed.astype(jnp.bfloat16)
    d_mamba = jnp.dot(d_mixed_b, bw_out, preferred_element_type=jnp.float32)
    d_attn = jnp.dot(d_mixed_b, bw_o, preferred_element_type=jnp.float32)
    d_proj32, grad_cw, grad_cb, grad_al, grad_ds, grad_db, grad_gm = pull_mamba(d_mamba)
    d_q32, d_k32, d_v32 = pull_attn(d_attn)
    d_proj = d_proj32.astype(jnp.bfloat16)
    d_q = d_q32.astype(jnp.bfloat16)
    d_k = d_k32.astype(jnp.bfloat16)
    d_v = d_v32.astype(jnp.bfloat16)
    d_normed = mul_t(d_proj, bw_in) + mul_t(d_q, bw_q) + mul_t(d_k, bw_k) + mul_t(d_v, bw_v)
    d_tok_n, grad_g_in = pull_norm_in(d_normed)
    grad_tokens = (d_mixed + d_tok_n).astype(jnp.bfloat16)
    pairs = (
        (normed, jnp.concatenate([d_proj, d_q, d_k, d_v], 1)),
        (d_mixed_b, jnp.concatenate([attn_out, mamba_out], 1)),
        (hidden_norm, jnp.concatenate([d_gate, d_up], 1)),
        (cotangent, act_ff),
    )
    pieces = []
    for left_op, right_op in pairs:
        pieces.append(
            lax.dot_general(
                left_op, right_op, (((0,), (0,)), ((), ())), preferred_element_type=jnp.float32
            )
        )
    grad_block = lax.psum_scatter(
        jnp.concatenate(pieces, 1), "fsdp", scatter_dimension=0, tiled=True
    )
    grad_block = lax.psum(grad_block.astype(jnp.bfloat16), "dp").astype(jnp.float32)
    split_grads = []
    column = 0
    for shard in shards:
        split_grads.append(grad_block[:, column : column + shard.shape[1]])
        column = column + shard.shape[1]
    small_sum = lax.psum(
        (grad_g_in, grad_g_ff, grad_gm, grad_cw, grad_cb, grad_al, grad_ds, grad_db), ("fsdp", "dp")
    )
    return (
        output,
        grad_tokens,
        split_grads[0],
        split_grads[1],
        split_grads[2],
        split_grads[3],
        split_grads[4],
        split_grads[5],
        split_grads[6],
        split_grads[7],
        split_grads[8],
        small_sum[0],
        small_sum[1],
        small_sum[2],
        small_sum[3],
        small_sum[4],
        small_sum[5],
        small_sum[6],
        small_sum[7],
    )


def solution(mesh):
    in_specs = (
        P(("fsdp", "dp"), None),
        P(("fsdp", "dp")),
        P(("fsdp", "dp"), None),
        P("fsdp", None),
        P("fsdp", None),
        P("fsdp", None),
        P("fsdp", None),
        P("fsdp", None),
        P("fsdp", None),
        P("fsdp", None),
        P("fsdp", None),
        P("fsdp", None),
        P(),
        P(),
        P(),
        P(),
        P(),
        P(),
        P(),
        P(),
    )
    out_specs = (
        P(("fsdp", "dp"), None),
        P(("fsdp", "dp"), None),
        P("fsdp", None),
        P("fsdp", None),
        P("fsdp", None),
        P("fsdp", None),
        P("fsdp", None),
        P("fsdp", None),
        P("fsdp", None),
        P("fsdp", None),
        P("fsdp", None),
        P(),
        P(),
        P(),
        P(),
        P(),
        P(),
        P(),
        P(),
    )
    return jax.shard_map(body, mesh=mesh, in_specs=in_specs, out_specs=out_specs, check_vma=False)
```

profile of v0, /device:TPU:0, one launch (start us, length us, event | category | flops | bytes accessed | tf_op | source)
XLA Modules:
  0.0 999.9 jit_solution(9902658869883574687)
XLA Ops:
  15.9 11.0 %all_gather.30 = bf16[1024,128]{1,0:T(8,128)(2,1)S(1)} all-gather(bf16[128,128]{1,0:T(8,128)(2,1)S(1)} %copy-done.83), channel_id=1, replica_groups=mesh['fsdp'=8,'dp'=4] {'fsdp'}, dimensions={0}, use_global_device_ids=true | all-gather | bytes 294912 | tf_op jit(solution)/shard_map/all_gather | solution.py:141
  26.9 9.6 all_gather.29
  37.8 1.8 fusion.116
  43.0 45.3 %all-gather.8.cloned.1.call-done = bf16[1024,3352]{0,1:T(8,128)(2,1)} async-done(((bf16[128,3352]{0,1:T(8,128)(2,1)}), bf16[1024,3352]{0,1:T(8,128)(2,1)}) %all-gather.8.cloned.1.call-update) | async-done | bytes 6864912 | tf_op jit(solution)/shard_map/all_gather | solution.py:139
  88.3 5.0 fusion.122
  96.5 5.3 fusion.44
  103.1 3.3 fusion.16
  108.0 14.4 %all-gather.10.cloned.1.call-done = bf16[1024,1536]{1,0:T(8,128)(2,1)} async-done(((bf16[128,1536]{1,0:T(8,128)(2,1)}), bf16[1024,1536]{1,0:T(8,128)(2,1)}) %all-gather.10.cloned.1.call-update) | async-done | bytes 3145744 | tf_op jit(solution)/shard_map/all_gather | solution.py:144
  122.4 3.1 convolution_add_fusion.4
  125.5 22.1 %all-gather.14.cloned.1.call-done = bf16[1024,512]{1,0:T(8,128)(2,1)} async-done(((bf16[128,512]{1,0:T(8,128)(2,1)}), bf16[1024,512]{1,0:T(8,128)(2,1)}) %all-gather.14.cloned.1.call-update) | async-done | bytes 1048592 | tf_op jit(solution)/shard_map/all_gather | solution.py:143
  147.6 1.9 multiply_reduce_fusion.14
  150.2 35.7 %all-gather.18.cloned.1.call-done = bf16[1024,2048]{1,0:T(8,128)(2,1)} async-done(((bf16[128,2048]{1,0:T(8,128)(2,1)}), bf16[1024,2048]{1,0:T(8,128)(2,1)}) %all-gather.18.cloned.1.call-update) | async-done | bytes 4194320 | tf_op jit(solution)/shard_map/all_gather | solution.py:146
  185.9 3.9 fusion.133
  189.8 34.5 %all-gather.16.cloned.1.call-done = bf16[1024,2048]{1,0:T(8,128)(2,1)} async-done(((bf16[128,2048]{1,0:T(8,128)(2,1)}), bf16[1024,2048]{1,0:T(8,128)(2,1)}) %all-gather.16.cloned.1.call-update) | async-done | bytes 4194320 | tf_op jit(solution)/shard_map/all_gather | solution.py:145
  224.3 3.9 fusion.132
  228.2 34.6 %all-gather.20.cloned.1.call-done = bf16[1024,2048]{1,0:T(8,128)(2,1)} async-done(((bf16[128,2048]{1,0:T(8,128)(2,1)}), bf16[1024,2048]{1,0:T(8,128)(2,1)}) %all-gather.20.cloned.1.call-update) | async-done | bytes 4194320 | tf_op jit(solution)/shard_map/all_gather | solution.py:147
  262.8 4.9 multiply_convert_fusion
  267.7 1.5 fusion.134
  270.0 2.2 multiply_reduce_fusion.10
  273.6 2.2 multiply_reduce_fusion.7
  275.9 2.2 multiply_reduce_fusion.6
  278.1 4.2 fusion.46
  284.7 1.4 fusion.22
  287.3 1.3 convolution_bitcast_fusion.2
  289.1 4.5 fusion.71
  293.7 8.1 fusion.34
  303.9 3.7 fusion.13
  307.6 2.1 fusion.124
  311.6 4.6 convolution_bitcast_fusion
  318.3 2.4 fusion.23
  320.7 40.1 %pad_maximum_fusion = f32[1024,12312]{0,1:T(8,128)} fusion(f32[1024,2048]{0,1:T(8,128)} %convolution_bitcast_fusion, f32[1024,4096]{0,1:T(8,128)} %fusion.34, f32[1024,2048]{0,1:T(8,128)} %fusion.71, f32[1024,4120]{0,1:T(8,128)S(1)} %fusion.23), kind=kLoop, calls=%fused_computation | loop fusion | flops 37822464 | bytes 100859904 | tf_op jit(solution)/shard_map/concatenate | solution.py:213
  360.8 484.2 %reduce-scatter.2.cloned.1.call-done = f32[128,12312]{0,1:T(8,128)} async-done(((f32[1024,12312]{0,1:T(8,128)}), f32[128,12312]{0,1:T(8,128)}) %reduce-scatter.2.cloned.1.call-update) | async-done | bytes 6303760 | tf_op jit(solution)/shard_map/reduce_scatter | solution.py:212
  845.0 4.4 convert_element_type.107
  851.0 4.4 fusion.135
  855.5 1.4 fusion.65
  856.9 43.4 %all-reduce.22 = (f32[1024]{0:T(1024)}, f32[1024]{0:T(1024)}, f32[1536]{0:T(1024)}, f32[4,1792]{1,0:T(4,128)}, f32[1792]{0:T(1024)}, /*index=5*/f32[24]{0:T(128)}, f32[24]{0:T(128)}, f32[24]{0:T(128)}) all-reduce(f32[1024]{0:T(1024)S(1)} %get-tuple-element.108, ...), channel_id=1, replica_groups=mesh['fsdp'=8,'dp'=4] {'fsdp','dp'}, use_global_device_ids=true, to_apply=%region_21.22 | all-reduce | flops 12616 | bytes 100928 | tf_op jit(solution)/shard_map/psum | solution.py:221
  900.3 1.9 fusion.68
  902.3 4.4 fusion.21
  906.7 64.6 %all-reduce.25.cloned.1.call-done = bf16[128,12312]{0,1:T(8,128)(2,1)} async-done(((bf16[128,12312]{0,1:T(8,128)(2,1)}), bf16[128,12312]{0,1:T(8,128)(2,1)}) %all-reduce.25.cloned.1.call-update) | async-done | bytes 3151888 | tf_op jit(solution)/shard_map/psum | solution.py:215
  973.6 1.7 fusion.130
  975.3 1.9 copy.129
  978.1 1.9 slice.145
  980.0 2.3 copy.130
  982.3 1.7 fusion.129
  984.0 2.5 copy.133
  986.6 2.5 copy.132
  989.1 2.5 copy.131
  991.6 1.3 slice.140
  (347 shorter events, 35.7 us)
Async XLA Ops:
  7.2 4.8 copy-start.86
  7.2 5.6 copy-start.121
  7.2 5.6 copy-start.2
  7.2 7.7 copy-start.85
  7.2 8.7 copy-start.83
  7.2 19.7 %copy-start.84 = (bf16[128,128]{1,0:T(8,128)(2,1)S(1)}, bf16[128,128]{1,0:T(8,128)(2,1)}, u32[]{:S(2)}) copy-start(bf16[128,128]{1,0:T(8,128)(2,1)} %param.26) | copy-start | bytes 98308
  7.3 30.5 %all-gather.12.cloned.1.call-start = ((), (), s32[]{:S(2)}) async-start(), calls=%async_computation.3 | async-start | bytes 1179648 | tf_op jit(solution)/shard_map/all_gather | solution.py:140
  8.0 29.0 %copy-start.36 = (f32[1024]{0:T(1024)S(1)}, f32[1024]{0:T(1024)}, u32[]{:S(2)}) copy-start(f32[1024]{0:T(1024)} %param.32) | copy-start | bytes 12292
  8.0 80.3 %all-gather.8.cloned.1.call-start = ((), (), s32[]{:S(2)}) async-start(), calls=%async_computation.1 | async-start | bytes 7723008 | tf_op jit(solution)/shard_map/all_gather | solution.py:139
  8.7 113.7 %all-gather.10.cloned.1.call-start = ((), (), s32[]{:S(2)}) async-start(), calls=%async_computation.2 | async-start | bytes 3538944 | tf_op jit(solution)/shard_map/all_gather | solution.py:144
  9.5 138.1 %all-gather.14.cloned.1.call-start = ((), (), s32[]{:S(2)}) async-start(), calls=%async_computation.4 | async-start | bytes 1179648 | tf_op jit(solution)/shard_map/all_gather | solution.py:143
  10.1 175.9 %all-gather.18.cloned.1.call-start = ((), (), s32[]{:S(2)}) async-start(), calls=%async_computation.6 | async-start | bytes 4718592 | tf_op jit(solution)/shard_map/all_gather | solution.py:146
  10.6 213.6 %all-gather.16.cloned.1.call-start = ((), (), s32[]{:S(2)}) async-start(), calls=%async_computation.5 | async-start | bytes 4718592 | tf_op jit(solution)/shard_map/all_gather | solution.py:145
  11.2 251.6 %all-gather.20.cloned.1.call-start = ((), (), s32[]{:S(2)}) async-start(), calls=%async_computation.7 | async-start | bytes 4718592 | tf_op jit(solution)/shard_map/all_gather | solution.py:147
  12.0 833.0 %reduce-scatter.2.cloned.1.call-start = ((), (), s32[]{:S(2)}) async-start(), calls=%async_computation.8 | async-start | bytes 56733696 | tf_op jit(solution)/shard_map/reduce_scatter | solution.py:212
  12.8 24.0 %copy-start.70 = (pred[128,128]{1,0:T(8,128)(4,1)}, pred[128,128]{1,0:T(8,128)(4,1)S(1)}, u32[]{:S(2)}) copy-start(pred[128,128]{1,0:T(8,128)(4,1)S(1)} %get-tuple-element.160) | copy-start | bytes 49156
  12.8 82.6 %copy-start.106 = (f32[24]{0:T(128)}, f32[24]{0:T(128)S(1)}, u32[]{:S(2)}) copy-start(f32[24]{0:T(128)S(1)} %exp.34) | copy-start | bytes 292
  13.0 26.7 %copy-start.109 = (f32[128]{0:T(128)}, f32[128]{0:T(128)S(1)}, u32[]{:S(2)}) copy-start(f32[128]{0:T(128)S(1)} %fusion.69) | copy-start | bytes 1540
  13.1 24.6 %copy-start.96 = (pred[128]{0:T(512)(128)(4,1)}, pred[128]{0:T(512)(128)(4,1)S(1)}, u32[]{:S(2)}) copy-start(pred[128]{0:T(512)(128)(4,1)S(1)} %get-tuple-element.161) | copy-start | bytes 388
  13.1 24.7 %copy-start.98 = (pred[128]{0:T(512)(128)(4,1)}, pred[128]{0:T(512)(128)(4,1)S(1)}, u32[]{:S(2)}) copy-start(pred[128]{0:T(512)(128)(4,1)S(1)} %get-tuple-element.162) | copy-start | bytes 388
  13.1 24.7 %copy-start.100 = (pred[128]{0:T(512)(128)(4,1)}, pred[128]{0:T(512)(128)(4,1)S(1)}, u32[]{:S(2)}) copy-start(pred[128]{0:T(512)(128)(4,1)S(1)} %get-tuple-element.163) | copy-start | bytes 388
  15.7 26.1 %copy-start.41 = (pred[128,128]{0,1:T(8,128)(4,1)}, pred[128,128]{0,1:T(8,128)(4,1)S(1)}, u32[]{:S(2)}) copy-start(pred[128,128]{0,1:T(8,128)(4,1)S(1)} %copy.113) | copy-start | bytes 49156
  26.9 12.8 %copy-start.34 = (bf16[1024,128]{1,0:T(8,128)(2,1)}, bf16[1024,128]{1,0:T(8,128)(2,1)S(1)}, u32[]{:S(2)}) copy-start(bf16[1024,128]{1,0:T(8,128)(2,1)S(1)} %all_gather.30) | copy-start | bytes 786436
  36.8 51.5 %copy-start.75 = (f32[128]{0:T(128)}, f32[128]{0:T(128)S(1)}, u32[]{:S(2)}) copy-start(f32[128]{0:T(128)S(1)} %fusion.97) | copy-start | bytes 1540
  37.7 5.3 copy-start.68
  93.4 8.4 copy-start.11
  96.4 6.6 copy-start.89
  96.4 6.6 copy-start.71
  96.4 6.7 copy-start.91
  96.5 6.6 copy-start.119
  108.0 17.5 %copy-start.20 = (bf16[128,1536]{0,1:T(8,128)(2,1)}, bf16[128,1536]{0,1:T(8,128)(2,1)S(1)}, u32[]{:S(2)}) copy-start(bf16[128,1536]{0,1:T(8,128)(2,1)S(1)} %multiply_convert_fusion.2) | copy-start | bytes 1179652
  149.5 119.8 %copy-start.3 = (f32[128,1024]{1,0:T(8,128)}, f32[128,1024]{1,0:T(8,128)S(1)}, u32[]{:S(2)}) copy-start(f32[128,1024]{1,0:T(8,128)S(1)} %get-tuple-element.167) | copy-start | bytes 1572868
  150.1 35.9 %copy-start.102 = (f32[128]{0:T(128)}, f32[128]{0:T(128)S(1)}, u32[]{:S(2)}) copy-start(f32[128]{0:T(128)S(1)} %fusion.99) | copy-start | bytes 1540
  150.2 74.1 %copy-start.16 = (bf16[128,1024]{1,0:T(8,128)(2,1)}, bf16[128,1024]{1,0:T(8,128)(2,1)S(1)}, u32[]{:S(2)}) copy-start(bf16[128,1024]{1,0:T(8,128)(2,1)S(1)} %multiply_convert_fusion.3) | copy-start | bytes 786436
  189.8 73.0 %copy-start.29 = (bf16[128,1024]{1,0:T(8,128)(2,1)S(1)}, bf16[128,1024]{1,0:T(8,128)(2,1)}, u32[]{:S(2)}) copy-start(bf16[128,1024]{1,0:T(8,128)(2,1)} %param.22) | copy-start | bytes 786436
  262.8 4.9 copy-start
  278.1 6.0 copy-start.15
  293.6 10.0 %copy-start.44 = (f32[128,32]{0,1:T(8,128)S(1)}, f32[128,32]{0,1:T(8,128)}, u32[]{:S(2)}) copy-start(f32[128,32]{0,1:T(8,128)} %copy-done.43) | copy-start | bytes 49156
  293.6 10.0 %copy-start.46 = (f32[128,32]{0,1:T(8,128)S(1)}, f32[128,32]{0,1:T(8,128)}, u32[]{:S(2)}) copy-start(f32[128,32]{0,1:T(8,128)} %copy-done.45) | copy-start | bytes 49156
  293.6 10.2 %copy-start.53 = (f32[128,2,64]{0,2,1:T(8,128)S(1)}, f32[128,2,64]{0,2,1:T(8,128)}, u32[]{:S(2)}) copy-start(f32[128,2,64]{0,2,1:T(8,128)} %convolution_bitcast_fusion.2) | copy-start | bytes 196612
  293.6 10.2 %copy-start.73 = (pred[128,128]{1,0:T(8,128)(4,1)S(1)}, pred[128,128]{1,0:T(8,128)(4,1)}, u32[]{:S(2)}) copy-start(pred[128,128]{1,0:T(8,128)(4,1)} %copy-done.70) | copy-start | bytes 49156
  293.6 10.2 %copy-start.120 = (f32[24]{0:T(128)S(1)}, f32[24]{0:T(128)}, u32[]{:S(2)}) copy-start(f32[24]{0:T(128)} %param.38) | copy-start | bytes 292
  311.6 5.4 copy-start.59
  360.8 610.6 %all-reduce.25.cloned.1.call-start = ((), (), s32[]{:S(2)}) async-start(), calls=%async_computation.9 | async-start | bytes 6303744 | tf_op jit(solution)/shard_map/psum | solution.py:215
  855.5 44.9 %copy-start.110 = (f32[128]{0:T(128)S(1)}, f32[128]{0:T(128)}, u32[]{:S(2)}) copy-start(f32[128]{0:T(128)} %copy-done.109) | copy-start | bytes 1540
  855.5 46.8 %copy-start.4 = (f32[128,1024]{1,0:T(8,128)S(1)}, f32[128,1024]{1,0:T(8,128)}, u32[]{:S(2)}) copy-start(f32[128,1024]{1,0:T(8,128)} %copy-done.3) | copy-start | bytes 1572868
  855.5 46.8 %copy-start.26 = (bf16[128,2048]{1,0:T(8,128)(2,1)S(1)}, bf16[128,2048]{1,0:T(8,128)(2,1)}, u32[]{:S(2)}) copy-start(bf16[128,2048]{1,0:T(8,128)(2,1)} %get-tuple-element.143) | copy-start | bytes 1572868
  975.3 7.0 copy-start.5
  (84 other events, 204.5 us)
Sparse Core Ops, SparseCore 0:
  9.9 26.9 all-gather.11
  38.8 49.4 all-gather.7
  90.2 32.2 all-gather.9
  124.2 23.3 all-gather.13
  149.3 36.5 all-gather.17
  187.7 36.5 all-gather.15
  226.2 36.5 all-gather.19
  360.9 484.0 reduce-scatter.1
  849.6 121.6 all-reduce.24
where the time goes:
time: 1010 us; the launch traced here: 1000 us
  waiting for transfers between devices  740 us (73%)
  matrix products  80.9 us (8%)
  other arithmetic  65.8 us (7%)
  blocking collectives  64 us (6%)
  local copies, waits for them, and re-layouts  33.1 us (3%)
  between operations  16 us (2%)
    reduce_scatter x1, waiting for transfers between devices, body(): lax.psum_scatter(jnp.concatenate(pieces, 1), 'fsdp', scatter_dimension=0,...  484 us
    psum x1, waiting for transfers between devices, body(): lax.psum(grad_block.astype(jnp.bfloat16), 'dp').astype(jnp.float32)  64.6 us
    all_gather x1, waiting for transfers between devices, body(): lax.all_gather(w_in, 'fsdp', axis=0, tiled=True)  45.3 us
    psum x1, blocking collectives, body(): lax.psum((grad_g_in, grad_g_ff, grad_gm, grad_cw, grad_cb, grad_al, grad_...  43.4 us
    concatenate x1, other arithmetic, body(): jnp.concatenate(pieces, 1)  40.1 us
    all_gather x1, waiting for transfers between devices, body(): lax.all_gather(w_up, 'fsdp', axis=0, tiled=True)  35.7 us
    all_gather x1, waiting for transfers between devices, body(): lax.all_gather(w_down, 'fsdp', axis=0, tiled=True)  34.6 us
    all_gather x1, waiting for transfers between devices, body(): lax.all_gather(w_gate, 'fsdp', axis=0, tiled=True)  34.5 us
  transfers between devices with their start and end apart: 9, of which 8 were waited for; matrix products, arithmetic and copies ran while one was open for 5% of the time, Pallas kernels for 0%

commit v1 on v0

v1 whole, which is shorter than its diff:
```python
import functools
import math

import jax
import jax.numpy as jnp
from jax import lax
from jax.experimental import pallas as pl
from jax.experimental.pallas import tpu as pltpu
from jax.sharding import PartitionSpec as P


HD = 64
norm_eps = 1e-05
rope_base = 10000.0
HIGH = lax.Precision.HIGHEST
BF = jnp.bfloat16
F32 = jnp.float32


def mm(left, right):
    return jnp.dot(left, right, preferred_element_type=F32)


def mul_t(left, right):
    return lax.dot_general(left, right, (((1,), (1,)), ((), ())), preferred_element_type=F32)


def t_mul(left, right):
    return lax.dot_general(left, right, (((0,), (0,)), ((), ())), preferred_element_type=F32)


def cols(w, start, size):
    return lax.dynamic_slice(w, (0, start), (w.shape[0], size))


tie = lax.optimization_barrier


def next_peer(x):
    n = lax.axis_size("dp")
    return lax.ppermute(x, "dp", [(i, (i + 1) % n) for i in range(n)])


def peer_blocks(x):
    blocks = [x]
    for _ in range(lax.axis_size("dp") - 1):
        blocks.append(next_peer(blocks[-1]))
    return blocks


def peer_rows(x):
    return jnp.concatenate(peer_blocks(x), 0)


def peer_direct(x):
    n = lax.axis_size("dp")
    return [x] + [
        lax.ppermute(x, "dp", [(i, (i + k) % n) for i in range(n)]) for k in range(n - 1, 0, -1)
    ][::-1]


def flip(x, bits):
    size = lax.axis_size("fsdp")
    return lax.ppermute(x, "fsdp", [(i, i ^ bits) for i in range(size)])


def is_cube(width):
    return lax.axis_size("fsdp") == 8 and width % 1024 == 0


ORDER = (0, 2, 4, 6, 1, 3, 5, 7)


def gather_start(w):
    return [w] + [flip(w, m) for m in ORDER[1:4]]


def scatter_first(pairs):
    height = pairs[0][0].shape[1]
    return flip(grads(pairs, height // 2, height), 1)


def scatter_own(pairs, got):
    return grads(pairs, 0, pairs[0][0].shape[1] // 2, add=got, blocks=4)


def scatter_rest(own):
    return [own[0]] + [flip(own[i], ORDER[i]) for i in range(1, 4)]


def add_up(parts):
    total = parts[0].astype(F32)
    for p in parts[1:]:
        total = total + p.astype(F32)
    return total


def grad_kernel(count, add, blocks, *refs):
    total = []
    for left, right in zip(refs[:count], refs[count : 2 * count]):
        total.append(t_mul(left[...], right[...]))
    total = jnp.concatenate(total, 1)
    outs = refs[2 * count :]
    if add:
        total = total + outs[0][...].astype(F32)
        outs = outs[1:]
    total = total.astype(BF)
    if blocks == 1:
        outs[0][...] = total
        return
    for i in range(blocks):

        @pl.when(pl.program_id(0) == i)
        def _():
            outs[i][...] = total


def grads(pairs, low, high, add=None, blocks=1):
    depth = pairs[0][0].shape[0]
    height = high - low
    width = sum(r.shape[1] for _, r in pairs)
    rows = min(height, 256) if blocks == 1 else height // blocks
    first = low // rows
    if blocks == 1:
        out_shape = [jax.ShapeDtypeStruct((height, width), BF)]
        out_specs = [pl.BlockSpec((rows, width), lambda i: (i, 0))]
    else:
        out_shape = [jax.ShapeDtypeStruct((rows, width), BF)] * blocks
        out_specs = [pl.BlockSpec((rows, width), lambda i: (0, 0))] * blocks
    out = pl.pallas_call(
        functools.partial(grad_kernel, len(pairs), add is not None, blocks),
        out_shape=out_shape,
        grid=(height // rows,),
        in_specs=[pl.BlockSpec((depth, rows), lambda i: (0, i + first))] * len(pairs)
        + [pl.BlockSpec((depth, r.shape[1]), lambda i: (0, 0)) for _, r in pairs]
        + ([] if add is None else [pl.BlockSpec((rows, width), lambda i: (i, 0))]),
        out_specs=out_specs,
        cost_estimate=pl.CostEstimate(
            flops=2 * depth * height * width,
            bytes_accessed=2 * (depth * (height * len(pairs) + width) + height * width),
            transcendentals=0,
        ),
    )(*[l for l, _ in pairs], *[r for _, r in pairs], *([] if add is None else [add]))
    return out[0] if blocks == 1 else out


def reorder_kernel(back, count, at_ref, *refs):
    at = at_ref[0]
    for x_ref, o_ref in zip(refs[:count], refs[count:]):
        size = x_ref.shape[1] // 8
        for i, m in enumerate(ORDER):
            there = pl.ds(pl.multiple_of((at ^ m) * size, 128), size)
            here = pl.ds(i * size, size)
            if back:
                o_ref[:, there] = x_ref[:, here]
            else:
                o_ref[:, here] = x_ref[:, there]


def reorder(arrays, back=False):
    at = lax.axis_index("fsdp").astype(jnp.int32).reshape(1)
    vmem = pl.BlockSpec(memory_space=pltpu.VMEM)
    return pl.pallas_call(
        functools.partial(reorder_kernel, back, len(arrays)),
        out_shape=[jax.ShapeDtypeStruct(a.shape, a.dtype) for a in arrays],
        in_specs=[pl.BlockSpec(memory_space=pltpu.SMEM)] + [vmem] * len(arrays),
        out_specs=[vmem] * len(arrays),
    )(at, *arrays)


def lay_kernel(plan, n, kv_of, rank_ref, *refs):
    blocks, outs = refs[:n], refs[n:]
    rank = rank_ref[0]
    for kind, src, size, out, base in plan:
        o_ref = outs[out]
        if kind == "slice":
            for k in range(n):
                owner = lax.rem(rank - k + n, n)
                there = pl.ds(pl.multiple_of(base + owner * size, 128), size)
                o_ref[:, there] = blocks[k][:, src : src + size].astype(F32)
        elif kind == "sum":
            total = blocks[0][:, src : src + size].astype(F32)
            for k in range(1, n):
                total += blocks[k][:, src : src + size].astype(F32)
            o_ref[:, base : base + size] = total
        elif kind == "kv":
            heads = o_ref.shape[1] // size
            pieces = [jnp.zeros((o_ref.shape[0], size), F32)] * heads
            for k in range(n):
                owner = lax.rem(rank - k + n, n)
                value = blocks[k][:, src : src + size].astype(F32)
                for h in range(heads):
                    pieces[h] = pieces[h] + jnp.where(kv_of(owner) == h, value, 0.0)
            o_ref[...] = jnp.concatenate(pieces, 1)
        else:
            value = [blocks[k][:, src : src + size].astype(F32) for k in range(n)]
            for p in range(n):
                total = jnp.zeros_like(value[0])
                for k in range(n):
                    owner = lax.rem(rank - k + n, n)
                    total = jnp.where(owner == p, value[k], total)
                o_ref[:, base + p * size : base + (p + 1) * size] = total


def lay(blocks, plan, widths, kv_of):
    n = len(blocks)
    rank = lax.axis_index("dp").astype(jnp.int32).reshape(1)
    vmem = pl.BlockSpec(memory_space=pltpu.VMEM)
    return pl.pallas_call(
        functools.partial(lay_kernel, plan, n, kv_of),
        out_shape=[jax.ShapeDtypeStruct((blocks[0].shape[0], w), F32) for w in widths],
        in_specs=[pl.BlockSpec(memory_space=pltpu.SMEM)] + [vmem] * n,
        out_specs=[vmem] * len(widths),
    )(rank, *blocks)


def peer_send(blocks):
    n = lax.axis_size("dp")
    return [blocks[0]] + [
        lax.ppermute(blocks[k], "dp", [(i, (i - k) % n) for i in range(n)])
        for k in range(n - 1, 0, -1)
    ]


def peer_scalar_sum(v):
    n = lax.axis_size("dp")
    total = v
    for m in range(1, n):
        got = lax.ppermute(v, "dp", [(i, (i - m) % n) for i in range(n)])
        total = total + jnp.roll(got, -m, 0)
    return total


def sum_level(values):
    while len(values) > 1:
        values = [values[i] + values[i + 1] for i in range(0, len(values), 2)]
    return values[0]


def sum_dp(v):
    n = lax.axis_size("dp")
    if n & (n - 1):
        return lax.psum(v, "dp")
    got = [lax.ppermute(v, "dp", [(i, i ^ m) for i in range(n)]) for m in range(1, n)]
    return sum_level([v] + got)


def sum_fsdp(v):
    n, step = lax.axis_size("fsdp"), 1
    if n & (n - 1):
        return lax.psum(v, "fsdp")
    while step < n:
        v = v + lax.ppermute(v, "fsdp", [(i, i ^ step) for i in range(n)])
        step *= 2
    return v


def transposed(m):
    return jnp.swapaxes(m, 0, 1)


def column(row):
    size = row.shape[1]
    return transposed(jnp.broadcast_to(row, (size, size)))


def exact(a, b, dims):
    return lax.dot_general(a, b, (dims, ((), ())), precision=HIGH, preferred_element_type=F32)


def quick(a, b, dims):
    return lax.dot_general(
        a.astype(BF), b.astype(BF), (dims, ((), ())), preferred_element_type=F32
    )


NN, NT, TN = ((1,), (0,)), ((1,), (1,)), ((0,), (0,))


def shift_down(x, lag):
    return jnp.concatenate([jnp.zeros((lag, x.shape[1]), x.dtype), x[: x.shape[0] - lag]], 0)


def shift_up(x, lag):
    return jnp.concatenate([x[lag:], jnp.zeros((lag, x.shape[1]), x.dtype)], 0)


def branch_common(start, proj, conv_p, head_p, sizes):
    rows, inner, both, _ = sizes
    t_col = lax.broadcasted_iota(jnp.int32, (rows, rows), 0)
    s_row = lax.broadcasted_iota(jnp.int32, (rows, rows), 1)
    start_t = start.astype(F32)
    keep = (start_t == transposed(start_t)) & (s_row <= t_col)
    first = start_t[:, :1].astype(jnp.int32)
    t_one = t_col[:, :1]
    conv_in = proj[:, inner : 2 * inner + both]
    conv = conv_in * conv_p[3:4]
    lagged = []
    for lag in range(1, 4):
        ok = t_one - lag >= first
        moved = jnp.where(ok, shift_down(conv_in, lag), 0.0)
        lagged.append((ok, moved))
        conv = conv + moved * conv_p[3 - lag : 4 - lag]
    pre = conv + conv_p[4:5]
    gate = jax.nn.sigmoid(pre)
    act = pre * gate
    x, b, c = act[:, :inner], act[:, inner : inner + both // 2], act[:, inner + both // 2 :]
    dt = proj[:, proj.shape[1] - 128 :] + head_p[2:3]
    delta = jnp.maximum(dt, 0.0) + jnp.log1p(jnp.exp(-jnp.abs(dt)))
    decay_log = -delta * jnp.exp(head_p[0:1])
    lower = (s_row <= t_col).astype(F32)
    cum = exact(lower, decay_log, NN)
    cum_t, delta_t = transposed(cum), transposed(delta)
    scores = exact(c, b, NT)

    def head_decay(h):
        gap = cum[:, h : h + 1] - cum_t[h : h + 1]
        return jnp.where(keep, jnp.exp(jnp.where(keep, gap, 0.0)), 0.0)

    return dict(
        t_col=t_col, s_row=s_row, keep=keep, first=first, t_one=t_one, conv_in=conv_in,
        lagged=lagged, pre=pre, gate=gate, x=x, b=b, c=c, dt=dt, delta=delta,
        decay_log=decay_log, lower=lower, delta_t=delta_t, scores=scores, head_decay=head_decay,
    )


def swap_halves(x):
    lane = lax.broadcasted_iota(jnp.int32, x.shape, 1)
    size, half = x.shape[1], HD // 2
    low = lane % HD < half
    return jnp.where(low, pltpu.roll(x, size - half, 1), pltpu.roll(x, half, 1))


def rotary(first, rows):
    lane = lax.broadcasted_iota(jnp.int32, (rows, 128), 1)
    t = lax.broadcasted_iota(jnp.int32, (rows, 128), 0)
    half = HD // 2
    frequency = jnp.exp((lane % half).astype(F32) * (-2.0 / HD * math.log(rope_base)))
    angle = (t - first).astype(F32) * frequency
    return jnp.cos(angle), jnp.where(lane % HD < half, -jnp.sin(angle), jnp.sin(angle))


def attn_common(q, kv, first, keep):
    rows = q.shape[0]
    lane = lax.broadcasted_iota(jnp.int32, (rows, 128), 1)
    low = lane < HD
    cosine, sine = rotary(first, rows)
    q_rot = q * cosine + swap_halves(q) * sine
    k_rot = kv * cosine + swap_halves(kv) * sine
    keys = jnp.where(low, k_rot, pltpu.roll(k_rot, HD, 1))
    values = jnp.where(low, pltpu.roll(kv, HD, 1), kv)
    probs, picks = [], []
    for h in range(2):
        pick = low if h == 0 else ~low
        logits = exact(jnp.where(pick, q_rot, 0.0), keys, NT) * HD ** (-0.5)
        logits = jnp.where(keep, logits, -1e30)
        expo = jnp.exp(logits - jnp.max(logits, -1, keepdims=True))
        probs.append(expo / jnp.sum(expo, -1, keepdims=True))
        picks.append(pick)
    return low, cosine, sine, q_rot, keys, values, probs, picks


def branch_forward(
    sizes, q_at, x_ref, a0_ref, a1_ref, g_ref, conv_ref, head_ref,
    normed_ref, proj_ref, y_ref, gated_ref, square_ref, attn_ref,
):
    rows, inner, _, heads = sizes
    width = g_ref.shape[1]
    x32 = x_ref[:, :width].astype(F32)
    scale = lax.rsqrt(jnp.mean(x32 * x32, -1, keepdims=True) + norm_eps)
    normed = (x32 * scale * g_ref[...]).astype(BF)
    normed_ref[...] = normed
    half = a0_ref.shape[0]
    proj = mm(normed[:, :half], a0_ref[...]) + mm(normed[:, half:], a1_ref[...])
    proj_ref[...] = proj
    start = x_ref[:, width:]
    conv_p, head_p = conv_ref[...], head_ref[...]
    v = branch_common(start, proj, conv_p, head_p, sizes)
    low = v["s_row"] < HD
    outs = []
    for pair in range(heads // 2):
        x_pair = v["x"][:, pair * 128 : pair * 128 + 128]
        y = []
        for h in (2 * pair, 2 * pair + 1):
            mixer = v["scores"] * v["head_decay"](h) * v["delta_t"][h : h + 1]
            y.append(quick(mixer, x_pair, NN))
        outs.append(jnp.where(low, y[0], y[1]))
    y = jnp.concatenate(outs, 1) + conv_p[5:6, :inner] * v["x"]
    z = proj[:, :inner]
    gated = y * (z * jax.nn.sigmoid(z))
    y_ref[...] = y
    gated_ref[...] = gated
    square = jnp.sum(gated * gated, -1, keepdims=True)
    square_ref[0] = transposed(jnp.broadcast_to(square, (rows, rows)))[:1]
    q, kv = proj[:, q_at : q_at + 128], proj[:, q_at + 128 : q_at + 256]
    low, _, _, _, _, values, probs, _ = attn_common(q, kv, v["first"], v["keep"])
    out = [quick(p, values, NN) for p in probs]
    attn_ref[...] = jnp.where(low, out[0], out[1]).astype(BF)


def branch_back_out(
    sizes, low, dm_ref, b0_ref, b1_ref, gated_ref, scale_ref, gm_ref,
    d_scaled_ref, d_attn_ref, inner_ref, g_gm_ref,
):
    rows, inner, _, _ = sizes
    d_mix = halved(dm_ref[...], b0_ref[:, low:], b1_ref[:, low:])
    d_out = d_mix[:, :inner]
    gated = gated_ref[...]
    scale = column(scale_ref[0])[:, :1]

    @pl.when(pl.program_id(0) == 0)
    def _():
        g_gm_ref[...] = jnp.zeros_like(g_gm_ref)

    g_gm_ref[...] += jnp.sum(d_out * gated * scale, 0, keepdims=True)
    d_scaled = d_out * gm_ref[...]
    d_scaled_ref[...] = d_scaled
    dot = jnp.sum(d_scaled * gated, -1, keepdims=True)
    inner_ref[0] = transposed(jnp.broadcast_to(dot, (rows, rows)))[:1]
    d_attn_ref[...] = d_mix[:, inner:]


def branch_back_attn(q_at, x_ref, proj_ref, d_attn_ref, d_qkv_ref):
    start = x_ref[...].astype(F32)
    rows = start.shape[0]
    t_col = lax.broadcasted_iota(jnp.int32, (rows, rows), 0)
    s_row = lax.broadcasted_iota(jnp.int32, (rows, rows), 1)
    keep = (start == transposed(start)) & (s_row <= t_col)
    first = start[:, :1].astype(jnp.int32)
    q = proj_ref[:, q_at : q_at + 128]
    kv = proj_ref[:, q_at + 128 : q_at + 256]
    low, cosine, sine, q_rot, keys, values, probs, picks = attn_common(q, kv, first, keep)
    d_attn = d_attn_ref[...]
    d_q = []
    d_k = jnp.zeros((rows, 128), F32)
    d_v = jnp.zeros((rows, 128), F32)
    for p, pick in zip(probs, picks):
        d_head = jnp.where(pick, d_attn, 0.0)
        d_p = quick(d_head, values, NT)
        d_logit = p * (d_p - jnp.sum(d_p * p, -1, keepdims=True)) * HD ** (-0.5)
        d_q.append(quick(d_logit, keys, NN))
        d_k += quick(d_logit, jnp.where(pick, q_rot, 0.0), TN)
        d_v += quick(p, d_head, TN)
    d_q = jnp.where(low, d_q[0], d_q[1])
    d_k = d_k + pltpu.roll(d_k, HD, 1)
    d_v = d_v + pltpu.roll(d_v, HD, 1)
    d_q = d_q * cosine + swap_halves(d_q * sine)
    d_k = d_k * cosine + swap_halves(d_k * sine)
    d_qkv_ref[:, :128] = d_q.astype(BF)
    d_qkv_ref[:, 128:] = jnp.where(low, d_k, d_v).astype(BF)


def branch_back_mamba(
    sizes, q_at, x_ref, proj_ref, y_ref, gated_ref, d_scaled_ref, scale_ref, inner_ref,
    d_qkv_ref, conv_ref, head_ref, whole,
    d_proj_ref, g_conv_ref, g_head_ref, g_skip_ref,
):
    rows, inner, both, heads = sizes

    @pl.when(pl.program_id(0) == 0)
    def _():
        g_conv_ref[...] = jnp.zeros_like(g_conv_ref)
        g_head_ref[...] = jnp.zeros_like(g_head_ref)
        g_skip_ref[...] = jnp.zeros_like(g_skip_ref)

    proj = proj_ref[...]
    conv_p, head_p = conv_ref[...], head_ref[...]
    v = branch_common(x_ref[...], proj, conv_p, head_p, sizes)
    scale = column(scale_ref[0])[:, :1]
    dot = column(inner_ref[0])[:, :1]
    d_gated = scale * d_scaled_ref[...] - gated_ref[...] * (scale * scale * scale * dot / whole)
    z = proj[:, :inner]
    zs = jax.nn.sigmoid(z)
    d_y = d_gated * (z * zs)
    d_z = d_gated * y_ref[...] * (zs * (1.0 + z * (1.0 - zs)))
    d_proj_ref[:, :inner] = d_z.astype(BF)
    x, scores, delta_t = v["x"], v["scores"], v["delta_t"]
    g_skip_ref[...] += jnp.sum(d_y * x, 0, keepdims=True)
    low = v["s_row"] < HD
    d_x = []
    d_scores = jnp.zeros((rows, rows), F32)
    d_cum = jnp.zeros((rows, rows), F32)
    d_delta_rows, d_cum_rows = [], []
    for pair in range(heads // 2):
        at = slice(pair * 128, pair * 128 + 128)
        x_pair, dy_pair = x[:, at], d_y[:, at]
        parts = []
        for h in (2 * pair, 2 * pair + 1):
            pick = low if h % 2 == 0 else ~low
            decay = v["head_decay"](h)
            scored = scores * decay
            mixer = scored * delta_t[h : h + 1]
            d_mixer = quick(jnp.where(pick, dy_pair, 0.0), x_pair, NT)
            parts.append(quick(mixer, dy_pair, TN))
            d_scores += d_mixer * (decay * delta_t[h : h + 1])
            d_delta_rows.append(jnp.sum(d_mixer * scored, 0, keepdims=True))
            flow = d_mixer * mixer
            d_cum_rows.append(jnp.sum(flow, 0, keepdims=True))
            d_cum = jnp.where(v["s_row"] == h, jnp.sum(flow, -1, keepdims=True), d_cum)
        d_x.append(jnp.where(low, parts[0], parts[1]))
    blank = jnp.zeros((rows - heads, rows), F32)
    d_delta = transposed(jnp.concatenate(d_delta_rows + [blank], 0))
    d_cum = d_cum - transposed(jnp.concatenate(d_cum_rows + [blank], 0))
    d_log = exact(v["lower"], d_cum, TN)
    d_delta = d_delta - jnp.exp(head_p[0:1]) * d_log
    d_dt = d_delta * jax.nn.sigmoid(v["dt"])
    g_head_ref[0:1] += jnp.sum(d_log * v["decay_log"], 0, keepdims=True)
    g_head_ref[1:2] += jnp.sum(d_dt, 0, keepdims=True)
    d_proj_ref[:, d_proj_ref.shape[1] - 128 :] = d_dt.astype(BF)
    d_act = jnp.concatenate(
        d_x + [quick(d_scores, v["c"], TN), quick(d_scores, v["b"], NN)], 1
    )
    d_act = jnp.concatenate(
        [d_act[:, :inner] + conv_p[5:6, :inner] * d_y, d_act[:, inner:]], 1
    )
    gate = v["gate"]
    d_conv = d_act * (gate * (1.0 + v["pre"] * (1.0 - gate)))
    g_conv_ref[4:5] += jnp.sum(d_conv, 0, keepdims=True)
    g_conv_ref[3:4] += jnp.sum(d_conv * v["conv_in"], 0, keepdims=True)
    d_in = d_conv * conv_p[3:4]
    for lag, (ok, moved) in zip(range(1, 4), v["lagged"]):
        g_conv_ref[3 - lag : 4 - lag] += jnp.sum(d_conv * moved, 0, keepdims=True)
        back = shift_up(jnp.where(ok, d_conv, 0.0), lag)
        d_in = d_in + back * conv_p[3 - lag : 4 - lag]
    d_proj_ref[:, inner : 2 * inner + both] = d_in.astype(BF)
    d_proj_ref[:, q_at : q_at + 256] = d_qkv_ref[...]


def halved(left, w0, w1):
    half = w0.shape[0]
    return mm(left[:, :half], w0) + mm(left[:, half:], w1)


def put_rows(outs, left, w0, w1):
    value = jnp.concatenate([mul_t(left, w0), mul_t(left, w1)], 1)
    for k, o_ref in enumerate(outs):

        @pl.when(pl.program_id(0) == k)
        def _():
            o_ref[...] = value.astype(o_ref.dtype)


def rows_out(n, rows, width):
    spec = pl.BlockSpec((rows, width), lambda i: (0, 0))
    shapes = [out_of((rows, width), F32)] + [out_of((rows, width), BF)] * (n - 1)
    return [spec] * n, shapes


def rows_kernel(low, high, left_ref, w0_ref, w1_ref, *outs):
    put_rows(outs, left_ref[...], w0_ref[:, low:high], w1_ref[:, low:high])


def partial_rows(n, left, halves, low, high):
    rows, width = left.shape[0] // n, 2 * halves[0].shape[0]
    specs, shapes = rows_out(n, rows, width)
    return pl.pallas_call(
        functools.partial(rows_kernel, low, high),
        grid=(n,),
        in_specs=[row_spec(rows, left.shape[1])] + [fixed_spec(a) for a in halves],
        out_specs=specs,
        out_shape=shapes,
    )(left, *halves)


def mix_kernel(low, gated_ref, scale_ref, gm_ref, attn_ref, w0_ref, w1_ref, mix_ref, *outs):
    scale = column(scale_ref[0])[:, :1]
    mamba = (gated_ref[...] * scale * gm_ref[...]).astype(BF)
    mix = jnp.concatenate([mamba, attn_ref[...]], 1)
    mix_ref[...] = mix
    put_rows(outs, mix, w0_ref[:, low:], w1_ref[:, low:])


def ffn_kernel(size, hid_ref, cot_ref, w0_ref, w1_ref, act_ref, d_gu_ref, *outs):
    gu = halved(hid_ref[...], w0_ref[:, : 2 * size], w1_ref[:, : 2 * size])
    gate, up = gu[:, :size], gu[:, size:]
    sig = jax.nn.sigmoid(gate)
    silu = gate * sig
    act_ref[...] = (silu * up).astype(BF)
    d_act = halved(cot_ref[...], w0_ref[:, 2 * size :], w1_ref[:, 2 * size :])
    d_gate = d_act * up * (sig * (1.0 + gate * (1.0 - sig)))
    d_gu = jnp.concatenate([d_gate.astype(BF), (d_act * silu).astype(BF)], 1)
    d_gu_ref[...] = d_gu
    put_rows(outs, d_gu, w0_ref[:, : 2 * size], w1_ref[:, : 2 * size])


def row_spec(*shape):
    return pl.BlockSpec(shape, lambda i: (i,) + (0,) * (len(shape) - 1))


def fixed_spec(a):
    return pl.BlockSpec(a.shape, lambda i: (0,) * len(a.shape))


def out_of(shape, dtype):
    return jax.ShapeDtypeStruct(shape, dtype)


def rms_scale(x):
    return lax.rsqrt(jnp.mean(x * x, -1, keepdims=True) + norm_eps)


def rms_back(x, scale, gain, d_out):
    scaled = d_out * gain
    inner = jnp.mean(scaled * x, -1, keepdims=True)
    return scale * scaled - x * (scale * scale * scale * inner), jnp.sum(d_out * x * scale, 0)


def body(
    tokens,
    segment_ids,
    cotangent,
    w_in,
    w_q,
    w_k,
    w_v,
    w_o,
    w_out,
    w_gate,
    w_up,
    w_down,
    g_in,
    g_ff,
    g_mamba,
    conv_weight,
    conv_bias,
    a_log,
    d_skip,
    dt_bias,
):
    n = lax.axis_size("dp")
    rank = lax.axis_index("dp")
    rows, width = tokens.shape
    inner, channels, heads = g_mamba.shape[0], conv_bias.shape[0], a_log.shape[0]
    hidden = w_gate.shape[1]
    q_heads, kv_heads = w_q.shape[1] // HD, w_k.shape[1] // HD
    my_inner, my_heads, my_hidden, my_q = inner // n, heads // n, hidden // n, q_heads // n
    per_kv = q_heads // kv_heads
    assert heads % n == 0 and q_heads % n == 0 and hidden % n == 0 and per_kv % my_q == 0
    kv = rank * my_q // per_kv
    both = channels - inner
    qc = my_q * HD

    cube = is_cube(width)
    tail_pad = -my_heads % 128
    assert rows <= 256
    start = (segment_ids - segment_ids[0]).astype(BF)
    start = jnp.broadcast_to(start[:, None], (rows, 128))
    sh_a = jnp.concatenate(
        [
            cols(w_in, rank * my_inner, my_inner),
            cols(w_in, inner + rank * my_inner, my_inner),
            w_in[:, 2 * inner : inner + channels],
            cols(w_q, rank * qc, qc),
            cols(w_k, kv * HD, HD),
            cols(w_v, kv * HD, HD),
            cols(w_in, inner + channels + rank * my_heads, my_heads),
            jnp.zeros((w_in.shape[0], tail_pad), BF),
            cols(w_out, rank * my_inner, my_inner),
            cols(w_o, rank * qc, qc),
        ],
        1,
    )
    sh_a, tokens, start = tie((sh_a, tokens, start))
    if cube:
        parts_a = gather_start(sh_a)
        tokens, cotangent, g_in, g_ff = reorder(
            [tokens, cotangent, g_in.reshape(1, width), g_ff.reshape(1, width)]
        )
    first = peer_rows(jnp.concatenate([tokens, start], 1))
    if cube:
        parts_a, first = tie((parts_a, first))
        own_a = jnp.concatenate(parts_a, 0)
        halves_a = [own_a, flip(own_a, 1)]
    else:
        full_a = lax.all_gather(sh_a, "fsdp", axis=0, tiled=True)
        halves_a = [full_a[: width // 2], full_a[width // 2 :]]

    sh_b = jnp.concatenate(
        [cols(w, rank * my_hidden, my_hidden) for w in (w_gate, w_up, w_down)], 1
    )
    if cube:
        sh_b, parts_a = tie((sh_b, parts_a))
        parts_b = gather_start(sh_b)
    cot_first, _ = tie((cotangent, first))
    cot_blocks = peer_direct(cot_first)

    o = 2 * my_inner + both
    mc = my_inner + qc
    span = sh_a.shape[1] - mc
    assert rows == 128 and qc == 128 and 2 * HD == 128 and conv_weight.shape[0] == 4
    assert my_heads % 2 == 0 and both % 256 == 0 and inner // heads == HD
    cw = jnp.concatenate(
        [cols(conv_weight, rank * my_inner, my_inner), conv_weight[:, inner:]], 1
    )
    cb = jnp.concatenate(
        [lax.dynamic_slice(conv_bias, (rank * my_inner,), (my_inner,)), conv_bias[inner:]]
    )

    def mine(p, size):
        return lax.dynamic_slice(p, (rank * size,), (size,))

    gm = mine(g_mamba, my_inner)

    sizes = (rows, my_inner, both, my_heads)
    skip = jnp.repeat(mine(d_skip, my_heads), HD)
    conv_p = jnp.concatenate(
        [cw, cb[None], jnp.pad(skip, (0, both))[None], jnp.zeros((2, cw.shape[1]), F32)], 0
    )
    head_p = jnp.stack(
        [mine(a_log, my_heads), mine(d_skip, my_heads), mine(dt_bias, my_heads)], 0
    )
    head_p = jnp.pad(head_p, ((0, 5), (0, 128 - my_heads)))
    gm = gm.reshape(1, my_inner)
    g_in_row = g_in.reshape(1, width)
    count = n * rows
    normed, proj, y, gated, square, attn = pl.pallas_call(
        functools.partial(branch_forward, sizes, o),
        grid=(n,),
        in_specs=[row_spec(rows, first.shape[1])]
        + [pl.BlockSpec((a.shape[0], span), lambda i: (0, 0)) for a in halves_a]
        + [fixed_spec(a) for a in (g_in_row, conv_p, head_p)],
        out_specs=[
            row_spec(rows, width),
            row_spec(rows, span),
            row_spec(rows, my_inner),
            row_spec(rows, my_inner),
            row_spec(1, 1, rows),
            row_spec(rows, qc),
        ],
        out_shape=[
            out_of((count, width), BF),
            out_of((count, span), F32),
            out_of((count, my_inner), F32),
            out_of((count, my_inner), F32),
            out_of((n, 1, rows), F32),
            out_of((count, qc), BF),
        ],
    )(first, *halves_a, g_in_row, conv_p, head_p)
    square = peer_scalar_sum(square.reshape(n, rows))
    scale_rows = lax.rsqrt(square / inner + norm_eps).reshape(n, 1, rows)
    specs, shapes = rows_out(n, rows, width)
    mix_in, *mix_parts = pl.pallas_call(
        functools.partial(mix_kernel, span),
        grid=(n,),
        in_specs=[row_spec(rows, my_inner), row_spec(1, 1, rows), fixed_spec(gm)]
        + [row_spec(rows, qc)]
        + [fixed_spec(a) for a in halves_a],
        out_specs=[row_spec(rows, mc)] + specs,
        out_shape=[out_of((count, mc), BF)] + shapes,
    )(gated, scale_rows, gm, attn, *halves_a)
    mix_parts = peer_send(mix_parts)
    if cube:
        mix_parts, parts_b, cot_blocks = tie((mix_parts, parts_b, cot_blocks))
        own_b = jnp.concatenate(parts_b, 0)
        halves_b = [own_b, flip(own_b, 1)]
    else:
        full_b = lax.all_gather(sh_b, "fsdp", axis=0, tiled=True)
        halves_b = [full_b[: width // 2], full_b[width // 2 :]]
    cot_all = jnp.concatenate(cot_blocks, 0)
    tok32 = tokens.astype(F32)
    mixed = tok32 + add_up(mix_parts)
    f_scale = rms_scale(mixed)
    hid_all = peer_rows((mixed * f_scale * g_ff).astype(BF))
    act, d_gu, *d_hidden = pl.pallas_call(
        functools.partial(ffn_kernel, my_hidden),
        grid=(n,),
        in_specs=[row_spec(rows, width)] * 2 + [fixed_spec(a) for a in halves_b],
        out_specs=[row_spec(rows, my_hidden), row_spec(rows, 2 * my_hidden)] + specs,
        out_shape=[out_of((count, my_hidden), BF), out_of((count, 2 * my_hidden), BF)]
        + shapes,
    )(hid_all, cot_all, *halves_b)
    d_hidden = peer_send(d_hidden)
    c_pairs = [(hid_all, d_gu), (cot_all, act)]
    if cube:
        c_own = scatter_own(c_pairs, scatter_first(c_pairs))
        grad_c = scatter_rest(c_own)
        d_hidden, c_own = tie((d_hidden, c_own))
    else:
        grad_c = grads(c_pairs, 0, width)
    d_mixed_n, grad_g_ff = rms_back(mixed, f_scale, g_ff, add_up(d_hidden))
    d_mixed = cotangent.astype(F32) + d_mixed_n
    dm_all = peer_rows(d_mixed.astype(BF))
    dm_all, grad_c = tie((dm_all, grad_c))
    if cube:
        grad_c = add_up(grad_c).astype(BF)
    else:
        grad_c = lax.psum_scatter(grad_c, "fsdp", scatter_dimension=0, tiled=True)
    start_all = first[:, width:]
    c_blocks = peer_direct(grad_c)
    d_scaled, d_attn, m_inner, grad_gm = pl.pallas_call(
        functools.partial(branch_back_out, sizes, span),
        grid=(n,),
        in_specs=[row_spec(rows, width)]
        + [fixed_spec(a) for a in halves_a]
        + [row_spec(rows, my_inner), row_spec(1, 1, rows), fixed_spec(gm)],
        out_specs=[
            row_spec(rows, my_inner),
            row_spec(rows, qc),
            row_spec(1, 1, rows),
            fixed_spec(gm),
        ],
        out_shape=[
            out_of((count, my_inner), F32),
            out_of((count, qc), F32),
            out_of((n, 1, rows), F32),
            out_of((1, my_inner), F32),
        ],
    )(dm_all, *halves_a, gated, scale_rows, gm)
    act, d_attn, m_inner = tie((act, d_attn, m_inner))
    d_qkv = pl.pallas_call(
        functools.partial(branch_back_attn, o),
        grid=(n,),
        in_specs=[row_spec(rows, rows), row_spec(rows, span), row_spec(rows, qc)],
        out_specs=row_spec(rows, 256),
        out_shape=out_of((count, 256), BF),
        cost_estimate=pl.CostEstimate(
            flops=30 * count * rows * 128, bytes_accessed=count * 5000, transcendentals=count * 512
        ),
    )(start_all, proj, d_attn)
    m_inner = peer_scalar_sum(m_inner.reshape(n, rows)).reshape(n, 1, rows)
    act, _ = tie((act, d_qkv))
    out_parts = partial_rows(n, act, halves_b, 2 * my_hidden, 3 * my_hidden)
    out_parts = peer_send(out_parts)
    m_inner, d_qkv, c_blocks = tie((m_inner, d_qkv, c_blocks))
    d_proj, g_conv, g_head, g_skip = pl.pallas_call(
        lambda *refs: branch_back_mamba(sizes, o, *refs[:10], float(inner), *refs[10:]),
        grid=(n,),
        in_specs=[
            row_spec(rows, rows),
            row_spec(rows, span),
            row_spec(rows, my_inner),
            row_spec(rows, my_inner),
            row_spec(rows, my_inner),
            row_spec(1, 1, rows),
            row_spec(1, 1, rows),
            row_spec(rows, 256),
            fixed_spec(conv_p),
            fixed_spec(head_p),
        ],
        out_specs=[
            row_spec(rows, span),
            fixed_spec(conv_p),
            fixed_spec(head_p),
            fixed_spec(gm),
        ],
        out_shape=[
            out_of((count, span), BF),
            out_of(conv_p.shape, F32),
            out_of(head_p.shape, F32),
            out_of((1, my_inner), F32),
        ],
    )(start_all, proj, y, gated, d_scaled, scale_rows, m_inner, d_qkv, conv_p, head_p)
    a_pairs = [(dm_all, mix_in), (normed, d_proj)]
    if cube:
        got = scatter_first(a_pairs)
        d_proj, _ = tie((d_proj, a_pairs))
    d_normed = partial_rows(n, d_proj, halves_a, 0, span)
    if cube:
        own = scatter_own(a_pairs, got)
        grad_a = scatter_rest(own)
        d_normed, out_parts, own = tie((d_normed, out_parts, own))
        d_normed = peer_send(d_normed)
        grad_a = add_up(grad_a).astype(BF)
    else:
        d_normed = peer_send(d_normed)
        grad_a = lax.psum_scatter(
            grads(a_pairs, 0, width), "fsdp", scatter_dimension=0, tiled=True
        )
    output = (mixed + add_up(out_parts)).astype(BF)
    d_tok_n, grad_g_in = rms_back(tok32, rms_scale(tok32), g_in, add_up(d_normed))
    grad_tokens = (d_mixed + d_tok_n).astype(BF)
    if cube:
        output, grad_tokens = reorder([output, grad_tokens], back=True)

    def place(v):
        spot = (jnp.arange(n) == rank).astype(F32)
        spread = spot[:, None, None] * v.reshape(v.shape[:-1] + (1, -1, 128))
        return spread.reshape(-1, 128)

    def ordered(v):
        v = v.reshape(-1, 128)
        if not cube:
            return v
        block = jnp.array(ORDER) ^ lax.axis_index("fsdp")
        hit = (jnp.arange(8)[:, None] == block[None, :]).astype(F32)
        v = v.reshape(8, 1, -1)
        return jnp.sum(hit.T[:, :, None] * v, 0).reshape(-1, 128)

    def head_row(v):
        spot = (jnp.arange(n) == rank).astype(F32)
        return jnp.pad((spot[:, None] * v[None]).reshape(1, -1), ((0, 0), (0, 128 - heads)))

    grad_gm, g_cw, g_cb = grad_gm[0], g_conv[:4], g_conv[4]
    g_al, g_db = g_head[0, :my_heads], g_head[1, :my_heads]
    g_ds = jnp.sum(g_skip.reshape(my_heads, HD), 1)
    small = [ordered(grad_g_in), ordered(grad_g_ff), place(grad_gm)]
    for row in range(g_cw.shape[0]):
        small += [place(g_cw[row, :my_inner]), g_cw[row, my_inner:].reshape(-1, 128)]
    small += [place(g_cb[:my_inner]), g_cb[my_inner:].reshape(-1, 128)]
    small += [head_row(g_al), head_row(g_ds), head_row(g_db)]
    flat = jnp.concatenate(small)
    flat = jnp.pad(flat, ((0, -flat.shape[0] % 8), (0, 0)))
    flat, grad_a = tie((sum_dp(flat), grad_a))
    a_blocks = peer_blocks(grad_a)
    flat = sum_fsdp(flat)

    def kv_of(owner):
        return owner * my_q // per_kv

    grad_gate, grad_up, grad_down = lay(
        c_blocks,
        [("slice", i * my_hidden, my_hidden, i, 0) for i in range(3)],
        [hidden] * 3,
        kv_of,
    )
    grad_in, grad_q, grad_k, grad_v, grad_out, grad_o = lay(
        a_blocks,
        [
            ("slice", 0, my_inner, 4, 0),
            ("slice", my_inner, qc, 5, 0),
            ("slice", mc, my_inner, 0, 0),
            ("slice", mc + my_inner, my_inner, 0, inner),
            ("sum", mc + 2 * my_inner, both, 0, 2 * inner),
            ("slice", mc + o, qc, 1, 0),
            ("kv", mc + o + qc, HD, 2, 0),
            ("kv", mc + o + qc + HD, HD, 3, 0),
            ("tail", mc + o + qc + 2 * HD, my_heads, 0, inner + channels),
        ],
        [w_in.shape[1], w_q.shape[1], w_k.shape[1], w_v.shape[1], inner, w_o.shape[1]],
        kv_of,
    )

    sizes = [width, width, inner, g_cw.shape[0] * channels, channels]
    sums, at = [], 0
    for size in sizes:
        sums.append(flat[at : at + size // 128].reshape(-1))
        at += size // 128
    for i in range(3):
        sums.append(flat[at + i, :heads])
    return (
        output,
        grad_tokens,
        grad_in,
        grad_q,
        grad_k,
        grad_v,
        grad_o,
        grad_out,
        grad_gate,
        grad_up,
        grad_down,
        sums[0],
        sums[1],
        sums[2],
        sums[3].reshape(conv_weight.shape),
        sums[4],
        sums[5],
        sums[6],
        sums[7],
    )


def solution(mesh):
    rows, shard, whole = P(("fsdp", "dp"), None), P("fsdp", None), P()
    in_specs = (rows, P(("fsdp", "dp")), rows) + (shard,) * 9 + (whole,) * 8
    out_specs = (rows, rows) + (shard,) * 9 + (whole,) * 8

    return jax.shard_map(body, mesh=mesh, in_specs=in_specs, out_specs=out_specs, check_vma=False)
```

time: 1010 us -> 413 us (0.41)
  waiting for transfers between devices: 740 us -> 200 us
  Pallas kernels: 0 us -> 93.1 us
  matrix products: 80.9 us -> 0 us
  starting transfers between devices: 0.35 us -> 77.1 us
  blocking collectives: 64 us -> 0 us
  other arithmetic: 65.8 us -> 16.7 us
  between operations: 16 us -> 1.43 us
  local copies, waits for them, and re-layouts: 33.1 us -> 23 us
    reduce_scatter x1 -> x0, waiting for transfers between devices: 484 us -> none  [body(): lax.psum_scatter(jnp.concatenate(pieces, 1), 'fsdp', scatter_dimension=0,...]
    ppermute x0 -> x58, waiting for transfers between devices: none -> 200 us  [the longest x12 81.9 us: next_peer(): return lax.ppermute(x, 'dp', [(i, (i + 1) % n) for i in range(n)])]
    all_gather x7 -> x0, waiting for transfers between devices: 187 us -> none  [the longest x1 45.3 us: body(): lax.all_gather(w_in, 'fsdp', axis=0, tiled=True)]
    pallas_call x0 -> x16, Pallas kernels: none -> 93.1 us  [the longest x4 19.3 us: grads(): pl.pallas_call(functools.partial(grad_kernel, len(pairs), add is not None...]
    dot_general x34 -> x0, matrix products: 80.9 us -> none  [the longest x4 19.7 us: body(): lax.dot_general(left_op, right_op, (((0,), (0,)), ((), ())), preferred_el...]
    ppermute x0 -> x58, starting transfers between devices: none -> 77.1 us  [the longest x12 24.4 us: peer_send(): lax.ppermute(blocks[k], 'dp', [(i, (i - k) % n) for i in range(n)])]
    psum x1 -> x0, waiting for transfers between devices: 64.6 us -> none  [body(): lax.psum(grad_block.astype(jnp.bfloat16), 'dp').astype(jnp.float32)]
    psum x1 -> x0, blocking collectives: 43.4 us -> none  [body(): lax.psum((grad_g_in, grad_g_ff, grad_gm, grad_cw, grad_cb, grad_al, grad_...]
  transfers between devices with their start and end apart: 9 -> 58, of which waited for: 8 -> 32; matrix products, arithmetic and copies ran while one was open for 5% -> 6% of each run, Pallas kernels for 0% -> 11%
where the time goes in v1:
time: 413 us; the launch traced here: 411 us
  waiting for transfers between devices  200 us (48%)
  Pallas kernels  93.1 us (23%)
  starting transfers between devices  77.1 us (19%)
  local copies, waits for them, and re-layouts  23 us (6%)
  other arithmetic  16.7 us (4%)
    ppermute x12, waiting for transfers between devices, next_peer(): return lax.ppermute(x, 'dp', [(i, (i + 1) % n) for i in range(n)])  81.9 us
    ppermute x12, waiting for transfers between devices, peer_send(): lax.ppermute(blocks[k], 'dp', [(i, (i - k) % n) for i in range(n)])  48.3 us
    ppermute x12, starting transfers between devices, peer_send(): lax.ppermute(blocks[k], 'dp', [(i, (i - k) % n) for i in range(n)])  24.4 us
    ppermute x16, waiting for transfers between devices, flip(): return lax.ppermute(x, 'fsdp', [(i, i ^ bits) for i in range(size)])  22.1 us
    ppermute x6, waiting for transfers between devices, peer_scalar_sum(): got = lax.ppermute(v, 'dp', [(i, (i - m) % n) for i in range(n)])  22 us
    ppermute x12, starting transfers between devices, next_peer(): return lax.ppermute(x, 'dp', [(i, (i + 1) % n) for i in range(n)])  20.1 us
    pallas_call x4, Pallas kernels, grads(): pl.pallas_call(functools.partial(grad_kernel, len(pairs), add is not None...  19.3 us
    ppermute x6, waiting for transfers between devices, peer_direct(): lax.ppermute(x, 'dp', [(i, (i + k) % n) for i in range(n)])  14.5 us
  transfers between devices with their start and end apart: 58, of which 32 were waited for; matrix products, arithmetic and copies ran while one was open for 6% of the time, Pallas kernels for 11%

profile of v1, /device:TPU:0, one launch (start us, length us, event | category | flops | bytes accessed | tf_op | source)
XLA Modules:
  0.0 411.4 jit_solution(7753629278723105162)
XLA Ops:
  10.9 3.1 collective-permute-start.3
  14.0 9.0 %collective-permute-done.3 = bf16[128,1152]{1,0:T(8,128)(2,1)S(1)} collective-permute-done((bf16[128,1152]{1,0:T(8,128)(2,1)S(1)}, bf16[128,1152]{1,0:T(8,128)(2,1)S(1)}, u32[]{:S(2)}, u32[]{:S(2)}) %collective-permute-start.3) | collective-permute-done | bytes 294944 | tf_op jit(solution)/shard_map/ppermute | solution.py:41
  23.0 10.0 %collective-permute-done.4 = bf16[128,1152]{1,0:T(8,128)(2,1)S(1)} collective-permute-done((bf16[128,1152]{1,0:T(8,128)(2,1)S(1)}, bf16[128,1152]{1,0:T(8,128)(2,1)S(1)}, u32[]{:S(2)}, u32[]{:S(2)}) %collective-permute-start.4) | collective-permute-done | bytes 294944 | tf_op jit(solution)/shard_map/ppermute | solution.py:41
  36.5 5.6 %collective-permute-done.5 = bf16[128,1152]{1,0:T(8,128)(2,1)S(1)} collective-permute-done((bf16[128,1152]{1,0:T(8,128)(2,1)S(1)}, bf16[128,1152]{1,0:T(8,128)(2,1)S(1)}, u32[]{:S(2)}, u32[]{:S(2)}) %collective-permute-start.5) | collective-permute-done | bytes 294944 | tf_op jit(solution)/shard_map/ppermute | solution.py:41
  43.2 3.8 collective-permute-done
  47.1 8.7 %collective-permute-done.1 = bf16[128,1920]{1,0:T(8,128)(2,1)S(1)} collective-permute-done((bf16[128,1920]{1,0:T(8,128)(2,1)S(1)}, bf16[128,1920]{1,0:T(8,128)(2,1)S(1)}, u32[]{:S(2)}, u32[]{:S(2)}) %collective-permute-start.1) | collective-permute-done | bytes 491552 | tf_op jit(solution)/shard_map/ppermute | solution.py:64
  60.4 11.8 %shard_map.358 = (bf16[512,1024]{1,0:T(8,128)(2,1)}, f32[512,1408]{1,0:T(8,128)}, f32[512,384]{1,0:T(8,128)}, f32[512,384]{1,0:T(8,128)}, f32[4,1,128]{2,1,0:T(1,128)}, /*index=5*/bf16[512,128]{1,0:T(8,128)(2,1)}) custom-call(bf16[512,1152]{1,0:T(8,128)(2,1)} %pad_maximum_fusion.x_ref, bf16[512,1920]{1,0:T(8,128)(2,1)} %copy-done.2, ...), custom_call_target="tpu_custom_call" | custom-call | tf_op jit(solution)/shard_map/pallas_call | solution.py:716
  72.2 3.6 collective-permute-start.7
  82.2 17.1 %collective-permute-done.8 = f32[4,128]{1,0:T(4,128)S(1)} collective-permute-done((f32[4,128]{1,0:T(4,128)}, f32[4,128]{1,0:T(4,128)S(1)}, u32[]{:S(2)}, u32[]{:S(2)}) %collective-permute-start.8) | collective-permute-done | bytes 2080 | tf_op jit(solution)/shard_map/ppermute | solution.py:229
  100.0 4.9 %collective-permute-done.9 = f32[4,128]{1,0:T(4,128)S(1)} collective-permute-done((f32[4,128]{1,0:T(4,128)}, f32[4,128]{1,0:T(4,128)S(1)}, u32[]{:S(2)}, u32[]{:S(2)}) %collective-permute-start.9) | collective-permute-done | bytes 2080 | tf_op jit(solution)/shard_map/ppermute | solution.py:229
  107.0 6.2 %shard_map.359 = (bf16[512,512]{1,0:T(8,128)(2,1)}, f32[128,1024]{1,0:T(8,128)}, bf16[128,1024]{1,0:T(8,128)(2,1)}, bf16[128,1024]{1,0:T(8,128)(2,1)}, bf16[128,1024]{1,0:T(8,128)(2,1)}) custom-call(f32[512,384]{1,0:T(8,128)} %get-tuple-element.137.gated_ref.refs_3_, f32[4,1,128]{2,1,0:T(1,128)} %add_rsqrt_fusion.scale_ref.refs_5_, ...), custom_call_target="tpu_custom_call" | custom-call | tf_op jit(solution)/shard_map/pallas_call | solution.py:742
  117.8 6.7 %collective-permute-done.10 = bf16[128,1024]{1,0:T(8,128)(2,1)S(1)} collective-permute-done((bf16[128,1024]{1,0:T(8,128)(2,1)}, bf16[128,1024]{1,0:T(8,128)(2,1)S(1)}, u32[]{:S(2)}, u32[]{:S(2)}) %collective-permute-start.10) | collective-permute-done | bytes 262176 | tf_op jit(solution)/shard_map/ppermute | solution.py:220
  124.5 8.1 %collective-permute-done.11 = bf16[128,1024]{1,0:T(8,128)(2,1)S(1)} collective-permute-done((bf16[128,1024]{1,0:T(8,128)(2,1)}, bf16[128,1024]{1,0:T(8,128)(2,1)S(1)}, u32[]{:S(2)}, u32[]{:S(2)}) %collective-permute-start.11) | collective-permute-done | bytes 262176 | tf_op jit(solution)/shard_map/ppermute | solution.py:220
  133.4 6.1 %collective-permute-start.19 = (bf16[128,1024]{1,0:T(8,128)(2,1)S(1)}, bf16[128,1024]{1,0:T(8,128)(2,1)S(1)}, u32[]{:S(2)}, u32[]{:S(2)}) collective-permute-start(bf16[128,1024]{1,0:T(8,128)(2,1)S(1)} %multiply_convert_fusion), channel_id=1, source_target_pairs={{0,1},{1,2},{2,3},{3,0},{4,5},{5,6},{6,7},{7,4},{8,9},{9,10},{10,1... | collective-permute-start | bytes 786440 | tf_op jit(solution)/shard_map/ppermute | solution.py:41
  139.6 6.7 %collective-permute-done.19 = bf16[128,1024]{1,0:T(8,128)(2,1)S(1)} collective-permute-done((bf16[128,1024]{1,0:T(8,128)(2,1)S(1)}, bf16[128,1024]{1,0:T(8,128)(2,1)S(1)}, u32[]{:S(2)}, u32[]{:S(2)}) %collective-permute-start.19) | collective-permute-done | bytes 262176 | tf_op jit(solution)/shard_map/ppermute | solution.py:41
  148.1 7.9 %collective-permute-done.20 = bf16[128,1024]{1,0:T(8,128)(2,1)S(1)} collective-permute-done((bf16[128,1024]{1,0:T(8,128)(2,1)S(1)}, bf16[128,1024]{1,0:T(8,128)(2,1)S(1)}, u32[]{:S(2)}, u32[]{:S(2)}) %collective-permute-start.20) | collective-permute-done | bytes 262176 | tf_op jit(solution)/shard_map/ppermute | solution.py:41
  156.1 8.8 %collective-permute-done.21 = bf16[128,1024]{1,0:T(8,128)(2,1)S(1)} collective-permute-done((bf16[128,1024]{1,0:T(8,128)(2,1)S(1)}, bf16[128,1024]{1,0:T(8,128)(2,1)S(1)}, u32[]{:S(2)}, u32[]{:S(2)}) %collective-permute-start.21) | collective-permute-done | bytes 262176 | tf_op jit(solution)/shard_map/ppermute | solution.py:41
  166.0 8.8 %shard_map.360 = (bf16[512,512]{1,0:T(8,128)(2,1)}, bf16[512,1024]{1,0:T(8,128)(2,1)}, f32[128,1024]{1,0:T(8,128)}, bf16[128,1024]{1,0:T(8,128)(2,1)}, bf16[128,...) custom-call(bf16[512,1024]{1,0:T(8,128)(2,1)} %pad_maximum_fusion.1.hid_ref.refs_0_, bf16[512,1024]{1,0:T(8,128)(2,1)} %copy-done.3, ...), custom_call_target="tpu_custom_call" | custom-call | tf_op jit(solution)/shard_map/pallas_call | solution.py:764
  174.8 3.8 shard_map.361
  178.7 3.7 collective-permute-start.25
  183.6 5.4 %shard_map.362 = (bf16[128,1536]{1,0:T(8,128)(2,1)}, bf16[128,1536]{1,0:T(8,128)(2,1)}, bf16[128,1536]{1,0:T(8,128)(2,1)}, bf16[128,1536]{1,0:T(8,128)(2,1)}) custom-call(bf16[512,1024]{1,0:T(8,128)(2,1)} %pad_maximum_fusion.1.hid_ref.refs_0_, bf16[512,1024]{1,0:T(8,128)(2,1)} %copy-done.3, bf16[512,1024]{1,0:T(8,128)(2,1)} %get-tuple-element.166.refs_2_, ...), custom_call_target="tpu_custom_call" | custom-call | flops 805306368 | bytes 4194304 | tf_op jit(solution)/shard_map/pallas_call | solution.py:130
  189.9 10.3 %collective-permute-done.24 = bf16[128,1024]{1,0:T(8,128)(2,1)S(1)} collective-permute-done((bf16[128,1024]{1,0:T(8,128)(2,1)}, bf16[128,1024]{1,0:T(8,128)(2,1)S(1)}, u32[]{:S(2)}, u32[]{:S(2)}) %collective-permute-start.24) | collective-permute-done | bytes 262176 | tf_op jit(solution)/shard_map/ppermute | solution.py:220
  201.7 5.8 %collective-permute-start.27 = (bf16[128,1024]{1,0:T(8,128)(2,1)S(1)}, bf16[128,1024]{1,0:T(8,128)(2,1)S(1)}, u32[]{:S(2)}, u32[]{:S(2)}) collective-permute-start(bf16[128,1024]{1,0:T(8,128)(2,1)S(1)} %fusion.13), channel_id=1, source_target_pairs={{0,1},{1,2},{2,3},{3,0},{4,5},{5,6},{6,7},{7,4},{8,9},{9,10},{10,1... | collective-permute-start | bytes 786440 | tf_op jit(solution)/shard_map/ppermute | solution.py:41
  207.5 5.3 %collective-permute-done.27 = bf16[128,1024]{1,0:T(8,128)(2,1)S(1)} collective-permute-done((bf16[128,1024]{1,0:T(8,128)(2,1)S(1)}, bf16[128,1024]{1,0:T(8,128)(2,1)S(1)}, u32[]{:S(2)}, u32[]{:S(2)}) %collective-permute-start.27) | collective-permute-done | bytes 262176 | tf_op jit(solution)/shard_map/ppermute | solution.py:41
  215.3 6.3 %collective-permute-done.28 = bf16[128,1024]{1,0:T(8,128)(2,1)S(1)} collective-permute-done((bf16[128,1024]{1,0:T(8,128)(2,1)S(1)}, bf16[128,1024]{1,0:T(8,128)(2,1)S(1)}, u32[]{:S(2)}, u32[]{:S(2)}) %collective-permute-start.28) | collective-permute-done | bytes 262176 | tf_op jit(solution)/shard_map/ppermute | solution.py:41
  230.8 3.5 collective-permute-done.30
  234.2 4.4 %collective-permute-done.31 = bf16[128,1536]{1,0:T(8,128)(2,1)S(1)} collective-permute-done((bf16[128,1536]{1,0:T(8,128)(2,1)S(1)}, bf16[128,1536]{1,0:T(8,128)(2,1)S(1)}, u32[]{:S(2)}, u32[]{:S(2)}) %collective-permute-start.31) | collective-permute-done | bytes 393248 | tf_op jit(solution)/shard_map/ppermute | solution.py:64
  240.3 5.8 %shard_map.363 = (f32[512,384]{1,0:T(8,128)}, f32[512,128]{1,0:T(8,128)}, f32[4,1,128]{2,1,0:T(1,128)}, f32[1,384]{1,0:T(1,128)}) custom-call(bf16[512,1024]{1,0:T(8,128)(2,1)} %pad_maximum_fusion.2.dm_ref.refs_0_, bf16[512,1920]{1,0:T(8,128)(2,1)} %copy-done.2, bf16[512,1920]{1,0:T(8,128)(2,1)} %collective-permute-done.6.a1_ref.w1_ref.b1_ref, ...), custom_call_target="tpu_custom_call" | custom-call | tf_op jit(solution)/shard_map/pallas_call | solution.py:790
  246.0 3.2 collective-permute-start.33
  251.1 3.1 collective-permute-start.36
  255.1 8.5 %shard_map.364.refs_7_ = bf16[512,256]{1,0:T(8,128)(2,1)} custom-call(bf16[512,128]{1,0:T(8,128)(2,1)} %slice.141.x_ref.refs_0_, f32[512,1408]{1,0:T(8,128)} %get-tuple-element.151.proj_ref.refs_1_, f32[512,128]{1,0:T(8,128)} %get-tuple-element.181.d_attn_ref), custom_call_target="tpu_custom_call" | custom-call | flops 251658240 | bytes 2560000 | tf_op jit(solution)/shard_map/pallas_call | solution.py:810
  265.8 11.6 %collective-permute-done.37.refs_2_ = bf16[128,1536]{1,0:T(8,128)(2,1)S(1)} collective-permute-done((bf16[128,1536]{1,0:T(8,128)(2,1)S(1)}, bf16[128,1536]{1,0:T(8,128)(2,1)S(1)}, u32[]{:S(2)}, u32[]{:S(2)}) %collective-permute-start.37) | collective-permute-done | bytes 393248 | tf_op jit(solution)/shard_map/ppermute | solution.py:58
  280.2 9.0 %shard_map.365 = (bf16[512,1408]{1,0:T(8,128)(2,1)}, f32[8,640]{1,0:T(8,128)}, f32[8,128]{1,0:T(8,128)}, f32[1,384]{1,0:T(1,128)}) custom-call(bf16[512,128]{1,0:T(8,128)(2,1)} %slice.141.x_ref.refs_0_, f32[512,1408]{1,0:T(8,128)} %get-tuple-element.151.proj_ref.refs_1_, f32[512,384]{1,0:T(8,128)} %get-tuple-element.152.refs_2_, ...), custom_call_target="tpu_custom_call" | custom-call | tf_op jit(solution)/shard_map/pallas_call | solution.py:825
  289.3 4.1 %shard_map.368 = bf16[512,1920]{1,0:T(8,128)(2,1)} custom-call(bf16[512,1024]{1,0:T(8,128)(2,1)} %pad_maximum_fusion.2.dm_ref.refs_0_, bf16[512,1024]{1,0:T(8,128)(2,1)} %get-tuple-element.190.refs_1_, bf16[512,512]{1,0:T(8,128)(2,1)} %get-tuple-element.189.refs_2_, bf16[512,1408]{1,0:T(8,128)(2,1)} %get-tuple-element.191.left_ref.refs_3_), custom_call_target="tpu_custom_call" | custom-call | flops 1006632960 | bytes 4980736 | tf_op jit(solution)/shard_map/pallas_call | solution.py:130
  293.7 5.5 %shard_map.367 = (f32[128,1024]{1,0:T(8,128)}, bf16[128,1024]{1,0:T(8,128)(2,1)}, bf16[128,1024]{1,0:T(8,128)(2,1)}, bf16[128,1024]{1,0:T(8,128)(2,1)}) custom-call(bf16[512,512]{1,0:T(8,128)(2,1)} %get-tuple-element.197.refs_3_.left_ref, bf16[512,1536]{1,0:T(8,128)(2,1)} %copy-done.4, bf16[512,1536]{1,0:T(8,128)(2,1)} %collective-permute-done.22.w1_ref), custom_call_target="tpu_custom_call" | custom-call | tf_op jit(solution)/shard_map/pallas_call | solution.py:556
  299.2 6.1 %collective-permute-start.39 = (bf16[128,1024]{1,0:T(8,128)(2,1)}, bf16[128,1024]{1,0:T(8,128)(2,1)S(1)}, u32[]{:S(2)}, u32[]{:S(2)}) collective-permute-start(bf16[128,1024]{1,0:T(8,128)(2,1)} %get-tuple-element.199), channel_id=1, source_target_pairs={{0,1},{1,2},{2,3},{3,0},{4,5},{5,6},{6,7},{7,4},{8,9},{9,10},{10,1... | collective-permute-start | bytes 786440 | tf_op jit(solution)/shard_map/ppermute | solution.py:220
  307.9 7.7 %shard_map.366 = (f32[128,1024]{1,0:T(8,128)}, bf16[128,1024]{1,0:T(8,128)(2,1)}, bf16[128,1024]{1,0:T(8,128)(2,1)}, bf16[128,1024]{1,0:T(8,128)(2,1)}) custom-call(bf16[512,1408]{1,0:T(8,128)(2,1)} %get-tuple-element.191.left_ref.refs_3_, bf16[512,1920]{1,0:T(8,128)(2,1)} %copy-done.2, bf16[512,1920]{1,0:T(8,128)(2,1)} %collective-permute-done.6.a1_ref.w1_ref.b1_ref), custom_call_target="tpu_custom_call" | custom-call | tf_op jit(solution)/shard_map/pallas_call | solution.py:556
  316.5 6.0 %shard_map.369 = (bf16[128,1920]{1,0:T(8,128)(2,1)}, bf16[128,1920]{1,0:T(8,128)(2,1)}, bf16[128,1920]{1,0:T(8,128)(2,1)}, bf16[128,1920]{1,0:T(8,128)(2,1)}) custom-call(bf16[512,1024]{1,0:T(8,128)(2,1)} %pad_maximum_fusion.2.dm_ref.refs_0_, bf16[512,1024]{1,0:T(8,128)(2,1)} %get-tuple-element.190.refs_1_, bf16[512,512]{1,0:T(8,128)(2,1)} %get-tuple-element.189.refs_2_, ...), custom_call_target="tpu_custom_call" | custom-call | flops 1006632960 | bytes 4980736 | tf_op jit(solution)/shard_map/pallas_call | solution.py:130
  324.7 7.0 %collective-permute-start.45 = (bf16[128,1024]{1,0:T(8,128)(2,1)}, bf16[128,1024]{1,0:T(8,128)(2,1)S(1)}, u32[]{:S(2)}, u32[]{:S(2)}) collective-permute-start(bf16[128,1024]{1,0:T(8,128)(2,1)} %get-tuple-element.213), channel_id=1, source_target_pairs={{0,3},{1,0},{2,1},{3,2},{4,7},{5,4},{6,5},{7,6},{8,11},{9,8},{10,9... | collective-permute-start | bytes 786440 | tf_op jit(solution)/shard_map/ppermute | solution.py:220
  334.9 3.9 collective-permute-done.45
  339.4 16.3 %collective-permute-done.44 = bf16[128,1024]{1,0:T(8,128)(2,1)} collective-permute-done((bf16[128,1024]{1,0:T(8,128)(2,1)}, bf16[128,1024]{1,0:T(8,128)(2,1)}, u32[]{:S(2)}, u32[]{:S(2)}) %collective-permute-start.44) | collective-permute-done | bytes 262176 | tf_op jit(solution)/shard_map/ppermute | solution.py:220
  359.7 3.7 collective-permute-done.47
  369.5 3.2 shard_map.372
  373.4 3.6 collective-permute-done.56
  377.7 3.1 collective-permute-done.52.refs_1_
  385.4 7.2 %collective-permute-done.53.refs_2_ = bf16[128,1920]{1,0:T(8,128)(2,1)} collective-permute-done((bf16[128,1920]{1,0:T(8,128)(2,1)}, bf16[128,1920]{1,0:T(8,128)(2,1)}, u32[]{:S(2)}, u32[]{:S(2)}) %collective-permute-start.53) | collective-permute-done | bytes 491552 | tf_op jit(solution)/shard_map/ppermute | solution.py:41
  394.9 9.6 %collective-permute-done.54.refs_3_ = bf16[128,1920]{1,0:T(8,128)(2,1)S(1)} collective-permute-done((bf16[128,1920]{1,0:T(8,128)(2,1)}, bf16[128,1920]{1,0:T(8,128)(2,1)S(1)}, u32[]{:S(2)}, u32[]{:S(2)}) %collective-permute-start.54) | collective-permute-done | bytes 491552 | tf_op jit(solution)/shard_map/ppermute | solution.py:41
  405.3 3.4 shard_map.371
  (289 shorter events, 93.0 us)
Async XLA Ops:
  10.9 12.1 %collective-permute-start.3 = (bf16[128,1152]{1,0:T(8,128)(2,1)S(1)}, bf16[128,1152]{1,0:T(8,128)(2,1)S(1)}, u32[]{:S(2)}, u32[]{:S(2)}) collective-permute-start(bf16[128,1152]{1,0:T(8,128)(2,1)S(1)} %constant_dynamic-update-slice_fusion), channel_id=1, source_target_pairs={{0,1},{1,2},{2,3},{3,0},{4,5},{5,6},{6,7},{7,4},{8,9},{9,10},{10,1... | collective-permute-start | bytes 884744 | tf_op jit(solution)/shard_map/ppermute | solution.py:41
  23.0 10.0 %collective-permute-start.4 = (bf16[128,1152]{1,0:T(8,128)(2,1)S(1)}, bf16[128,1152]{1,0:T(8,128)(2,1)S(1)}, u32[]{:S(2)}, u32[]{:S(2)}) collective-permute-start(bf16[128,1152]{1,0:T(8,128)(2,1)S(1)} %collective-permute-done.3), channel_id=1, source_target_pairs={{0,1},{1,2},{2,3},{3,0},{4,5},{5,6},{6,7},{7,4},{8,9},{9,10},{10,1... | collective-permute-start | bytes 884744 | tf_op jit(solution)/shard_map/ppermute | solution.py:41
  33.0 9.1 %collective-permute-start.5 = (bf16[128,1152]{1,0:T(8,128)(2,1)S(1)}, bf16[128,1152]{1,0:T(8,128)(2,1)S(1)}, u32[]{:S(2)}, u32[]{:S(2)}) collective-permute-start(bf16[128,1152]{1,0:T(8,128)(2,1)S(1)} %collective-permute-done.4), channel_id=1, source_target_pairs={{0,1},{1,2},{2,3},{3,0},{4,5},{5,6},{6,7},{7,4},{8,9},{9,10},{10,1... | collective-permute-start | bytes 884744 | tf_op jit(solution)/shard_map/ppermute | solution.py:41
  33.0 14.1 %collective-permute-start = (bf16[128,1920]{1,0:T(8,128)(2,1)S(1)}, bf16[128,1920]{1,0:T(8,128)(2,1)S(1)}, u32[]{:S(2)}, u32[]{:S(2)}) collective-permute-start(bf16[128,1920]{1,0:T(8,128)(2,1)S(1)} %concatenate.90), channel_id=1, source_target_pairs={{0,8},{4,12},{8,0},{12,4},{16,24},{20,28},{24,16},{28,20},{1,9},{5... | collective-permute-start | bytes 1474568 | tf_op jit(solution)/shard_map/ppermute | solution.py:64
  34.2 21.6 %collective-permute-start.1 = (bf16[128,1920]{1,0:T(8,128)(2,1)S(1)}, bf16[128,1920]{1,0:T(8,128)(2,1)S(1)}, u32[]{:S(2)}, u32[]{:S(2)}) collective-permute-start(bf16[128,1920]{1,0:T(8,128)(2,1)S(1)} %concatenate.90), channel_id=1, source_target_pairs={{0,16},{4,20},{8,24},{12,28},{16,0},{20,4},{24,8},{28,12},{1,17},{... | collective-permute-start | bytes 1474568 | tf_op jit(solution)/shard_map/ppermute | solution.py:64
  35.8 20.0 %collective-permute-start.2 = (bf16[128,1920]{1,0:T(8,128)(2,1)S(1)}, bf16[128,1920]{1,0:T(8,128)(2,1)S(1)}, u32[]{:S(2)}, u32[]{:S(2)}) collective-permute-start(bf16[128,1920]{1,0:T(8,128)(2,1)S(1)} %concatenate.90), channel_id=1, source_target_pairs={{0,24},{4,28},{8,16},{12,20},{16,8},{20,12},{24,0},{28,4},{1,25},{... | collective-permute-start | bytes 1474568 | tf_op jit(solution)/shard_map/ppermute | solution.py:64
  77.2 38.2 %collective-permute-start.13 = (bf16[128,1536]{1,0:T(8,128)(2,1)S(1)}, bf16[128,1536]{1,0:T(8,128)(2,1)S(1)}, u32[]{:S(2)}, u32[]{:S(2)}) collective-permute-start(bf16[128,1536]{1,0:T(8,128)(2,1)S(1)} %pad_maximum_fusion.3), channel_id=1, source_target_pairs={{0,8},{4,12},{8,0},{12,4},{16,24},{20,28},{24,16},{28,20},{1,9},{5... | collective-permute-start | bytes 1179656 | tf_op jit(solution)/shard_map/ppermute | solution.py:64
  78.4 39.4 %collective-permute-start.14 = (bf16[128,1536]{1,0:T(8,128)(2,1)S(1)}, bf16[128,1536]{1,0:T(8,128)(2,1)S(1)}, u32[]{:S(2)}, u32[]{:S(2)}) collective-permute-start(bf16[128,1536]{1,0:T(8,128)(2,1)S(1)} %pad_maximum_fusion.3), channel_id=1, source_target_pairs={{0,16},{4,20},{8,24},{12,28},{16,0},{20,4},{24,8},{28,12},{1,17},{... | collective-permute-start | bytes 1179656 | tf_op jit(solution)/shard_map/ppermute | solution.py:64
  79.2 25.7 %collective-permute-start.16 = (bf16[128,1024]{1,0:T(8,128)(2,1)S(1)}, bf16[128,1024]{1,0:T(8,128)(2,1)S(1)}, u32[]{:S(2)}, u32[]{:S(2)}) collective-permute-start(bf16[128,1024]{1,0:T(8,128)(2,1)S(1)} %copy-done.6), channel_id=1, source_target_pairs={{0,1},{1,2},{2,3},{3,0},{4,5},{5,6},{6,7},{7,4},{8,9},{9,10},{10,1... | collective-permute-start | bytes 786440 | tf_op jit(solution)/shard_map/ppermute | solution.py:58
  79.2 34.0 %collective-permute-start.17 = (bf16[128,1024]{1,0:T(8,128)(2,1)S(1)}, bf16[128,1024]{1,0:T(8,128)(2,1)S(1)}, u32[]{:S(2)}, u32[]{:S(2)}) collective-permute-start(bf16[128,1024]{1,0:T(8,128)(2,1)S(1)} %copy-done.6), channel_id=1, source_target_pairs={{0,2},{1,3},{2,0},{3,1},{4,6},{5,7},{6,4},{7,5},{8,10},{9,11},{10,... | collective-permute-start | bytes 786440 | tf_op jit(solution)/shard_map/ppermute | solution.py:58
  79.8 19.5 %collective-permute-start.8 = (f32[4,128]{1,0:T(4,128)}, f32[4,128]{1,0:T(4,128)S(1)}, u32[]{:S(2)}, u32[]{:S(2)}) collective-permute-start(f32[4,128]{1,0:T(4,128)} %bitcast.101), channel_id=1, source_target_pairs={{0,2},{1,3},{2,0},{3,1},{4,6},{5,7},{6,4},{7,5},{8,10},{9,11},{10,... | collective-permute-start | bytes 6152 | tf_op jit(solution)/shard_map/ppermute | solution.py:229
  104.9 10.4 %collective-permute-start.18 = (bf16[128,1024]{1,0:T(8,128)(2,1)S(1)}, bf16[128,1024]{1,0:T(8,128)(2,1)S(1)}, u32[]{:S(2)}, u32[]{:S(2)}) collective-permute-start(bf16[128,1024]{1,0:T(8,128)(2,1)S(1)} %copy-done.6), channel_id=1, source_target_pairs={{0,3},{1,0},{2,1},{3,2},{4,7},{5,4},{6,5},{7,6},{8,11},{9,8},{10,9... | collective-permute-start | bytes 786440 | tf_op jit(solution)/shard_map/ppermute | solution.py:58
  104.9 12.9 %collective-permute-start.15 = (bf16[128,1536]{1,0:T(8,128)(2,1)S(1)}, bf16[128,1536]{1,0:T(8,128)(2,1)S(1)}, u32[]{:S(2)}, u32[]{:S(2)}) collective-permute-start(bf16[128,1536]{1,0:T(8,128)(2,1)S(1)} %pad_maximum_fusion.3), channel_id=1, source_target_pairs={{0,24},{4,28},{8,16},{12,20},{16,8},{20,12},{24,0},{28,4},{1,25},{... | collective-permute-start | bytes 1179656 | tf_op jit(solution)/shard_map/ppermute | solution.py:64
  113.3 11.2 %collective-permute-start.10 = (bf16[128,1024]{1,0:T(8,128)(2,1)}, bf16[128,1024]{1,0:T(8,128)(2,1)S(1)}, u32[]{:S(2)}, u32[]{:S(2)}) collective-permute-start(bf16[128,1024]{1,0:T(8,128)(2,1)} %get-tuple-element.141), channel_id=1, source_target_pairs={{0,1},{1,2},{2,3},{3,0},{4,5},{5,6},{6,7},{7,4},{8,9},{9,10},{10,1... | collective-permute-start | bytes 786440 | tf_op jit(solution)/shard_map/ppermute | solution.py:220
  115.3 17.2 %collective-permute-start.11 = (bf16[128,1024]{1,0:T(8,128)(2,1)}, bf16[128,1024]{1,0:T(8,128)(2,1)S(1)}, u32[]{:S(2)}, u32[]{:S(2)}) collective-permute-start(bf16[128,1024]{1,0:T(8,128)(2,1)} %get-tuple-element.142), channel_id=1, source_target_pairs={{0,2},{1,3},{2,0},{3,1},{4,6},{5,7},{6,4},{7,5},{8,10},{9,11},{10,... | collective-permute-start | bytes 786440 | tf_op jit(solution)/shard_map/ppermute | solution.py:220
  115.3 17.2 %collective-permute-start.12 = (bf16[128,1024]{1,0:T(8,128)(2,1)}, bf16[128,1024]{1,0:T(8,128)(2,1)S(1)}, u32[]{:S(2)}, u32[]{:S(2)}) collective-permute-start(bf16[128,1024]{1,0:T(8,128)(2,1)} %get-tuple-element.143), channel_id=1, source_target_pairs={{0,3},{1,0},{2,1},{3,2},{4,7},{5,4},{6,5},{7,6},{8,11},{9,8},{10,9... | collective-permute-start | bytes 786440 | tf_op jit(solution)/shard_map/ppermute | solution.py:220
  132.7 33.2 %collective-permute-start.22 = (bf16[512,1536]{1,0:T(8,128)(2,1)S(1)}, bf16[512,1536]{1,0:T(8,128)(2,1)}, u32[]{:S(2)}, u32[]{:S(2)}) collective-permute-start(bf16[512,1536]{1,0:T(8,128)(2,1)S(1)} %constant_dynamic-update-slice_fusion.10.w0_ref), channel_id=1, source_target_pairs={{0,4},{4,0},{8,12},{12,8},{16,20},{20,16},{24,28},{28,24},{1,5},{5... | collective-permute-start | bytes 4718600 | tf_op jit(solution)/shard_map/ppermute | solution.py:64
  133.4 12.9 %collective-permute-start.19 = (bf16[128,1024]{1,0:T(8,128)(2,1)S(1)}, bf16[128,1024]{1,0:T(8,128)(2,1)S(1)}, u32[]{:S(2)}, u32[]{:S(2)}) collective-permute-start(bf16[128,1024]{1,0:T(8,128)(2,1)S(1)} %multiply_convert_fusion), channel_id=1, source_target_pairs={{0,1},{1,2},{2,3},{3,0},{4,5},{5,6},{6,7},{7,4},{8,9},{9,10},{10,1... | collective-permute-start | bytes 786440 | tf_op jit(solution)/shard_map/ppermute | solution.py:41
  146.3 9.7 %collective-permute-start.20 = (bf16[128,1024]{1,0:T(8,128)(2,1)S(1)}, bf16[128,1024]{1,0:T(8,128)(2,1)S(1)}, u32[]{:S(2)}, u32[]{:S(2)}) collective-permute-start(bf16[128,1024]{1,0:T(8,128)(2,1)S(1)} %collective-permute-done.19), channel_id=1, source_target_pairs={{0,1},{1,2},{2,3},{3,0},{4,5},{5,6},{6,7},{7,4},{8,9},{9,10},{10,1... | collective-permute-start | bytes 786440 | tf_op jit(solution)/shard_map/ppermute | solution.py:41
  156.0 8.9 %collective-permute-start.21 = (bf16[128,1024]{1,0:T(8,128)(2,1)S(1)}, bf16[128,1024]{1,0:T(8,128)(2,1)S(1)}, u32[]{:S(2)}, u32[]{:S(2)}) collective-permute-start(bf16[128,1024]{1,0:T(8,128)(2,1)S(1)} %collective-permute-done.20), channel_id=1, source_target_pairs={{0,1},{1,2},{2,3},{3,0},{4,5},{5,6},{6,7},{7,4},{8,9},{9,10},{10,1... | collective-permute-start | bytes 786440 | tf_op jit(solution)/shard_map/ppermute | solution.py:41
  178.6 11.3 %collective-permute-start.23 = (bf16[128,1024]{1,0:T(8,128)(2,1)}, bf16[128,1024]{1,0:T(8,128)(2,1)S(1)}, u32[]{:S(2)}, u32[]{:S(2)}) collective-permute-start(bf16[128,1024]{1,0:T(8,128)(2,1)} %get-tuple-element.163), channel_id=1, source_target_pairs={{0,1},{1,2},{2,3},{3,0},{4,5},{5,6},{6,7},{7,4},{8,9},{9,10},{10,1... | collective-permute-start | bytes 786440 | tf_op jit(solution)/shard_map/ppermute | solution.py:220
  178.6 21.6 %collective-permute-start.24 = (bf16[128,1024]{1,0:T(8,128)(2,1)}, bf16[128,1024]{1,0:T(8,128)(2,1)S(1)}, u32[]{:S(2)}, u32[]{:S(2)}) collective-permute-start(bf16[128,1024]{1,0:T(8,128)(2,1)} %get-tuple-element.164), channel_id=1, source_target_pairs={{0,2},{1,3},{2,0},{3,1},{4,6},{5,7},{6,4},{7,5},{8,10},{9,11},{10,... | collective-permute-start | bytes 786440 | tf_op jit(solution)/shard_map/ppermute | solution.py:220
  178.7 21.5 %collective-permute-start.25 = (bf16[128,1024]{1,0:T(8,128)(2,1)}, bf16[128,1024]{1,0:T(8,128)(2,1)}, u32[]{:S(2)}, u32[]{:S(2)}) collective-permute-start(bf16[128,1024]{1,0:T(8,128)(2,1)} %get-tuple-element.165), channel_id=1, source_target_pairs={{0,3},{1,0},{2,1},{3,2},{4,7},{5,4},{6,5},{7,6},{8,11},{9,8},{10,9... | collective-permute-start | bytes 786440 | tf_op jit(solution)/shard_map/ppermute | solution.py:220
  201.7 11.1 %collective-permute-start.27 = (bf16[128,1024]{1,0:T(8,128)(2,1)S(1)}, bf16[128,1024]{1,0:T(8,128)(2,1)S(1)}, u32[]{:S(2)}, u32[]{:S(2)}) collective-permute-start(bf16[128,1024]{1,0:T(8,128)(2,1)S(1)} %fusion.13), channel_id=1, source_target_pairs={{0,1},{1,2},{2,3},{3,0},{4,5},{5,6},{6,7},{7,4},{8,9},{9,10},{10,1... | collective-permute-start | bytes 786440 | tf_op jit(solution)/shard_map/ppermute | solution.py:41
  212.8 8.7 %collective-permute-start.28 = (bf16[128,1024]{1,0:T(8,128)(2,1)S(1)}, bf16[128,1024]{1,0:T(8,128)(2,1)S(1)}, u32[]{:S(2)}, u32[]{:S(2)}) collective-permute-start(bf16[128,1024]{1,0:T(8,128)(2,1)S(1)} %collective-permute-done.27), channel_id=1, source_target_pairs={{0,1},{1,2},{2,3},{3,0},{4,5},{5,6},{6,7},{7,4},{8,9},{9,10},{10,1... | collective-permute-start | bytes 786440 | tf_op jit(solution)/shard_map/ppermute | solution.py:41
  221.6 8.2 %collective-permute-start.29 = (bf16[128,1024]{1,0:T(8,128)(2,1)S(1)}, bf16[128,1024]{1,0:T(8,128)(2,1)S(1)}, u32[]{:S(2)}, u32[]{:S(2)}) collective-permute-start(bf16[128,1024]{1,0:T(8,128)(2,1)S(1)} %collective-permute-done.28), channel_id=1, source_target_pairs={{0,1},{1,2},{2,3},{3,0},{4,5},{5,6},{6,7},{7,4},{8,9},{9,10},{10,1... | collective-permute-start | bytes 786440 | tf_op jit(solution)/shard_map/ppermute | solution.py:41
  222.3 12.0 %collective-permute-start.30 = (bf16[128,1536]{1,0:T(8,128)(2,1)S(1)}, bf16[128,1536]{1,0:T(8,128)(2,1)S(1)}, u32[]{:S(2)}, u32[]{:S(2)}) collective-permute-start(bf16[128,1536]{1,0:T(8,128)(2,1)S(1)} %copy-done.36), channel_id=1, source_target_pairs={{0,8},{4,12},{8,0},{12,4},{16,24},{20,28},{24,16},{28,20},{1,9},{5... | collective-permute-start | bytes 1179656 | tf_op jit(solution)/shard_map/ppermute | solution.py:64
  223.5 15.1 %collective-permute-start.31 = (bf16[128,1536]{1,0:T(8,128)(2,1)S(1)}, bf16[128,1536]{1,0:T(8,128)(2,1)S(1)}, u32[]{:S(2)}, u32[]{:S(2)}) collective-permute-start(bf16[128,1536]{1,0:T(8,128)(2,1)S(1)} %copy-done.35), channel_id=1, source_target_pairs={{0,16},{4,20},{8,24},{12,28},{16,0},{20,4},{24,8},{28,12},{1,17},{... | collective-permute-start | bytes 1179656 | tf_op jit(solution)/shard_map/ppermute | solution.py:64
  224.3 15.9 %collective-permute-start.32 = (bf16[128,1536]{1,0:T(8,128)(2,1)S(1)}, bf16[128,1536]{1,0:T(8,128)(2,1)S(1)}, u32[]{:S(2)}, u32[]{:S(2)}) collective-permute-start(bf16[128,1536]{1,0:T(8,128)(2,1)S(1)} %copy-done.34), channel_id=1, source_target_pairs={{0,24},{4,28},{8,16},{12,20},{16,8},{20,12},{24,0},{28,4},{1,25},{... | collective-permute-start | bytes 1179656 | tf_op jit(solution)/shard_map/ppermute | solution.py:64
  246.0 17.5 %collective-permute-start.33 = (f32[4,128]{1,0:T(4,128)}, f32[4,128]{1,0:T(4,128)S(1)}, u32[]{:S(2)}, u32[]{:S(2)}) collective-permute-start(f32[4,128]{1,0:T(4,128)} %bitcast.104), channel_id=1, source_target_pairs={{0,3},{1,0},{2,1},{3,2},{4,7},{5,4},{6,5},{7,6},{8,11},{9,8},{10,9... | collective-permute-start | bytes 6152 | tf_op jit(solution)/shard_map/ppermute | solution.py:229
  249.2 15.9 %collective-permute-start.34 = (f32[4,128]{1,0:T(4,128)}, f32[4,128]{1,0:T(4,128)S(1)}, u32[]{:S(2)}, u32[]{:S(2)}) collective-permute-start(f32[4,128]{1,0:T(4,128)} %bitcast.105), channel_id=1, source_target_pairs={{0,2},{1,3},{2,0},{3,1},{4,6},{5,7},{6,4},{7,5},{8,10},{9,11},{10,... | collective-permute-start | bytes 6152 | tf_op jit(solution)/shard_map/ppermute | solution.py:229
  249.2 15.9 %collective-permute-start.35 = (f32[4,128]{1,0:T(4,128)}, f32[4,128]{1,0:T(4,128)S(1)}, u32[]{:S(2)}, u32[]{:S(2)}) collective-permute-start(f32[4,128]{1,0:T(4,128)} %bitcast.106), channel_id=1, source_target_pairs={{0,1},{1,2},{2,3},{3,0},{4,5},{5,6},{6,7},{7,4},{8,9},{9,10},{10,1... | collective-permute-start | bytes 6152 | tf_op jit(solution)/shard_map/ppermute | solution.py:229
  251.1 14.7 %collective-permute-start.36 = (bf16[128,1536]{1,0:T(8,128)(2,1)S(1)}, bf16[128,1536]{1,0:T(8,128)(2,1)S(1)}, u32[]{:S(2)}, u32[]{:S(2)}) collective-permute-start(bf16[128,1536]{1,0:T(8,128)(2,1)S(1)} %add_convert_fusion.1.refs_0_), channel_id=1, source_target_pairs={{0,1},{1,2},{2,3},{3,0},{4,5},{5,6},{6,7},{7,4},{8,9},{9,10},{10,1... | collective-permute-start | bytes 1179656 | tf_op jit(solution)/shard_map/ppermute | solution.py:58
  254.2 23.2 %collective-permute-start.37 = (bf16[128,1536]{1,0:T(8,128)(2,1)S(1)}, bf16[128,1536]{1,0:T(8,128)(2,1)S(1)}, u32[]{:S(2)}, u32[]{:S(2)}) collective-permute-start(bf16[128,1536]{1,0:T(8,128)(2,1)S(1)} %add_convert_fusion.1.refs_0_), channel_id=1, source_target_pairs={{0,2},{1,3},{2,0},{3,1},{4,6},{5,7},{6,4},{7,5},{8,10},{9,11},{10,... | collective-permute-start | bytes 1179656 | tf_op jit(solution)/shard_map/ppermute | solution.py:58
  263.5 16.7 %collective-permute-start.38 = (bf16[128,1536]{1,0:T(8,128)(2,1)S(1)}, bf16[128,1536]{1,0:T(8,128)(2,1)S(1)}, u32[]{:S(2)}, u32[]{:S(2)}) collective-permute-start(bf16[128,1536]{1,0:T(8,128)(2,1)S(1)} %add_convert_fusion.1.refs_0_), channel_id=1, source_target_pairs={{0,3},{1,0},{2,1},{3,2},{4,7},{5,4},{6,5},{7,6},{8,11},{9,8},{10,9... | collective-permute-start | bytes 1179656 | tf_op jit(solution)/shard_map/ppermute | solution.py:58
  293.4 23.1 %collective-permute-start.42 = (bf16[512,1920]{1,0:T(8,128)(2,1)}, bf16[512,1920]{1,0:T(8,128)(2,1)}, u32[]{:S(2)}, u32[]{:S(2)}) collective-permute-start(bf16[512,1920]{1,0:T(8,128)(2,1)} %shard_map.368), channel_id=1, source_target_pairs={{0,4},{4,0},{8,12},{12,8},{16,20},{20,16},{24,28},{28,24},{1,5},{5... | collective-permute-start | bytes 5898248 | tf_op jit(solution)/shard_map/ppermute | solution.py:64
  299.2 23.3 %collective-permute-start.39 = (bf16[128,1024]{1,0:T(8,128)(2,1)}, bf16[128,1024]{1,0:T(8,128)(2,1)S(1)}, u32[]{:S(2)}, u32[]{:S(2)}) collective-permute-start(bf16[128,1024]{1,0:T(8,128)(2,1)} %get-tuple-element.199), channel_id=1, source_target_pairs={{0,1},{1,2},{2,3},{3,0},{4,5},{5,6},{6,7},{7,4},{8,9},{9,10},{10,1... | collective-permute-start | bytes 786440 | tf_op jit(solution)/shard_map/ppermute | solution.py:220
  305.3 19.4 %collective-permute-start.40 = (bf16[128,1024]{1,0:T(8,128)(2,1)}, bf16[128,1024]{1,0:T(8,128)(2,1)S(1)}, u32[]{:S(2)}, u32[]{:S(2)}) collective-permute-start(bf16[128,1024]{1,0:T(8,128)(2,1)} %get-tuple-element.200), channel_id=1, source_target_pairs={{0,2},{1,3},{2,0},{3,1},{4,6},{5,7},{6,4},{7,5},{8,10},{9,11},{10,... | collective-permute-start | bytes 786440 | tf_op jit(solution)/shard_map/ppermute | solution.py:220
  306.8 18.0 %collective-permute-start.41 = (bf16[128,1024]{1,0:T(8,128)(2,1)}, bf16[128,1024]{1,0:T(8,128)(2,1)S(1)}, u32[]{:S(2)}, u32[]{:S(2)}) collective-permute-start(bf16[128,1024]{1,0:T(8,128)(2,1)} %get-tuple-element.201), channel_id=1, source_target_pairs={{0,3},{1,0},{2,1},{3,2},{4,7},{5,4},{6,5},{7,6},{8,11},{9,8},{10,9... | collective-permute-start | bytes 786440 | tf_op jit(solution)/shard_map/ppermute | solution.py:220
  324.7 14.1 %collective-permute-start.45 = (bf16[128,1024]{1,0:T(8,128)(2,1)}, bf16[128,1024]{1,0:T(8,128)(2,1)S(1)}, u32[]{:S(2)}, u32[]{:S(2)}) collective-permute-start(bf16[128,1024]{1,0:T(8,128)(2,1)} %get-tuple-element.213), channel_id=1, source_target_pairs={{0,3},{1,0},{2,1},{3,2},{4,7},{5,4},{6,5},{7,6},{8,11},{9,8},{10,9... | collective-permute-start | bytes 786440 | tf_op jit(solution)/shard_map/ppermute | solution.py:220
  331.7 24.0 %collective-permute-start.44 = (bf16[128,1024]{1,0:T(8,128)(2,1)}, bf16[128,1024]{1,0:T(8,128)(2,1)}, u32[]{:S(2)}, u32[]{:S(2)}) collective-permute-start(bf16[128,1024]{1,0:T(8,128)(2,1)} %get-tuple-element.212), channel_id=1, source_target_pairs={{0,2},{1,3},{2,0},{3,1},{4,6},{5,7},{6,4},{7,5},{8,10},{9,11},{10,... | collective-permute-start | bytes 786440 | tf_op jit(solution)/shard_map/ppermute | solution.py:220
  332.3 23.4 %collective-permute-start.43 = (bf16[128,1024]{1,0:T(8,128)(2,1)}, bf16[128,1024]{1,0:T(8,128)(2,1)}, u32[]{:S(2)}, u32[]{:S(2)}) collective-permute-start(bf16[128,1024]{1,0:T(8,128)(2,1)} %get-tuple-element.211), channel_id=1, source_target_pairs={{0,1},{1,2},{2,3},{3,0},{4,5},{5,6},{6,7},{7,4},{8,9},{9,10},{10,1... | collective-permute-start | bytes 786440 | tf_op jit(solution)/shard_map/ppermute | solution.py:220
  332.9 34.7 %collective-permute-start.51 = (bf16[128,1920]{1,0:T(8,128)(2,1)}, bf16[128,1920]{1,0:T(8,128)(2,1)}, u32[]{:S(2)}, u32[]{:S(2)}) collective-permute-start(bf16[128,1920]{1,0:T(8,128)(2,1)} %get-tuple-element.205), channel_id=1, source_target_pairs={{0,24},{4,28},{8,16},{12,20},{16,8},{20,12},{24,0},{28,4},{1,25},{... | collective-permute-start | bytes 1474568 | tf_op jit(solution)/shard_map/ppermute | solution.py:64
  334.1 33.4 %collective-permute-start.50 = (bf16[128,1920]{1,0:T(8,128)(2,1)}, bf16[128,1920]{1,0:T(8,128)(2,1)}, u32[]{:S(2)}, u32[]{:S(2)}) collective-permute-start(bf16[128,1920]{1,0:T(8,128)(2,1)} %get-tuple-element.204), channel_id=1, source_target_pairs={{0,16},{4,20},{8,24},{12,28},{16,0},{20,4},{24,8},{28,12},{1,17},{... | collective-permute-start | bytes 1474568 | tf_op jit(solution)/shard_map/ppermute | solution.py:64
  338.8 28.8 %collective-permute-start.49 = (bf16[128,1920]{1,0:T(8,128)(2,1)}, bf16[128,1920]{1,0:T(8,128)(2,1)}, u32[]{:S(2)}, u32[]{:S(2)}) collective-permute-start(bf16[128,1920]{1,0:T(8,128)(2,1)} %get-tuple-element.203), channel_id=1, source_target_pairs={{0,8},{4,12},{8,0},{12,4},{16,24},{20,28},{24,16},{28,20},{1,9},{5... | collective-permute-start | bytes 1474568 | tf_op jit(solution)/shard_map/ppermute | solution.py:64
  369.4 11.4 %collective-permute-start.52 = (bf16[128,1920]{1,0:T(8,128)(2,1)S(1)}, bf16[128,1920]{1,0:T(8,128)(2,1)}, u32[]{:S(2)}, u32[]{:S(2)}) collective-permute-start(bf16[128,1920]{1,0:T(8,128)(2,1)S(1)} %add_convert_fusion.refs_0_), channel_id=1, source_target_pairs={{0,1},{1,2},{2,3},{3,0},{4,5},{5,6},{6,7},{7,4},{8,9},{9,10},{10,1... | collective-permute-start | bytes 1474568 | tf_op jit(solution)/shard_map/ppermute | solution.py:41
  380.8 11.8 %collective-permute-start.53 = (bf16[128,1920]{1,0:T(8,128)(2,1)}, bf16[128,1920]{1,0:T(8,128)(2,1)}, u32[]{:S(2)}, u32[]{:S(2)}) collective-permute-start(bf16[128,1920]{1,0:T(8,128)(2,1)} %collective-permute-done.52.refs_1_), channel_id=1, source_target_pairs={{0,1},{1,2},{2,3},{3,0},{4,5},{5,6},{6,7},{7,4},{8,9},{9,10},{10,1... | collective-permute-start | bytes 1474568 | tf_op jit(solution)/shard_map/ppermute | solution.py:41
  392.6 12.0 %collective-permute-start.54 = (bf16[128,1920]{1,0:T(8,128)(2,1)}, bf16[128,1920]{1,0:T(8,128)(2,1)S(1)}, u32[]{:S(2)}, u32[]{:S(2)}) collective-permute-start(bf16[128,1920]{1,0:T(8,128)(2,1)} %collective-permute-done.53.refs_2_), channel_id=1, source_target_pairs={{0,1},{1,2},{2,3},{3,0},{4,5},{5,6},{6,7},{7,4},{8,9},{9,10},{10,1... | collective-permute-start | bytes 1474568 | tf_op jit(solution)/shard_map/ppermute | solution.py:41
  (50 other events, 757.9 us)

commit v2 on v1

--- a/solution.py
+++ b/solution.py
@@ -46,10 +46,6 @@
     for _ in range(lax.axis_size("dp") - 1):
         blocks.append(next_peer(blocks[-1]))
     return blocks
-
-
-def peer_rows(x):
-    return jnp.concatenate(peer_blocks(x), 0)
 
 
 def peer_direct(x):
@@ -105,35 +101,25 @@
         total = total + outs[0][...].astype(F32)
         outs = outs[1:]
     total = total.astype(BF)
-    if blocks == 1:
-        outs[0][...] = total
-        return
+    rows = total.shape[0] // blocks
     for i in range(blocks):
-
-        @pl.when(pl.program_id(0) == i)
-        def _():
-            outs[i][...] = total
+        outs[i][...] = total[i * rows : (i + 1) * rows]
 
 
 def grads(pairs, low, high, add=None, blocks=1):
     depth = pairs[0][0].shape[0]
     height = high - low
     width = sum(r.shape[1] for _, r in pairs)
-    rows = min(height, 256) if blocks == 1 else height // blocks
-    first = low // rows
-    if blocks == 1:
-        out_shape = [jax.ShapeDtypeStruct((height, width), BF)]
-        out_specs = [pl.BlockSpec((rows, width), lambda i: (i, 0))]
-    else:
-        out_shape = [jax.ShapeDtypeStruct((rows, width), BF)] * blocks
-        out_specs = [pl.BlockSpec((rows, width), lambda i: (0, 0))] * blocks
+    rows = height // blocks
+    out_shape = [jax.ShapeDtypeStruct((rows, width), BF)] * blocks
+    out_specs = [pl.BlockSpec((rows, width), lambda i: (0, 0))] * blocks
     out = pl.pallas_call(
         functools.partial(grad_kernel, len(pairs), add is not None, blocks),
         out_shape=out_shape,
-        grid=(height // rows,),
-        in_specs=[pl.BlockSpec((depth, rows), lambda i: (0, i + first))] * len(pairs)
+        grid=(1,),
+        in_specs=[pl.BlockSpec((depth, height), lambda i: (0, low // height))] * len(pairs)
         + [pl.BlockSpec((depth, r.shape[1]), lambda i: (0, 0)) for _, r in pairs]
-        + ([] if add is None else [pl.BlockSpec((rows, width), lambda i: (i, 0))]),
+        + ([] if add is None else [pl.BlockSpec((height, width), lambda i: (0, 0))]),
         out_specs=out_specs,
         cost_estimate=pl.CostEstimate(
             flops=2 * depth * height * width,
@@ -142,6 +128,52 @@
         ),
     )(*[l for l, _ in pairs], *[r for _, r in pairs], *([] if add is None else [add]))
     return out[0] if blocks == 1 else out
+
+
+def slice_kernel(dims, rank_ref, *refs):
+    inner, channels, my_inner, my_heads, my_hidden, qc, my_q, per_kv, n = dims
+    w_in, w_q, w_k, w_v, w_o, w_out, w_gate, w_up, w_down, ab_ref, cd_ref = refs
+    rank = rank_ref[0]
+    kv = rank * my_q // per_kv
+
+    def wide(base, size):
+        return jnp.swapaxes(w_in[pl.ds(pl.multiple_of(base, 128), size), :], 0, 1)
+
+    def piece(ref, base, size):
+        return ref[:, pl.ds(pl.multiple_of(base + rank * size, 128), size)]
+
+    def pick(ref, base, size, which, count):
+        value = ref[:, base : base + size].astype(F32)
+        for i in range(1, count):
+            at = base + i * size
+            value = jnp.where(which == i, ref[:, at : at + size].astype(F32), value)
+        return value
+
+    heads = w_k.shape[1] // HD
+    dt_at = inner + channels
+    tail = w_in[dt_at : dt_at + n * my_heads, :].astype(F32)
+    tail = jnp.concatenate([tail, jnp.zeros((128 - n * my_heads, tail.shape[1]), F32)], 0)
+    tail = jnp.swapaxes(tail, 0, 1)
+    dt = tail[:, :my_heads]
+    for i in range(1, n):
+        dt = jnp.where(rank == i, tail[:, i * my_heads : (i + 1) * my_heads], dt)
+    blank = jnp.zeros((dt.shape[0], -my_heads % 128), F32)
+    parts = [
+        wide(rank * my_inner, my_inner),
+        wide(inner + rank * my_inner, my_inner),
+        wide(2 * inner, channels - inner),
+        piece(w_q, 0, qc),
+        jnp.concatenate([pick(w, 0, HD, kv, heads) for w in (w_k, w_v)], 1).astype(BF),
+        jnp.concatenate([dt, blank], 1).astype(BF),
+        piece(w_out, 0, my_inner),
+        piece(w_o, 0, qc),
+    ]
+    at = 0
+    for part in parts:
+        ab_ref[:, at : at + part.shape[1]] = part
+        at += part.shape[1]
+    for i, w in enumerate((w_gate, w_up, w_down)):
+        cd_ref[:, i * my_hidden : (i + 1) * my_hidden] = piece(w, 0, my_hidden)
 
 
 def reorder_kernel(back, count, at_ref, *refs):
@@ -239,18 +271,15 @@
 
 def sum_dp(v):
     n = lax.axis_size("dp")
-    if n & (n - 1):
-        return lax.psum(v, "dp")
-    got = [lax.ppermute(v, "dp", [(i, i ^ m) for i in range(n)]) for m in range(1, n)]
-    return sum_level([v] + got)
-
-
-def sum_fsdp(v):
-    n, step = lax.axis_size("fsdp"), 1
-    if n & (n - 1):
-        return lax.psum(v, "fsdp")
+    return [v] + [
+        lax.ppermute(v, "dp", [(i, i ^ m) for i in range(n)]) for m in range(1, n)
+    ]
+
+
+def sum_fsdp(v, step=1, stop=None):
+    n = stop or lax.axis_size("fsdp")
     while step < n:
-        v = v + lax.ppermute(v, "fsdp", [(i, i ^ step) for i in range(n)])
+        v = v + lax.ppermute(v, "fsdp", [(i, i ^ step) for i in range(lax.axis_size("fsdp"))])
         step *= 2
     return v
 
@@ -262,6 +291,10 @@
 def column(row):
     size = row.shape[1]
     return transposed(jnp.broadcast_to(row, (size, size)))
+
+
+def columns(ref):
+    return jnp.concatenate([column(ref[k])[:, :1] for k in range(ref.shape[0])], 0)
 
 
 def exact(a, b, dims):
@@ -361,9 +394,16 @@
 
 
 def branch_forward(
-    sizes, q_at, x_ref, a0_ref, a1_ref, g_ref, conv_ref, head_ref,
-    normed_ref, proj_ref, y_ref, gated_ref, square_ref, attn_ref,
+    sizes, n, *refs
 ):
+    a0_ref, a1_ref, g_ref, conv_ref, head_ref = refs[n : n + 5]
+    normed_ref, proj_ref, y_ref, gated_ref, square_ref, x_ref = refs[n + 5 :]
+    for k in range(n):
+
+        @pl.when(pl.program_id(0) == k)
+        def _():
+            x_ref[...] = refs[k][...]
+
     rows, inner, _, heads = sizes
     width = g_ref.shape[1]
     x32 = x_ref[:, :width].astype(F32)
@@ -392,43 +432,50 @@
     gated_ref[...] = gated
     square = jnp.sum(gated * gated, -1, keepdims=True)
     square_ref[0] = transposed(jnp.broadcast_to(square, (rows, rows)))[:1]
-    q, kv = proj[:, q_at : q_at + 128], proj[:, q_at + 128 : q_at + 256]
-    low, _, _, _, _, values, probs, _ = attn_common(q, kv, v["first"], v["keep"])
+
+
+def links(start):
+    shape = start.shape
+    t_col = lax.broadcasted_iota(jnp.int32, shape, 0)
+    s_row = lax.broadcasted_iota(jnp.int32, shape, 1)
+    return start[:, :1].astype(jnp.int32), (start == transposed(start)) & (s_row <= t_col)
+
+
+def attn_forward(x_ref, qkv_ref, attn_ref):
+    first, keep = links(x_ref[...].astype(F32))
+    low, _, _, _, _, values, probs, _ = attn_common(
+        qkv_ref[:, :128], qkv_ref[:, 128:], first, keep
+    )
     out = [quick(p, values, NN) for p in probs]
     attn_ref[...] = jnp.where(low, out[0], out[1]).astype(BF)
 
 
 def branch_back_out(
-    sizes, low, dm_ref, b0_ref, b1_ref, gated_ref, scale_ref, gm_ref,
-    d_scaled_ref, d_attn_ref, inner_ref, g_gm_ref,
+    inner, low, n, *refs
 ):
-    rows, inner, _, _ = sizes
-    d_mix = halved(dm_ref[...], b0_ref[:, low:], b1_ref[:, low:])
+    b0_ref, b1_ref, gated_ref, scale_ref, gm_ref = refs[n : n + 5]
+    d_scaled_ref, d_attn_ref, inner_ref, g_gm_ref, dm_ref = refs[n + 5 :]
+    dm = jnp.concatenate([r[...] for r in refs[:n]], 0)
+    dm_ref[...] = dm
+    d_mix = halved(dm, b0_ref[:, low:], b1_ref[:, low:])
     d_out = d_mix[:, :inner]
     gated = gated_ref[...]
-    scale = column(scale_ref[0])[:, :1]
-
-    @pl.when(pl.program_id(0) == 0)
-    def _():
-        g_gm_ref[...] = jnp.zeros_like(g_gm_ref)
-
-    g_gm_ref[...] += jnp.sum(d_out * gated * scale, 0, keepdims=True)
+    g_gm_ref[...] = jnp.sum(d_out * gated * columns(scale_ref), 0, keepdims=True)
     d_scaled = d_out * gm_ref[...]
     d_scaled_ref[...] = d_scaled
     dot = jnp.sum(d_scaled * gated, -1, keepdims=True)
-    inner_ref[0] = transposed(jnp.broadcast_to(dot, (rows, rows)))[:1]
+    rows = inner_ref.shape[2]
+    for k in range(inner_ref.shape[0]):
+        block = jnp.broadcast_to(dot[k * rows : (k + 1) * rows], (rows, rows))
+        inner_ref[k] = transposed(block)[:1]
     d_attn_ref[...] = d_mix[:, inner:]
 
 
-def branch_back_attn(q_at, x_ref, proj_ref, d_attn_ref, d_qkv_ref):
+def branch_back_attn(x_ref, qkv_ref, d_attn_ref, d_qkv_ref):
     start = x_ref[...].astype(F32)
     rows = start.shape[0]
-    t_col = lax.broadcasted_iota(jnp.int32, (rows, rows), 0)
-    s_row = lax.broadcasted_iota(jnp.int32, (rows, rows), 1)
-    keep = (start == transposed(start)) & (s_row <= t_col)
-    first = start[:, :1].astype(jnp.int32)
-    q = proj_ref[:, q_at : q_at + 128]
-    kv = proj_ref[:, q_at + 128 : q_at + 256]
+    first, keep = links(start)
+    q, kv = qkv_ref[:, :128], qkv_ref[:, 128:]
     low, cosine, sine, q_rot, keys, values, probs, picks = attn_common(q, kv, first, keep)
     d_attn = d_attn_ref[...]
     d_q = []
@@ -533,45 +580,47 @@
 
 def put_rows(outs, left, w0, w1):
     value = jnp.concatenate([mul_t(left, w0), mul_t(left, w1)], 1)
+    rows = left.shape[0] // len(outs)
     for k, o_ref in enumerate(outs):
-
-        @pl.when(pl.program_id(0) == k)
-        def _():
-            o_ref[...] = value.astype(o_ref.dtype)
+        o_ref[...] = value[k * rows : (k + 1) * rows].astype(o_ref.dtype)
+    return value
 
 
 def rows_out(n, rows, width):
-    spec = pl.BlockSpec((rows, width), lambda i: (0, 0))
-    shapes = [out_of((rows, width), F32)] + [out_of((rows, width), BF)] * (n - 1)
-    return [spec] * n, shapes
+    return [out_of((rows, width), F32)] + [out_of((rows, width), BF)] * (n - 1)
 
 
 def rows_kernel(low, high, left_ref, w0_ref, w1_ref, *outs):
     put_rows(outs, left_ref[...], w0_ref[:, low:high], w1_ref[:, low:high])
 
 
+def back_in_kernel(width, span, left_ref, x_ref, w0_ref, w1_ref, g_in_ref, *outs):
+    value = put_rows(outs, left_ref[...], w0_ref[:, :span], w1_ref[:, :span])
+    x32 = x_ref[:, :width].astype(F32)
+    scale = lax.rsqrt(jnp.mean(x32 * x32, -1, keepdims=True) + norm_eps)
+    g_in_ref[...] = jnp.sum(value * x32 * scale, 0, keepdims=True)
+
+
 def partial_rows(n, left, halves, low, high):
     rows, width = left.shape[0] // n, 2 * halves[0].shape[0]
-    specs, shapes = rows_out(n, rows, width)
     return pl.pallas_call(
-        functools.partial(rows_kernel, low, high),
-        grid=(n,),
-        in_specs=[row_spec(rows, left.shape[1])] + [fixed_spec(a) for a in halves],
-        out_specs=specs,
-        out_shape=shapes,
+        functools.partial(rows_kernel, low, high), out_shape=rows_out(n, rows, width)
     )(left, *halves)
 
 
 def mix_kernel(low, gated_ref, scale_ref, gm_ref, attn_ref, w0_ref, w1_ref, mix_ref, *outs):
-    scale = column(scale_ref[0])[:, :1]
+    scale = columns(scale_ref)
     mamba = (gated_ref[...] * scale * gm_ref[...]).astype(BF)
     mix = jnp.concatenate([mamba, attn_ref[...]], 1)
     mix_ref[...] = mix
     put_rows(outs, mix, w0_ref[:, low:], w1_ref[:, low:])
 
 
-def ffn_kernel(size, hid_ref, cot_ref, w0_ref, w1_ref, act_ref, d_gu_ref, *outs):
-    gu = halved(hid_ref[...], w0_ref[:, : 2 * size], w1_ref[:, : 2 * size])
+def ffn_kernel(size, n, *refs):
+    cot_ref, w0_ref, w1_ref, act_ref, d_gu_ref, hid_ref, *outs = refs[n:]
+    hid = jnp.concatenate([r[...] for r in refs[:n]], 0)
+    hid_ref[...] = hid
+    gu = halved(hid, w0_ref[:, : 2 * size], w1_ref[:, : 2 * size])
     gate, up = gu[:, :size], gu[:, size:]
     sig = jax.nn.sigmoid(gate)
     silu = gate * sig
@@ -636,7 +685,6 @@
     my_inner, my_heads, my_hidden, my_q = inner // n, heads // n, hidden // n, q_heads // n
     per_kv = q_heads // kv_heads
     assert heads % n == 0 and q_heads % n == 0 and hidden % n == 0 and per_kv % my_q == 0
-    kv = rank * my_q // per_kv
     both = channels - inner
     qc = my_q * HD
 
@@ -645,50 +693,48 @@
     assert rows <= 256
     start = (segment_ids - segment_ids[0]).astype(BF)
     start = jnp.broadcast_to(start[:, None], (rows, 128))
-    sh_a = jnp.concatenate(
-        [
-            cols(w_in, rank * my_inner, my_inner),
-            cols(w_in, inner + rank * my_inner, my_inner),
-            w_in[:, 2 * inner : inner + channels],
-            cols(w_q, rank * qc, qc),
-            cols(w_k, kv * HD, HD),
-            cols(w_v, kv * HD, HD),
-            cols(w_in, inner + channels + rank * my_heads, my_heads),
-            jnp.zeros((w_in.shape[0], tail_pad), BF),
-            cols(w_out, rank * my_inner, my_inner),
-            cols(w_o, rank * qc, qc),
+    o = 2 * my_inner + both
+    span = o + qc + 2 * HD + my_heads + tail_pad
+    mc = my_inner + qc
+    vmem = pl.BlockSpec(memory_space=pltpu.VMEM)
+    shards = (w_in.T, w_q, w_k, w_v, w_o, w_out, w_gate, w_up, w_down)
+    dims = (inner, channels, my_inner, my_heads, my_hidden, qc, my_q, per_kv, n)
+    sh_a, sh_b = pl.pallas_call(
+        functools.partial(slice_kernel, dims),
+        out_shape=[
+            out_of((w_in.shape[0], span + mc), BF),
+            out_of((w_in.shape[0], 3 * my_hidden), BF),
         ],
-        1,
-    )
-    sh_a, tokens, start = tie((sh_a, tokens, start))
+        in_specs=[pl.BlockSpec(memory_space=pltpu.SMEM)] + [vmem] * 9,
+        out_specs=[vmem] * 2,
+    )(rank.astype(jnp.int32).reshape(1), *shards)
     if cube:
         parts_a = gather_start(sh_a)
         tokens, cotangent, g_in, g_ff = reorder(
             [tokens, cotangent, g_in.reshape(1, width), g_ff.reshape(1, width)]
         )
-    first = peer_rows(jnp.concatenate([tokens, start], 1))
+    first = peer_blocks(jnp.concatenate([tokens, start], 1))
     if cube:
-        parts_a, first = tie((parts_a, first))
+        parts_a, tok_held = tie((parts_a, first[-2]))
         own_a = jnp.concatenate(parts_a, 0)
         halves_a = [own_a, flip(own_a, 1)]
+        tok_blocks, first = first, jnp.concatenate(first, 0)
     else:
+        tok_held = first[-2]
+        tok_blocks, first = first, jnp.concatenate(first, 0)
         full_a = lax.all_gather(sh_a, "fsdp", axis=0, tiled=True)
         halves_a = [full_a[: width // 2], full_a[width // 2 :]]
 
-    sh_b = jnp.concatenate(
-        [cols(w, rank * my_hidden, my_hidden) for w in (w_gate, w_up, w_down)], 1
-    )
     if cube:
         sh_b, parts_a = tie((sh_b, parts_a))
         parts_b = gather_start(sh_b)
-    cot_first, _ = tie((cotangent, first))
+    cot_first, _ = tie((cotangent, tok_held))
     cot_blocks = peer_direct(cot_first)
 
-    o = 2 * my_inner + both
-    mc = my_inner + qc
-    span = sh_a.shape[1] - mc
+    assert n == 4 and lax.axis_size("fsdp") & (lax.axis_size("fsdp") - 1) == 0
     assert rows == 128 and qc == 128 and 2 * HD == 128 and conv_weight.shape[0] == 4
     assert my_heads % 2 == 0 and both % 256 == 0 and inner // heads == HD
+    assert o % 256 == 0 and width % 128 == 0
     cw = jnp.concatenate(
         [cols(conv_weight, rank * my_inner, my_inner), conv_weight[:, inner:]], 1
     )
@@ -713,10 +759,11 @@
     gm = gm.reshape(1, my_inner)
     g_in_row = g_in.reshape(1, width)
     count = n * rows
-    normed, proj, y, gated, square, attn = pl.pallas_call(
-        functools.partial(branch_forward, sizes, o),
+    normed, proj, y, gated, square = pl.pallas_call(
+        functools.partial(branch_forward, sizes, n),
         grid=(n,),
-        in_specs=[row_spec(rows, first.shape[1])]
+        scratch_shapes=[pltpu.VMEM((rows, first.shape[1]), BF)],
+        in_specs=[fixed_spec(a) for a in tok_blocks]
         + [pl.BlockSpec((a.shape[0], span), lambda i: (0, 0)) for a in halves_a]
         + [fixed_spec(a) for a in (g_in_row, conv_p, head_p)],
         out_specs=[
@@ -725,7 +772,6 @@
             row_spec(rows, my_inner),
             row_spec(rows, my_inner),
             row_spec(1, 1, rows),
-            row_spec(rows, qc),
         ],
         out_shape=[
             out_of((count, width), BF),
@@ -733,24 +779,27 @@
             out_of((count, my_inner), F32),
             out_of((count, my_inner), F32),
             out_of((n, 1, rows), F32),
-            out_of((count, qc), BF),
         ],
-    )(first, *halves_a, g_in_row, conv_p, head_p)
+    )(*tok_blocks, *halves_a, g_in_row, conv_p, head_p)
     square = peer_scalar_sum(square.reshape(n, rows))
+    start_spec = pl.BlockSpec((rows, 128), lambda i: (i, width // 128))
+    qkv_spec = pl.BlockSpec((rows, 256), lambda i: (i, o // 256))
+    attn = pl.pallas_call(
+        attn_forward,
+        grid=(n,),
+        in_specs=[start_spec, qkv_spec],
+        out_specs=row_spec(rows, qc),
+        out_shape=out_of((count, qc), BF),
+    )(first, proj)
     scale_rows = lax.rsqrt(square / inner + norm_eps).reshape(n, 1, rows)
-    specs, shapes = rows_out(n, rows, width)
+    shapes = rows_out(n, rows, width)
     mix_in, *mix_parts = pl.pallas_call(
         functools.partial(mix_kernel, span),
-        grid=(n,),
-        in_specs=[row_spec(rows, my_inner), row_spec(1, 1, rows), fixed_spec(gm)]
-        + [row_spec(rows, qc)]
-        + [fixed_spec(a) for a in halves_a],
-        out_specs=[row_spec(rows, mc)] + specs,
         out_shape=[out_of((count, mc), BF)] + shapes,
     )(gated, scale_rows, gm, attn, *halves_a)
     mix_parts = peer_send(mix_parts)
     if cube:
-        mix_parts, parts_b, cot_blocks = tie((mix_parts, parts_b, cot_blocks))
+        mix_parts, cot_blocks = tie((mix_parts, cot_blocks))
         own_b = jnp.concatenate(parts_b, 0)
         halves_b = [own_b, flip(own_b, 1)]
     else:
@@ -760,15 +809,13 @@
     tok32 = tokens.astype(F32)
     mixed = tok32 + add_up(mix_parts)
     f_scale = rms_scale(mixed)
-    hid_all = peer_rows((mixed * f_scale * g_ff).astype(BF))
-    act, d_gu, *d_hidden = pl.pallas_call(
-        functools.partial(ffn_kernel, my_hidden),
-        grid=(n,),
-        in_specs=[row_spec(rows, width)] * 2 + [fixed_spec(a) for a in halves_b],
-        out_specs=[row_spec(rows, my_hidden), row_spec(rows, 2 * my_hidden)] + specs,
+    hid_blocks = peer_blocks((mixed * f_scale * g_ff).astype(BF))
+    act, d_gu, hid_all, *d_hidden = pl.pallas_call(
+        functools.partial(ffn_kernel, my_hidden, n),
         out_shape=[out_of((count, my_hidden), BF), out_of((count, 2 * my_hidden), BF)]
+        + [out_of((count, width), BF)]
         + shapes,
-    )(hid_all, cot_all, *halves_b)
+    )(*hid_blocks, cot_all, *halves_b)
     d_hidden = peer_send(d_hidden)
     c_pairs = [(hid_all, d_gu), (cot_all, act)]
     if cube:
@@ -779,54 +826,42 @@
         grad_c = grads(c_pairs, 0, width)
     d_mixed_n, grad_g_ff = rms_back(mixed, f_scale, g_ff, add_up(d_hidden))
     d_mixed = cotangent.astype(F32) + d_mixed_n
-    dm_all = peer_rows(d_mixed.astype(BF))
-    dm_all, grad_c = tie((dm_all, grad_c))
+    dm_blocks = peer_blocks(d_mixed.astype(BF))
+    dm_blocks, grad_c = tie((dm_blocks, grad_c))
     if cube:
         grad_c = add_up(grad_c).astype(BF)
     else:
         grad_c = lax.psum_scatter(grad_c, "fsdp", scatter_dimension=0, tiled=True)
-    start_all = first[:, width:]
     c_blocks = peer_direct(grad_c)
-    d_scaled, d_attn, m_inner, grad_gm = pl.pallas_call(
-        functools.partial(branch_back_out, sizes, span),
-        grid=(n,),
-        in_specs=[row_spec(rows, width)]
-        + [fixed_spec(a) for a in halves_a]
-        + [row_spec(rows, my_inner), row_spec(1, 1, rows), fixed_spec(gm)],
-        out_specs=[
-            row_spec(rows, my_inner),
-            row_spec(rows, qc),
-            row_spec(1, 1, rows),
-            fixed_spec(gm),
-        ],
+    out_parts = partial_rows(n, act, halves_b, 2 * my_hidden, 3 * my_hidden)
+    out_parts = peer_send(out_parts)
+    d_scaled, d_attn, m_inner, grad_gm, dm_all = pl.pallas_call(
+        functools.partial(branch_back_out, my_inner, span, n),
         out_shape=[
             out_of((count, my_inner), F32),
             out_of((count, qc), F32),
             out_of((n, 1, rows), F32),
             out_of((1, my_inner), F32),
+            out_of((count, width), BF),
         ],
-    )(dm_all, *halves_a, gated, scale_rows, gm)
-    act, d_attn, m_inner = tie((act, d_attn, m_inner))
+    )(*dm_blocks, *halves_a, gated, scale_rows, gm)
     d_qkv = pl.pallas_call(
-        functools.partial(branch_back_attn, o),
+        branch_back_attn,
         grid=(n,),
-        in_specs=[row_spec(rows, rows), row_spec(rows, span), row_spec(rows, qc)],
+        in_specs=[start_spec, qkv_spec, row_spec(rows, qc)],
         out_specs=row_spec(rows, 256),
         out_shape=out_of((count, 256), BF),
         cost_estimate=pl.CostEstimate(
             flops=30 * count * rows * 128, bytes_accessed=count * 5000, transcendentals=count * 512
         ),
-    )(start_all, proj, d_attn)
+    )(first, proj, d_attn)
     m_inner = peer_scalar_sum(m_inner.reshape(n, rows)).reshape(n, 1, rows)
-    act, _ = tie((act, d_qkv))
-    out_parts = partial_rows(n, act, halves_b, 2 * my_hidden, 3 * my_hidden)
-    out_parts = peer_send(out_parts)
-    m_inner, d_qkv, c_blocks = tie((m_inner, d_qkv, c_blocks))
+    m_inner, d_qkv = tie((m_inner, d_qkv))
     d_proj, g_conv, g_head, g_skip = pl.pallas_call(
         lambda *refs: branch_back_mamba(sizes, o, *refs[:10], float(inner), *refs[10:]),
         grid=(n,),
         in_specs=[
-            row_spec(rows, rows),
+            start_spec,
             row_spec(rows, span),
             row_spec(rows, my_inner),
             row_spec(rows, my_inner),
@@ -849,28 +884,15 @@
             out_of(head_p.shape, F32),
             out_of((1, my_inner), F32),
         ],
-    )(start_all, proj, y, gated, d_scaled, scale_rows, m_inner, d_qkv, conv_p, head_p)
+    )(first, proj, y, gated, d_scaled, scale_rows, m_inner, d_qkv, conv_p, head_p)
     a_pairs = [(dm_all, mix_in), (normed, d_proj)]
     if cube:
         got = scatter_first(a_pairs)
         d_proj, _ = tie((d_proj, a_pairs))
-    d_normed = partial_rows(n, d_proj, halves_a, 0, span)
-    if cube:
-        own = scatter_own(a_pairs, got)
-        grad_a = scatter_rest(own)
-        d_normed, out_parts, own = tie((d_normed, out_parts, own))
-        d_normed = peer_send(d_normed)
-        grad_a = add_up(grad_a).astype(BF)
-    else:
-        d_normed = peer_send(d_normed)
-        grad_a = lax.psum_scatter(
-            grads(a_pairs, 0, width), "fsdp", scatter_dimension=0, tiled=True
-        )
-    output = (mixed + add_up(out_parts)).astype(BF)
-    d_tok_n, grad_g_in = rms_back(tok32, rms_scale(tok32), g_in, add_up(d_normed))
-    grad_tokens = (d_mixed + d_tok_n).astype(BF)
-    if cube:
-        output, grad_tokens = reorder([output, grad_tokens], back=True)
+    grad_g_in, *d_normed = pl.pallas_call(
+        functools.partial(back_in_kernel, width, span),
+        out_shape=[out_of((1, width), F32)] + shapes,
+    )(d_proj, first, *halves_a)
 
     def place(v):
         spot = (jnp.arange(n) == rank).astype(F32)
@@ -900,9 +922,32 @@
     small += [head_row(g_al), head_row(g_ds), head_row(g_db)]
     flat = jnp.concatenate(small)
     flat = jnp.pad(flat, ((0, -flat.shape[0] % 8), (0, 0)))
-    flat, grad_a = tie((sum_dp(flat), grad_a))
-    a_blocks = peer_blocks(grad_a)
-    flat = sum_fsdp(flat)
+    flat = sum_dp(flat)
+
+    if cube:
+        own = scatter_own(a_pairs, got)
+        grad_a = scatter_rest(own)
+        d_normed, c_blocks, out_parts, own = tie((d_normed, c_blocks, out_parts, own))
+        d_normed = peer_send(d_normed)
+        grad_a = add_up(grad_a).astype(BF)
+    else:
+        d_normed = peer_send(d_normed)
+        grad_a = lax.psum_scatter(
+            grads(a_pairs, 0, width), "fsdp", scatter_dimension=0, tiled=True
+        )
+    output = (mixed + add_up(out_parts)).astype(BF)
+    d_tok_n, _ = rms_back(tok32, rms_scale(tok32), g_in, add_up(d_normed))
+    grad_tokens = (d_mixed + d_tok_n).astype(BF)
+    if cube:
+        output, grad_tokens = reorder([output, grad_tokens], back=True)
+
+    a_blocks = [grad_a, next_peer(grad_a)]
+    while len(a_blocks) < n:
+        a_blocks[-1], flat = tie((a_blocks[-1], flat))
+        a_blocks.append(next_peer(a_blocks[-1]))
+        if len(a_blocks) == 3:
+            flat = sum_fsdp(sum_level(flat), 1, 4)
+    flat = sum_fsdp(flat, 4)
 
     def kv_of(owner):
         return owner * my_q // per_kv

time: 413 us -> 399 us (0.966)
  waiting for transfers between devices: 200 us -> 150 us
  starting transfers between devices: 77.1 us -> 108 us
  local copies, waits for them, and re-layouts: 23 us -> 31.3 us
    ppermute x12, waiting for transfers between devices: 81.9 us -> 44.2 us  [next_peer(): return lax.ppermute(x, 'dp', [(i, (i + 1) % n) for i in range(n)])]
    ppermute x16, waiting for transfers between devices: 22.1 us -> 40.5 us  [flip(): return lax.ppermute(x, 'fsdp', [(i, i ^ bits) for i in range(size)])]
    ppermute x6, waiting for transfers between devices: 22 us -> 5.47 us  [peer_scalar_sum(): got = lax.ppermute(v, 'dp', [(i, (i - m) % n) for i in range(n)])]
    ppermute x6, waiting for transfers between devices: 14.5 us -> 0.02 us  [peer_direct(): lax.ppermute(x, 'dp', [(i, (i + k) % n) for i in range(n)])]
    ppermute x3, starting transfers between devices: 1.94 us -> 14.7 us  [sum_dp(): lax.ppermute(v, 'dp', [(i, i ^ m) for i in range(n)])]
    ppermute x12, starting transfers between devices: 20.1 us -> 31.9 us  [next_peer(): return lax.ppermute(x, 'dp', [(i, (i + 1) % n) for i in range(n)])]
    unnamed x93 -> x114, local copies, waits for them, and re-layouts: 6.78 us -> 13.6 us
    ppermute x6, starting transfers between devices: 6.11 us -> 12.4 us  [peer_direct(): lax.ppermute(x, 'dp', [(i, (i + k) % n) for i in range(n)])]
  transfers between devices with their start and end apart: 58 -> 58, of which waited for: 32 -> 27; matrix products, arithmetic and copies ran while one was open for 6% -> 9% of each run, Pallas kernels for 11% -> 14%
where the time goes in v2:
time: 399 us; the launch traced here: 398 us
  waiting for transfers between devices  150 us (38%)
  starting transfers between devices  108 us (27%)
  Pallas kernels  89.4 us (22%)
  local copies, waits for them, and re-layouts  31.3 us (8%)
  other arithmetic  18 us (5%)
    ppermute x12, waiting for transfers between devices, peer_send(): lax.ppermute(blocks[k], 'dp', [(i, (i - k) % n) for i in range(n)])  54 us
    ppermute x12, waiting for transfers between devices, next_peer(): return lax.ppermute(x, 'dp', [(i, (i + 1) % n) for i in range(n)])  44.2 us
    ppermute x16, waiting for transfers between devices, flip(): return lax.ppermute(x, 'fsdp', [(i, i ^ bits) for i in range(size)])  40.5 us
    ppermute x12, starting transfers between devices, next_peer(): return lax.ppermute(x, 'dp', [(i, (i + 1) % n) for i in range(n)])  31.9 us
    ppermute x12, starting transfers between devices, peer_send(): lax.ppermute(blocks[k], 'dp', [(i, (i - k) % n) for i in range(n)])  21.7 us
    pallas_call x4, Pallas kernels, grads(): pl.pallas_call(functools.partial(grad_kernel, len(pairs), add is not None...  17.7 us
    ppermute x16, starting transfers between devices, flip(): return lax.ppermute(x, 'fsdp', [(i, i ^ bits) for i in range(size)])  15.2 us
    ppermute x3, starting transfers between devices, sum_dp(): lax.ppermute(v, 'dp', [(i, i ^ m) for i in range(n)])  14.7 us
  transfers between devices with their start and end apart: 58, of which 27 were waited for; matrix products, arithmetic and copies ran while one was open for 9% of the time, Pallas kernels for 14%

profile of v2, /device:TPU:0, one launch (start us, length us, event | category | flops | bytes accessed | tf_op | source)
XLA Modules:
  0.0 398.0 jit_solution(5748277526144309133)
XLA Ops:
  5.6 3.1 collective-permute-start
  8.7 3.1 shard_map.358
  17.9 9.4 %collective-permute-done.5 = bf16[128,1920]{1,0:T(8,128)(2,1)S(1)} collective-permute-done((bf16[128,1920]{1,0:T(8,128)(2,1)}, bf16[128,1920]{1,0:T(8,128)(2,1)S(1)}, u32[]{:S(2)}, u32[]{:S(2)}) %collective-permute-start.5) | collective-permute-done | bytes 491552 | tf_op jit(solution)/shard_map/ppermute | solution.py:60
  27.2 9.1 %collective-permute-done.4 = bf16[128,1920]{1,0:T(8,128)(2,1)S(1)} collective-permute-done((bf16[128,1920]{1,0:T(8,128)(2,1)}, bf16[128,1920]{1,0:T(8,128)(2,1)S(1)}, u32[]{:S(2)}, u32[]{:S(2)}) %collective-permute-start.4) | collective-permute-done | bytes 491552 | tf_op jit(solution)/shard_map/ppermute | solution.py:60
  49.6 11.2 %collective-permute-done.2.refs_3_ = bf16[128,1152]{1,0:T(8,128)(2,1)S(1)} collective-permute-done((bf16[128,1152]{1,0:T(8,128)(2,1)}, bf16[128,1152]{1,0:T(8,128)(2,1)S(1)}, u32[]{:S(2)}, u32[]{:S(2)}) %collective-permute-start.2) | collective-permute-done | bytes 294944 | tf_op jit(solution)/shard_map/ppermute | solution.py:41
  60.7 5.0 %collective-permute-start.13 = (bf16[128,1024]{1,0:T(8,128)(2,1)}, bf16[128,1024]{1,0:T(8,128)(2,1)}, u32[]{:S(2)}, u32[]{:S(2)}) collective-permute-start(bf16[128,1024]{1,0:T(8,128)(2,1)} %get-tuple-element.147), channel_id=1, source_target_pairs={{0,1},{1,2},{2,3},{3,0},{4,5},{5,6},{6,7},{7,4},{8,9},{9,10},{10,1... | collective-permute-start | bytes 786440 | tf_op jit(solution)/shard_map/ppermute | solution.py:54
  69.6 9.4 %shard_map.359 = (bf16[512,1024]{1,0:T(8,128)(2,1)}, f32[512,1408]{1,0:T(8,128)}, f32[512,384]{1,0:T(8,128)}, f32[512,384]{1,0:T(8,128)}, f32[4,1,128]{2,1,0:T(1,128)}) custom-call(bf16[128,1152]{1,0:T(8,128)(2,1)} %copy-done.10, bf16[128,1152]{1,0:T(8,128)(2,1)} %collective-permute-done.refs_1_, bf16[128,1152]{1,0:T(8,128)(2,1)} %collective-permute-done.1.refs_2_, ...), custom_call_target="tpu_custom_call" | custom-call | tf_op jit(solution)/shard_map/pallas_call | solution.py:762
  80.1 5.9 %shard_map.360.attn_ref = bf16[512,128]{1,0:T(8,128)(2,1)} custom-call(bf16[512,1152]{1,0:T(8,128)(2,1)} %pad_maximum_fusion.x_ref.refs_0_, f32[512,1408]{1,0:T(8,128)} %get-tuple-element.135.qkv_ref.refs_1_), custom_call_target="tpu_custom_call" | custom-call | tf_op jit(solution)/shard_map/pallas_call | solution.py:787
  86.0 3.9 collective-permute-start.8
  92.9 3.9 collective-permute-done.9
  98.8 4.5 %shard_map.361 = (bf16[512,512]{1,0:T(8,128)(2,1)}, f32[128,1024]{1,0:T(8,128)}, bf16[128,1024]{1,0:T(8,128)(2,1)}, bf16[128,1024]{1,0:T(8,128)(2,1)}, bf16[128,1024]{1,0:T(8,128)(2,1)}) custom-call(f32[512,384]{1,0:T(8,128)} %get-tuple-element.133.gated_ref.refs_6_.refs_3_, f32[4,1,128]{2,1,0:T(1,128)} %add_rsqrt_fusion.scale_ref.refs_7_.refs_5_, ...), custom_call_target="tpu_custom_call" | custom-call | tf_op jit(solution)/shard_map/pallas_call | solution.py:796
  108.5 6.0 %collective-permute-done.10 = bf16[128,1024]{1,0:T(8,128)(2,1)S(1)} collective-permute-done((bf16[128,1024]{1,0:T(8,128)(2,1)}, bf16[128,1024]{1,0:T(8,128)(2,1)S(1)}, u32[]{:S(2)}, u32[]{:S(2)}) %collective-permute-start.10) | collective-permute-done | bytes 262176 | tf_op jit(solution)/shard_map/ppermute | solution.py:252
  114.5 7.3 %collective-permute-done.11 = bf16[128,1024]{1,0:T(8,128)(2,1)S(1)} collective-permute-done((bf16[128,1024]{1,0:T(8,128)(2,1)}, bf16[128,1024]{1,0:T(8,128)(2,1)S(1)}, u32[]{:S(2)}, u32[]{:S(2)}) %collective-permute-start.11) | collective-permute-done | bytes 262176 | tf_op jit(solution)/shard_map/ppermute | solution.py:252
  123.3 8.1 %collective-permute-start.16 = (bf16[128,1024]{1,0:T(8,128)(2,1)S(1)}, bf16[128,1024]{1,0:T(8,128)(2,1)S(1)}, u32[]{:S(2)}, u32[]{:S(2)}) collective-permute-start(bf16[128,1024]{1,0:T(8,128)(2,1)S(1)} %multiply_convert_fusion.refs_0_), channel_id=1, source_target_pairs={{0,1},{1,2},{2,3},{3,0},{4,5},{5,6},{6,7},{7,4},{8,9},{9,10},{10,1... | collective-permute-start | bytes 786440 | tf_op jit(solution)/shard_map/ppermute | solution.py:41
  131.4 6.0 %collective-permute-done.16.refs_1_ = bf16[128,1024]{1,0:T(8,128)(2,1)S(1)} collective-permute-done((bf16[128,1024]{1,0:T(8,128)(2,1)S(1)}, bf16[128,1024]{1,0:T(8,128)(2,1)S(1)}, u32[]{:S(2)}, u32[]{:S(2)}) %collective-permute-start.16) | collective-permute-done | bytes 262176 | tf_op jit(solution)/shard_map/ppermute | solution.py:41
  140.9 7.3 %collective-permute-done.17.refs_2_ = bf16[128,1024]{1,0:T(8,128)(2,1)S(1)} collective-permute-done((bf16[128,1024]{1,0:T(8,128)(2,1)S(1)}, bf16[128,1024]{1,0:T(8,128)(2,1)S(1)}, u32[]{:S(2)}, u32[]{:S(2)}) %collective-permute-start.17) | collective-permute-done | bytes 262176 | tf_op jit(solution)/shard_map/ppermute | solution.py:41
  152.8 3.7 collective-permute-done.18.refs_3_
  156.5 6.9 %shard_map.362 = (bf16[512,512]{1,0:T(8,128)(2,1)}, bf16[512,1024]{1,0:T(8,128)(2,1)}, bf16[512,1024]{1,0:T(8,128)(2,1)}, f32[128,1024]{1,0:T(8,128)}, bf16[128,...) custom-call(bf16[128,1024]{1,0:T(8,128)(2,1)} %copy-done.12, bf16[128,1024]{1,0:T(8,128)(2,1)} %copy-done.29, ...), custom_call_target="tpu_custom_call" | custom-call | tf_op jit(solution)/shard_map/pallas_call | solution.py:813
  163.4 3.9 shard_map.363
  167.8 3.3 collective-permute-start.25
  172.4 4.3 %shard_map.364 = (bf16[128,1536]{1,0:T(8,128)(2,1)}, bf16[128,1536]{1,0:T(8,128)(2,1)}, bf16[128,1536]{1,0:T(8,128)(2,1)}, bf16[128,1536]{1,0:T(8,128)(2,1)}) custom-call(bf16[512,1024]{1,0:T(8,128)(2,1)} %get-tuple-element.157.refs_0_, bf16[512,1024]{1,0:T(8,128)(2,1)} %copy-done.1, bf16[512,1024]{1,0:T(8,128)(2,1)} %get-tuple-element.158.refs_2_, ...), custom_call_target="tpu_custom_call" | custom-call | flops 805306368 | bytes 4194304 | tf_op jit(solution)/shard_map/pallas_call | solution.py:116
  178.7 10.3 %collective-permute-done.24 = bf16[128,1024]{1,0:T(8,128)(2,1)S(1)} collective-permute-done((bf16[128,1024]{1,0:T(8,128)(2,1)}, bf16[128,1024]{1,0:T(8,128)(2,1)S(1)}, u32[]{:S(2)}, u32[]{:S(2)}) %collective-permute-start.24) | collective-permute-done | bytes 262176 | tf_op jit(solution)/shard_map/ppermute | solution.py:252
  192.3 5.1 %collective-permute-start.27 = (bf16[128,1024]{1,0:T(8,128)(2,1)S(1)}, bf16[128,1024]{1,0:T(8,128)(2,1)S(1)}, u32[]{:S(2)}, u32[]{:S(2)}) collective-permute-start(bf16[128,1024]{1,0:T(8,128)(2,1)S(1)} %fusion.11.refs_0_), channel_id=1, source_target_pairs={{0,1},{1,2},{2,3},{3,0},{4,5},{5,6},{6,7},{7,4},{8,9},{9,10},{10,1... | collective-permute-start | bytes 786440 | tf_op jit(solution)/shard_map/ppermute | solution.py:41
  197.5 5.3 %collective-permute-done.27.refs_1_ = bf16[128,1024]{1,0:T(8,128)(2,1)S(1)} collective-permute-done((bf16[128,1024]{1,0:T(8,128)(2,1)S(1)}, bf16[128,1024]{1,0:T(8,128)(2,1)S(1)}, u32[]{:S(2)}, u32[]{:S(2)}) %collective-permute-start.27) | collective-permute-done | bytes 262176 | tf_op jit(solution)/shard_map/ppermute | solution.py:41
  208.8 2.8 collective-permute-done.28.refs_2_
  212.2 5.0 %collective-permute-done.30 = bf16[128,1536]{1,0:T(8,128)(2,1)S(1)} collective-permute-done((bf16[128,1536]{1,0:T(8,128)(2,1)S(1)}, bf16[128,1536]{1,0:T(8,128)(2,1)S(1)}, u32[]{:S(2)}, u32[]{:S(2)}) %collective-permute-start.30) | collective-permute-done | bytes 393248 | tf_op jit(solution)/shard_map/ppermute | solution.py:60
  217.5 5.9 %collective-permute-done.32 = bf16[128,1536]{1,0:T(8,128)(2,1)S(1)} collective-permute-done((bf16[128,1536]{1,0:T(8,128)(2,1)S(1)}, bf16[128,1536]{1,0:T(8,128)(2,1)S(1)}, u32[]{:S(2)}, u32[]{:S(2)}) %collective-permute-start.32) | collective-permute-done | bytes 393248 | tf_op jit(solution)/shard_map/ppermute | solution.py:60
  223.5 4.8 %shard_map.365 = (f32[512,384]{1,0:T(8,128)}, f32[512,128]{1,0:T(8,128)}, f32[4,1,128]{2,1,0:T(1,128)}, f32[1,384]{1,0:T(1,128)}, bf16[512,1024]{1,0:T(8,128)(2,1)}) custom-call(bf16[128,1024]{1,0:T(8,128)(2,1)} %copy-done.11, bf16[128,1024]{1,0:T(8,128)(2,1)} %copy-done.26, bf16[128,1024]{1,0:T(8,128)(2,1)} %copy-done.27, ...), custom_call_target="tpu_custom_call" | custom-call | tf_op jit(solution)/shard_map/pallas_call | solution.py:838
  232.2 8.3 %shard_map.366.refs_7_ = bf16[512,256]{1,0:T(8,128)(2,1)} custom-call(bf16[512,1152]{1,0:T(8,128)(2,1)} %pad_maximum_fusion.x_ref.refs_0_, f32[512,1408]{1,0:T(8,128)} %get-tuple-element.135.qkv_ref.refs_1_, f32[512,128]{1,0:T(8,128)} %get-tuple-element.174.d_attn_ref), custom_call_target="tpu_custom_call" | custom-call | flops 251658240 | bytes 2560000 | tf_op jit(solution)/shard_map/pallas_call | solution.py:848
  241.1 8.8 %shard_map.367 = (bf16[512,1408]{1,0:T(8,128)(2,1)}, f32[8,640]{1,0:T(8,128)}, f32[8,128]{1,0:T(8,128)}, f32[1,384]{1,0:T(1,128)}) custom-call(bf16[512,1152]{1,0:T(8,128)(2,1)} %pad_maximum_fusion.x_ref.refs_0_, f32[512,1408]{1,0:T(8,128)} %get-tuple-element.135.qkv_ref.refs_1_, f32[512,384]{1,0:T(8,128)} %get-tuple-element.145.refs_2_, ...), custom_call_target="tpu_custom_call" | custom-call | tf_op jit(solution)/shard_map/pallas_call | solution.py:860
  250.0 4.5 %shard_map.370 = bf16[512,1920]{1,0:T(8,128)(2,1)} custom-call(bf16[512,1024]{1,0:T(8,128)(2,1)} %get-tuple-element.178.refs_0_, bf16[512,1024]{1,0:T(8,128)(2,1)} %get-tuple-element.180.refs_1_, bf16[512,512]{1,0:T(8,128)(2,1)} %get-tuple-element.179.refs_2_, bf16[512,1408]{1,0:T(8,128)(2,1)} %get-tuple-element.181.left_ref.refs_3_), custom_call_target="tpu_custom_call" | custom-call | flops 1006632960 | bytes 4980736 | tf_op jit(solution)/shard_map/pallas_call | solution.py:116
  255.3 3.8 shard_map.369
  261.4 5.0 %shard_map.371 = (bf16[128,1920]{1,0:T(8,128)(2,1)}, bf16[128,1920]{1,0:T(8,128)(2,1)}, bf16[128,1920]{1,0:T(8,128)(2,1)}, bf16[128,1920]{1,0:T(8,128)(2,1)}) custom-call(bf16[512,1024]{1,0:T(8,128)(2,1)} %get-tuple-element.178.refs_0_, bf16[512,1024]{1,0:T(8,128)(2,1)} %get-tuple-element.180.refs_1_, bf16[512,512]{1,0:T(8,128)(2,1)} %get-tuple-element.179.refs_2_, ...), custom_call_target="tpu_custom_call" | custom-call | flops 1006632960 | bytes 4980736 | tf_op jit(solution)/shard_map/pallas_call | solution.py:116
  270.9 5.8 %shard_map.368 = (f32[1,1024]{1,0:T(1,128)}, f32[128,1024]{1,0:T(8,128)}, bf16[128,1024]{1,0:T(8,128)(2,1)}, bf16[128,1024]{1,0:T(8,128)(2,1)}, bf16[128,1024]{1,0:T(8,128)(2,1)}) custom-call(bf16[512,1408]{1,0:T(8,128)(2,1)} %get-tuple-element.181.left_ref.refs_3_, bf16[512,1152]{1,0:T(8,128)(2,1)} %pad_maximum_fusion.x_ref.refs_0_, ...), custom_call_target="tpu_custom_call" | custom-call | tf_op jit(solution)/shard_map/pallas_call | solution.py:892
  280.7 2.9 collective-permute-start.38
  283.6 8.1 %collective-permute-done.47 = bf16[128,1920]{1,0:T(8,128)(2,1)S(1)} collective-permute-done((bf16[128,1920]{1,0:T(8,128)(2,1)}, bf16[128,1920]{1,0:T(8,128)(2,1)S(1)}, u32[]{:S(2)}, u32[]{:S(2)}) %collective-permute-start.47) | collective-permute-done | bytes 491552 | tf_op jit(solution)/shard_map/ppermute | solution.py:60
  301.5 3.7 concatenate.104
  305.9 15.9 %collective-permute-done.41 = bf16[128,1024]{1,0:T(8,128)(2,1)S(1)} collective-permute-done((bf16[128,1024]{1,0:T(8,128)(2,1)}, bf16[128,1024]{1,0:T(8,128)(2,1)S(1)}, u32[]{:S(2)}, u32[]{:S(2)}) %collective-permute-start.41) | collective-permute-done | bytes 262176 | tf_op jit(solution)/shard_map/ppermute | solution.py:252
  322.8 13.6 %collective-permute-start.51 = (f32[104,128]{1,0:T(8,128)}, f32[104,128]{1,0:T(8,128)}, u32[]{:S(2)}, u32[]{:S(2)}) collective-permute-start(f32[104,128]{1,0:T(8,128)} %pad.27), channel_id=1, source_target_pairs={{0,2},{1,3},{2,0},{3,1},{4,6},{5,7},{6,4},{7,5},{8,10},{9,11},{10,... | collective-permute-start | bytes 159752 | tf_op jit(solution)/shard_map/ppermute | solution.py:275
  338.5 7.4 %collective-permute-start.44 = (bf16[128,1024]{1,0:T(8,128)(2,1)}, bf16[128,1024]{1,0:T(8,128)(2,1)S(1)}, u32[]{:S(2)}, u32[]{:S(2)}) collective-permute-start(bf16[128,1024]{1,0:T(8,128)(2,1)} %get-tuple-element.204), channel_id=1, source_target_pairs={{0,2},{1,3},{2,0},{3,1},{4,6},{5,7},{6,4},{7,5},{8,10},{9,11},{10,... | collective-permute-start | bytes 786440 | tf_op jit(solution)/shard_map/ppermute | solution.py:252
  346.0 2.6 collective-permute-done.51
  349.7 3.2 shard_map.374
  354.8 12.6 %collective-permute-done.44 = bf16[128,1024]{1,0:T(8,128)(2,1)S(1)} collective-permute-done((bf16[128,1024]{1,0:T(8,128)(2,1)}, bf16[128,1024]{1,0:T(8,128)(2,1)S(1)}, u32[]{:S(2)}, u32[]{:S(2)}) %collective-permute-start.44) | collective-permute-done | bytes 262176 | tf_op jit(solution)/shard_map/ppermute | solution.py:252
  368.9 3.1 collective-permute-done.55
  377.8 5.0 %collective-permute-start.56 = (bf16[128,1920]{1,0:T(8,128)(2,1)}, bf16[128,1920]{1,0:T(8,128)(2,1)S(1)}, u32[]{:S(2)}, u32[]{:S(2)}) collective-permute-start(bf16[128,1920]{1,0:T(8,128)(2,1)} %collective-permute-done.53.refs_2_), channel_id=1, source_target_pairs={{0,1},{1,2},{2,3},{3,0},{4,5},{5,6},{6,7},{7,4},{8,9},{9,10},{10,1... | collective-permute-start | bytes 1474568 | tf_op jit(solution)/shard_map/ppermute | solution.py:41
  385.7 5.5 %collective-permute-done.56.refs_3_ = bf16[128,1920]{1,0:T(8,128)(2,1)S(1)} collective-permute-done((bf16[128,1920]{1,0:T(8,128)(2,1)}, bf16[128,1920]{1,0:T(8,128)(2,1)S(1)}, u32[]{:S(2)}, u32[]{:S(2)}) %collective-permute-start.56) | collective-permute-done | bytes 491552 | tf_op jit(solution)/shard_map/ppermute | solution.py:41
  392.0 3.3 shard_map.373
  395.3 2.7 copy.61
  (297 shorter events, 106.2 us)
Async XLA Ops:
  5.6 12.2 %collective-permute-start = (bf16[128,1152]{1,0:T(8,128)(2,1)S(1)}, bf16[128,1152]{1,0:T(8,128)(2,1)}, u32[]{:S(2)}, u32[]{:S(2)}) collective-permute-start(bf16[128,1152]{1,0:T(8,128)(2,1)S(1)} %pad_maximum_fusion.1.refs_0_), channel_id=1, source_target_pairs={{0,1},{1,2},{2,3},{3,0},{4,5},{5,6},{6,7},{7,4},{8,9},{9,10},{10,1... | collective-permute-start | bytes 884744 | tf_op jit(solution)/shard_map/ppermute | solution.py:41
  11.9 15.3 %collective-permute-start.5 = (bf16[128,1920]{1,0:T(8,128)(2,1)}, bf16[128,1920]{1,0:T(8,128)(2,1)S(1)}, u32[]{:S(2)}, u32[]{:S(2)}) collective-permute-start(bf16[128,1920]{1,0:T(8,128)(2,1)} %get-tuple-element.128), channel_id=1, source_target_pairs={{0,24},{4,28},{8,16},{12,20},{16,8},{20,12},{24,0},{28,4},{1,25},{... | collective-permute-start | bytes 1474568 | tf_op jit(solution)/shard_map/ppermute | solution.py:60
  14.4 21.9 %collective-permute-start.4 = (bf16[128,1920]{1,0:T(8,128)(2,1)}, bf16[128,1920]{1,0:T(8,128)(2,1)S(1)}, u32[]{:S(2)}, u32[]{:S(2)}) collective-permute-start(bf16[128,1920]{1,0:T(8,128)(2,1)} %get-tuple-element.128), channel_id=1, source_target_pairs={{0,16},{4,20},{8,24},{12,28},{16,0},{20,4},{24,8},{28,12},{1,17},{... | collective-permute-start | bytes 1474568 | tf_op jit(solution)/shard_map/ppermute | solution.py:60
  14.9 21.5 %collective-permute-start.3 = (bf16[128,1920]{1,0:T(8,128)(2,1)}, bf16[128,1920]{1,0:T(8,128)(2,1)S(1)}, u32[]{:S(2)}, u32[]{:S(2)}) collective-permute-start(bf16[128,1920]{1,0:T(8,128)(2,1)} %get-tuple-element.128), channel_id=1, source_target_pairs={{0,8},{4,12},{8,0},{12,4},{16,24},{20,28},{24,16},{28,20},{1,9},{5... | collective-permute-start | bytes 1474568 | tf_op jit(solution)/shard_map/ppermute | solution.py:60
  17.9 18.5 %collective-permute-start.1 = (bf16[128,1152]{1,0:T(8,128)(2,1)}, bf16[128,1152]{1,0:T(8,128)(2,1)}, u32[]{:S(2)}, u32[]{:S(2)}) collective-permute-start(bf16[128,1152]{1,0:T(8,128)(2,1)} %collective-permute-done.refs_1_), channel_id=1, source_target_pairs={{0,1},{1,2},{2,3},{3,0},{4,5},{5,6},{6,7},{7,4},{8,9},{9,10},{10,1... | collective-permute-start | bytes 884744 | tf_op jit(solution)/shard_map/ppermute | solution.py:41
  37.7 30.3 %collective-permute-start.6 = (bf16[512,1920]{1,0:T(8,128)(2,1)S(1)}, bf16[512,1920]{1,0:T(8,128)(2,1)}, u32[]{:S(2)}, u32[]{:S(2)}) collective-permute-start(bf16[512,1920]{1,0:T(8,128)(2,1)S(1)} %constant_dynamic-update-slice_fusion.refs_4_.w0_ref), channel_id=1, source_target_pairs={{0,4},{4,0},{8,12},{12,8},{16,20},{20,16},{24,28},{28,24},{1,5},{5... | collective-permute-start | bytes 5898248 | tf_op jit(solution)/shard_map/ppermute | solution.py:60
  37.7 65.5 %collective-permute-start.15 = (bf16[128,1024]{1,0:T(8,128)(2,1)}, bf16[128,1024]{1,0:T(8,128)(2,1)}, u32[]{:S(2)}, u32[]{:S(2)}) collective-permute-start(bf16[128,1024]{1,0:T(8,128)(2,1)} %get-tuple-element.147), channel_id=1, source_target_pairs={{0,3},{1,0},{2,1},{3,2},{4,7},{5,4},{6,5},{7,6},{8,11},{9,8},{10,9... | collective-permute-start | bytes 786440 | tf_op jit(solution)/shard_map/ppermute | solution.py:54
  40.2 68.3 %collective-permute-start.14 = (bf16[128,1024]{1,0:T(8,128)(2,1)}, bf16[128,1024]{1,0:T(8,128)(2,1)}, u32[]{:S(2)}, u32[]{:S(2)}) collective-permute-start(bf16[128,1024]{1,0:T(8,128)(2,1)} %get-tuple-element.147), channel_id=1, source_target_pairs={{0,2},{1,3},{2,0},{3,1},{4,6},{5,7},{6,4},{7,5},{8,10},{9,11},{10,... | collective-permute-start | bytes 786440 | tf_op jit(solution)/shard_map/ppermute | solution.py:54
  44.8 15.9 %collective-permute-start.2 = (bf16[128,1152]{1,0:T(8,128)(2,1)}, bf16[128,1152]{1,0:T(8,128)(2,1)S(1)}, u32[]{:S(2)}, u32[]{:S(2)}) collective-permute-start(bf16[128,1152]{1,0:T(8,128)(2,1)} %collective-permute-done.1.refs_2_), channel_id=1, source_target_pairs={{0,1},{1,2},{2,3},{3,0},{4,5},{5,6},{6,7},{7,4},{8,9},{9,10},{10,1... | collective-permute-start | bytes 884744 | tf_op jit(solution)/shard_map/ppermute | solution.py:41
  47.0 32.0 %collective-permute-start.19 = (bf16[128,1536]{1,0:T(8,128)(2,1)}, bf16[128,1536]{1,0:T(8,128)(2,1)}, u32[]{:S(2)}, u32[]{:S(2)}) collective-permute-start(bf16[128,1536]{1,0:T(8,128)(2,1)} %get-tuple-element.152), channel_id=1, source_target_pairs={{0,8},{4,12},{8,0},{12,4},{16,24},{20,28},{24,16},{28,20},{1,9},{5... | collective-permute-start | bytes 1179656 | tf_op jit(solution)/shard_map/ppermute | solution.py:60
  60.7 47.8 %collective-permute-start.13 = (bf16[128,1024]{1,0:T(8,128)(2,1)}, bf16[128,1024]{1,0:T(8,128)(2,1)}, u32[]{:S(2)}, u32[]{:S(2)}) collective-permute-start(bf16[128,1024]{1,0:T(8,128)(2,1)} %get-tuple-element.147), channel_id=1, source_target_pairs={{0,1},{1,2},{2,3},{3,0},{4,5},{5,6},{6,7},{7,4},{8,9},{9,10},{10,1... | collective-permute-start | bytes 786440 | tf_op jit(solution)/shard_map/ppermute | solution.py:54
  68.0 35.3 %collective-permute-start.21 = (bf16[128,1536]{1,0:T(8,128)(2,1)}, bf16[128,1536]{1,0:T(8,128)(2,1)}, u32[]{:S(2)}, u32[]{:S(2)}) collective-permute-start(bf16[128,1536]{1,0:T(8,128)(2,1)} %get-tuple-element.152), channel_id=1, source_target_pairs={{0,24},{4,28},{8,16},{12,20},{16,8},{20,12},{24,0},{28,4},{1,25},{... | collective-permute-start | bytes 1179656 | tf_op jit(solution)/shard_map/ppermute | solution.py:60
  103.2 11.3 %collective-permute-start.10 = (bf16[128,1024]{1,0:T(8,128)(2,1)}, bf16[128,1024]{1,0:T(8,128)(2,1)S(1)}, u32[]{:S(2)}, u32[]{:S(2)}) collective-permute-start(bf16[128,1024]{1,0:T(8,128)(2,1)} %get-tuple-element.137), channel_id=1, source_target_pairs={{0,1},{1,2},{2,3},{3,0},{4,5},{5,6},{6,7},{7,4},{8,9},{9,10},{10,1... | collective-permute-start | bytes 786440 | tf_op jit(solution)/shard_map/ppermute | solution.py:252
  103.3 18.5 %collective-permute-start.11 = (bf16[128,1024]{1,0:T(8,128)(2,1)}, bf16[128,1024]{1,0:T(8,128)(2,1)S(1)}, u32[]{:S(2)}, u32[]{:S(2)}) collective-permute-start(bf16[128,1024]{1,0:T(8,128)(2,1)} %get-tuple-element.138), channel_id=1, source_target_pairs={{0,2},{1,3},{2,0},{3,1},{4,6},{5,7},{6,4},{7,5},{8,10},{9,11},{10,... | collective-permute-start | bytes 786440 | tf_op jit(solution)/shard_map/ppermute | solution.py:252
  105.3 16.6 %collective-permute-start.12 = (bf16[128,1024]{1,0:T(8,128)(2,1)}, bf16[128,1024]{1,0:T(8,128)(2,1)S(1)}, u32[]{:S(2)}, u32[]{:S(2)}) collective-permute-start(bf16[128,1024]{1,0:T(8,128)(2,1)} %get-tuple-element.139), channel_id=1, source_target_pairs={{0,3},{1,0},{2,1},{3,2},{4,7},{5,4},{6,5},{7,6},{8,11},{9,8},{10,9... | collective-permute-start | bytes 786440 | tf_op jit(solution)/shard_map/ppermute | solution.py:252
  108.4 43.1 %collective-permute-start.22 = (bf16[512,1536]{1,0:T(8,128)(2,1)S(1)}, bf16[512,1536]{1,0:T(8,128)(2,1)S(1)}, u32[]{:S(2)}, u32[]{:S(2)}) collective-permute-start(bf16[512,1536]{1,0:T(8,128)(2,1)S(1)} %constant_dynamic-update-slice_fusion.8.refs_5_.w0_ref), channel_id=1, source_target_pairs={{0,4},{4,0},{8,12},{12,8},{16,20},{20,16},{24,28},{28,24},{1,5},{5... | collective-permute-start | bytes 4718600 | tf_op jit(solution)/shard_map/ppermute | solution.py:60
  123.3 14.2 %collective-permute-start.16 = (bf16[128,1024]{1,0:T(8,128)(2,1)S(1)}, bf16[128,1024]{1,0:T(8,128)(2,1)S(1)}, u32[]{:S(2)}, u32[]{:S(2)}) collective-permute-start(bf16[128,1024]{1,0:T(8,128)(2,1)S(1)} %multiply_convert_fusion.refs_0_), channel_id=1, source_target_pairs={{0,1},{1,2},{2,3},{3,0},{4,5},{5,6},{6,7},{7,4},{8,9},{9,10},{10,1... | collective-permute-start | bytes 786440 | tf_op jit(solution)/shard_map/ppermute | solution.py:41
  137.4 10.8 %collective-permute-start.17 = (bf16[128,1024]{1,0:T(8,128)(2,1)S(1)}, bf16[128,1024]{1,0:T(8,128)(2,1)S(1)}, u32[]{:S(2)}, u32[]{:S(2)}) collective-permute-start(bf16[128,1024]{1,0:T(8,128)(2,1)S(1)} %collective-permute-done.16.refs_1_), channel_id=1, source_target_pairs={{0,1},{1,2},{2,3},{3,0},{4,5},{5,6},{6,7},{7,4},{8,9},{9,10},{10,1... | collective-permute-start | bytes 786440 | tf_op jit(solution)/shard_map/ppermute | solution.py:41
  167.3 11.3 %collective-permute-start.23 = (bf16[128,1024]{1,0:T(8,128)(2,1)}, bf16[128,1024]{1,0:T(8,128)(2,1)S(1)}, u32[]{:S(2)}, u32[]{:S(2)}) collective-permute-start(bf16[128,1024]{1,0:T(8,128)(2,1)} %get-tuple-element.154), channel_id=1, source_target_pairs={{0,1},{1,2},{2,3},{3,0},{4,5},{5,6},{6,7},{7,4},{8,9},{9,10},{10,1... | collective-permute-start | bytes 786440 | tf_op jit(solution)/shard_map/ppermute | solution.py:252
  167.3 21.6 %collective-permute-start.24 = (bf16[128,1024]{1,0:T(8,128)(2,1)}, bf16[128,1024]{1,0:T(8,128)(2,1)S(1)}, u32[]{:S(2)}, u32[]{:S(2)}) collective-permute-start(bf16[128,1024]{1,0:T(8,128)(2,1)} %get-tuple-element.155), channel_id=1, source_target_pairs={{0,2},{1,3},{2,0},{3,1},{4,6},{5,7},{6,4},{7,5},{8,10},{9,11},{10,... | collective-permute-start | bytes 786440 | tf_op jit(solution)/shard_map/ppermute | solution.py:252
  167.8 21.1 %collective-permute-start.25 = (bf16[128,1024]{1,0:T(8,128)(2,1)}, bf16[128,1024]{1,0:T(8,128)(2,1)}, u32[]{:S(2)}, u32[]{:S(2)}) collective-permute-start(bf16[128,1024]{1,0:T(8,128)(2,1)} %get-tuple-element.156), channel_id=1, source_target_pairs={{0,3},{1,0},{2,1},{3,2},{4,7},{5,4},{6,5},{7,6},{8,11},{9,8},{10,9... | collective-permute-start | bytes 786440 | tf_op jit(solution)/shard_map/ppermute | solution.py:252
  192.3 10.5 %collective-permute-start.27 = (bf16[128,1024]{1,0:T(8,128)(2,1)S(1)}, bf16[128,1024]{1,0:T(8,128)(2,1)S(1)}, u32[]{:S(2)}, u32[]{:S(2)}) collective-permute-start(bf16[128,1024]{1,0:T(8,128)(2,1)S(1)} %fusion.11.refs_0_), channel_id=1, source_target_pairs={{0,1},{1,2},{2,3},{3,0},{4,5},{5,6},{6,7},{7,4},{8,9},{9,10},{10,1... | collective-permute-start | bytes 786440 | tf_op jit(solution)/shard_map/ppermute | solution.py:41
  205.3 12.0 %collective-permute-start.30 = (bf16[128,1536]{1,0:T(8,128)(2,1)S(1)}, bf16[128,1536]{1,0:T(8,128)(2,1)S(1)}, u32[]{:S(2)}, u32[]{:S(2)}) collective-permute-start(bf16[128,1536]{1,0:T(8,128)(2,1)S(1)} %copy-done.49), channel_id=1, source_target_pairs={{0,8},{4,12},{8,0},{12,4},{16,24},{20,28},{24,16},{28,20},{1,9},{5... | collective-permute-start | bytes 1179656 | tf_op jit(solution)/shard_map/ppermute | solution.py:60
  205.8 11.7 %collective-permute-start.31 = (bf16[128,1536]{1,0:T(8,128)(2,1)S(1)}, bf16[128,1536]{1,0:T(8,128)(2,1)S(1)}, u32[]{:S(2)}, u32[]{:S(2)}) collective-permute-start(bf16[128,1536]{1,0:T(8,128)(2,1)S(1)} %copy-done.48), channel_id=1, source_target_pairs={{0,16},{4,20},{8,24},{12,28},{16,0},{20,4},{24,8},{28,12},{1,17},{... | collective-permute-start | bytes 1179656 | tf_op jit(solution)/shard_map/ppermute | solution.py:60
  207.2 16.2 %collective-permute-start.32 = (bf16[128,1536]{1,0:T(8,128)(2,1)S(1)}, bf16[128,1536]{1,0:T(8,128)(2,1)S(1)}, u32[]{:S(2)}, u32[]{:S(2)}) collective-permute-start(bf16[128,1536]{1,0:T(8,128)(2,1)S(1)} %copy-done.47), channel_id=1, source_target_pairs={{0,24},{4,28},{8,16},{12,20},{16,8},{20,12},{24,0},{28,4},{1,25},{... | collective-permute-start | bytes 1179656 | tf_op jit(solution)/shard_map/ppermute | solution.py:60
  211.5 11.9 %collective-permute-start.29 = (bf16[128,1024]{1,0:T(8,128)(2,1)S(1)}, bf16[128,1024]{1,0:T(8,128)(2,1)}, u32[]{:S(2)}, u32[]{:S(2)}) collective-permute-start(bf16[128,1024]{1,0:T(8,128)(2,1)S(1)} %collective-permute-done.28.refs_2_), channel_id=1, source_target_pairs={{0,1},{1,2},{2,3},{3,0},{4,5},{5,6},{6,7},{7,4},{8,9},{9,10},{10,1... | collective-permute-start | bytes 786440 | tf_op jit(solution)/shard_map/ppermute | solution.py:41
  228.3 12.2 %collective-permute-start.35 = (f32[4,128]{1,0:T(4,128)}, f32[4,128]{1,0:T(4,128)S(1)}, u32[]{:S(2)}, u32[]{:S(2)}) collective-permute-start(f32[4,128]{1,0:T(4,128)} %bitcast.106), channel_id=1, source_target_pairs={{0,1},{1,2},{2,3},{3,0},{4,5},{5,6},{6,7},{7,4},{8,9},{9,10},{10,1... | collective-permute-start | bytes 6152 | tf_op jit(solution)/shard_map/ppermute | solution.py:261
  228.9 11.6 %collective-permute-start.34 = (f32[4,128]{1,0:T(4,128)}, f32[4,128]{1,0:T(4,128)S(1)}, u32[]{:S(2)}, u32[]{:S(2)}) collective-permute-start(f32[4,128]{1,0:T(4,128)} %bitcast.107), channel_id=1, source_target_pairs={{0,2},{1,3},{2,0},{3,1},{4,6},{5,7},{6,4},{7,5},{8,10},{9,11},{10,... | collective-permute-start | bytes 6152 | tf_op jit(solution)/shard_map/ppermute | solution.py:261
  259.1 37.7 %collective-permute-start.39 = (bf16[128,1024]{1,0:T(8,128)(2,1)}, bf16[128,1024]{1,0:T(8,128)(2,1)}, u32[]{:S(2)}, u32[]{:S(2)}) collective-permute-start(bf16[128,1024]{1,0:T(8,128)(2,1)} %get-tuple-element.191), channel_id=1, source_target_pairs={{0,1},{1,2},{2,3},{3,0},{4,5},{5,6},{6,7},{7,4},{8,9},{9,10},{10,1... | collective-permute-start | bytes 786440 | tf_op jit(solution)/shard_map/ppermute | solution.py:252
  259.6 39.0 %collective-permute-start.40 = (bf16[128,1024]{1,0:T(8,128)(2,1)}, bf16[128,1024]{1,0:T(8,128)(2,1)}, u32[]{:S(2)}, u32[]{:S(2)}) collective-permute-start(bf16[128,1024]{1,0:T(8,128)(2,1)} %get-tuple-element.192), channel_id=1, source_target_pairs={{0,2},{1,3},{2,0},{3,1},{4,6},{5,7},{6,4},{7,5},{8,10},{9,11},{10,... | collective-permute-start | bytes 786440 | tf_op jit(solution)/shard_map/ppermute | solution.py:252
  266.4 14.3 %collective-permute-start.46 = (bf16[128,1920]{1,0:T(8,128)(2,1)}, bf16[128,1920]{1,0:T(8,128)(2,1)S(1)}, u32[]{:S(2)}, u32[]{:S(2)}) collective-permute-start(bf16[128,1920]{1,0:T(8,128)(2,1)} %get-tuple-element.195), channel_id=1, source_target_pairs={{0,8},{4,12},{8,0},{12,4},{16,24},{20,28},{24,16},{28,20},{1,9},{5... | collective-permute-start | bytes 1474568 | tf_op jit(solution)/shard_map/ppermute | solution.py:60
  267.9 23.8 %collective-permute-start.47 = (bf16[128,1920]{1,0:T(8,128)(2,1)}, bf16[128,1920]{1,0:T(8,128)(2,1)S(1)}, u32[]{:S(2)}, u32[]{:S(2)}) collective-permute-start(bf16[128,1920]{1,0:T(8,128)(2,1)} %get-tuple-element.196), channel_id=1, source_target_pairs={{0,16},{4,20},{8,24},{12,28},{16,0},{20,4},{24,8},{28,12},{1,17},{... | collective-permute-start | bytes 1474568 | tf_op jit(solution)/shard_map/ppermute | solution.py:60
  268.6 24.3 %collective-permute-start.48 = (bf16[128,1920]{1,0:T(8,128)(2,1)}, bf16[128,1920]{1,0:T(8,128)(2,1)}, u32[]{:S(2)}, u32[]{:S(2)}) collective-permute-start(bf16[128,1920]{1,0:T(8,128)(2,1)} %get-tuple-element.197), channel_id=1, source_target_pairs={{0,24},{4,28},{8,16},{12,20},{16,8},{20,12},{24,0},{28,4},{1,25},{... | collective-permute-start | bytes 1474568 | tf_op jit(solution)/shard_map/ppermute | solution.py:60
  280.7 42.1 %collective-permute-start.38 = (bf16[128,1536]{1,0:T(8,128)(2,1)S(1)}, bf16[128,1536]{1,0:T(8,128)(2,1)}, u32[]{:S(2)}, u32[]{:S(2)}) collective-permute-start(bf16[128,1536]{1,0:T(8,128)(2,1)S(1)} %add_convert_fusion.1.refs_0_), channel_id=1, source_target_pairs={{0,3},{1,0},{2,1},{3,2},{4,7},{5,4},{6,5},{7,6},{8,11},{9,8},{10,9... | collective-permute-start | bytes 1179656 | tf_op jit(solution)/shard_map/ppermute | solution.py:54
  291.7 44.8 %collective-permute-start.37 = (bf16[128,1536]{1,0:T(8,128)(2,1)S(1)}, bf16[128,1536]{1,0:T(8,128)(2,1)}, u32[]{:S(2)}, u32[]{:S(2)}) collective-permute-start(bf16[128,1536]{1,0:T(8,128)(2,1)S(1)} %add_convert_fusion.1.refs_0_), channel_id=1, source_target_pairs={{0,2},{1,3},{2,0},{3,1},{4,6},{5,7},{6,4},{7,5},{8,10},{9,11},{10,... | collective-permute-start | bytes 1179656 | tf_op jit(solution)/shard_map/ppermute | solution.py:54
  294.6 58.4 %collective-permute-start.49 = (bf16[128,1920]{1,0:T(8,128)(2,1)S(1)}, bf16[128,1920]{1,0:T(8,128)(2,1)}, u32[]{:S(2)}, u32[]{:S(2)}) collective-permute-start(bf16[128,1920]{1,0:T(8,128)(2,1)S(1)} %add_convert_fusion.refs_0_), channel_id=1, source_target_pairs={{0,1},{1,2},{2,3},{3,0},{4,5},{5,6},{6,7},{7,4},{8,9},{9,10},{10,1... | collective-permute-start | bytes 1474568 | tf_op jit(solution)/shard_map/ppermute | solution.py:41
  296.7 25.0 %collective-permute-start.41 = (bf16[128,1024]{1,0:T(8,128)(2,1)}, bf16[128,1024]{1,0:T(8,128)(2,1)S(1)}, u32[]{:S(2)}, u32[]{:S(2)}) collective-permute-start(bf16[128,1024]{1,0:T(8,128)(2,1)} %get-tuple-element.193), channel_id=1, source_target_pairs={{0,3},{1,0},{2,1},{3,2},{4,7},{5,4},{6,5},{7,6},{8,11},{9,8},{10,9... | collective-permute-start | bytes 786440 | tf_op jit(solution)/shard_map/ppermute | solution.py:252
  298.6 37.9 %collective-permute-start.36 = (bf16[128,1536]{1,0:T(8,128)(2,1)S(1)}, bf16[128,1536]{1,0:T(8,128)(2,1)S(1)}, u32[]{:S(2)}, u32[]{:S(2)}) collective-permute-start(bf16[128,1536]{1,0:T(8,128)(2,1)S(1)} %add_convert_fusion.1.refs_0_), channel_id=1, source_target_pairs={{0,1},{1,2},{2,3},{3,0},{4,5},{5,6},{6,7},{7,4},{8,9},{9,10},{10,1... | collective-permute-start | bytes 1179656 | tf_op jit(solution)/shard_map/ppermute | solution.py:54
  321.8 16.8 %collective-permute-start.52 = (f32[104,128]{1,0:T(8,128)}, f32[104,128]{1,0:T(8,128)S(1)}, u32[]{:S(2)}, u32[]{:S(2)}) collective-permute-start(f32[104,128]{1,0:T(8,128)} %pad.27), channel_id=1, source_target_pairs={{0,3},{1,2},{2,1},{3,0},{4,7},{5,6},{6,5},{7,4},{8,11},{9,10},{10,... | collective-permute-start | bytes 159752 | tf_op jit(solution)/shard_map/ppermute | solution.py:275
  322.8 25.7 %collective-permute-start.51 = (f32[104,128]{1,0:T(8,128)}, f32[104,128]{1,0:T(8,128)}, u32[]{:S(2)}, u32[]{:S(2)}) collective-permute-start(f32[104,128]{1,0:T(8,128)} %pad.27), channel_id=1, source_target_pairs={{0,2},{1,3},{2,0},{3,1},{4,6},{5,7},{6,4},{7,5},{8,10},{9,11},{10,... | collective-permute-start | bytes 159752 | tf_op jit(solution)/shard_map/ppermute | solution.py:275
  336.5 16.5 %collective-permute-start.50 = (f32[104,128]{1,0:T(8,128)}, f32[104,128]{1,0:T(8,128)}, u32[]{:S(2)}, u32[]{:S(2)}) collective-permute-start(f32[104,128]{1,0:T(8,128)} %pad.27), channel_id=1, source_target_pairs={{0,1},{1,0},{2,3},{3,2},{4,5},{5,4},{6,7},{7,6},{8,9},{9,8},{10,11... | collective-permute-start | bytes 159752 | tf_op jit(solution)/shard_map/ppermute | solution.py:275
  336.5 18.3 %collective-permute-start.43 = (bf16[128,1024]{1,0:T(8,128)(2,1)}, bf16[128,1024]{1,0:T(8,128)(2,1)S(1)}, u32[]{:S(2)}, u32[]{:S(2)}) collective-permute-start(bf16[128,1024]{1,0:T(8,128)(2,1)} %get-tuple-element.203), channel_id=1, source_target_pairs={{0,1},{1,2},{2,3},{3,0},{4,5},{5,6},{6,7},{7,4},{8,9},{9,10},{10,1... | collective-permute-start | bytes 786440 | tf_op jit(solution)/shard_map/ppermute | solution.py:252
  338.5 28.9 %collective-permute-start.44 = (bf16[128,1024]{1,0:T(8,128)(2,1)}, bf16[128,1024]{1,0:T(8,128)(2,1)S(1)}, u32[]{:S(2)}, u32[]{:S(2)}) collective-permute-start(bf16[128,1024]{1,0:T(8,128)(2,1)} %get-tuple-element.204), channel_id=1, source_target_pairs={{0,2},{1,3},{2,0},{3,1},{4,6},{5,7},{6,4},{7,5},{8,10},{9,11},{10,... | collective-permute-start | bytes 786440 | tf_op jit(solution)/shard_map/ppermute | solution.py:252
  348.5 18.9 %collective-permute-start.45 = (bf16[128,1024]{1,0:T(8,128)(2,1)}, bf16[128,1024]{1,0:T(8,128)(2,1)S(1)}, u32[]{:S(2)}, u32[]{:S(2)}) collective-permute-start(bf16[128,1024]{1,0:T(8,128)(2,1)} %get-tuple-element.205), channel_id=1, source_target_pairs={{0,3},{1,0},{2,1},{3,2},{4,7},{5,4},{6,5},{7,6},{8,11},{9,8},{10,9... | collective-permute-start | bytes 786440 | tf_op jit(solution)/shard_map/ppermute | solution.py:252
  353.0 19.0 %collective-permute-start.53 = (bf16[128,1920]{1,0:T(8,128)(2,1)}, bf16[128,1920]{1,0:T(8,128)(2,1)}, u32[]{:S(2)}, u32[]{:S(2)}) collective-permute-start(bf16[128,1920]{1,0:T(8,128)(2,1)} %collective-permute-done.49.refs_1_), channel_id=1, source_target_pairs={{0,1},{1,2},{2,3},{3,0},{4,5},{5,6},{6,7},{7,4},{8,9},{9,10},{10,1... | collective-permute-start | bytes 1474568 | tf_op jit(solution)/shard_map/ppermute | solution.py:41
  354.7 13.0 %collective-permute-start.54 = (f32[104,128]{1,0:T(8,128)S(1)}, f32[104,128]{1,0:T(8,128)S(1)}, u32[]{:S(2)}, u32[]{:S(2)}) collective-permute-start(f32[104,128]{1,0:T(8,128)S(1)} %add_add_fusion), channel_id=1, source_target_pairs={{0,4},{4,0},{8,12},{12,8},{16,20},{20,16},{24,28},{28,24},{1,5},{5... | collective-permute-start | bytes 159752 | tf_op jit(solution)/shard_map/ppermute | solution.py:282
  372.0 10.8 %collective-permute-start.57 = (f32[104,128]{1,0:T(8,128)S(1)}, f32[104,128]{1,0:T(8,128)S(1)}, u32[]{:S(2)}, u32[]{:S(2)}) collective-permute-start(f32[104,128]{1,0:T(8,128)S(1)} %add.201), channel_id=1, source_target_pairs={{0,16},{4,20},{8,24},{12,28},{16,0},{20,4},{24,8},{28,12},{1,17},{... | collective-permute-start | bytes 159752 | tf_op jit(solution)/shard_map/ppermute | solution.py:282
  377.8 13.4 %collective-permute-start.56 = (bf16[128,1920]{1,0:T(8,128)(2,1)}, bf16[128,1920]{1,0:T(8,128)(2,1)S(1)}, u32[]{:S(2)}, u32[]{:S(2)}) collective-permute-start(bf16[128,1920]{1,0:T(8,128)(2,1)} %collective-permute-done.53.refs_2_), channel_id=1, source_target_pairs={{0,1},{1,2},{2,3},{3,0},{4,5},{5,6},{6,7},{7,4},{8,9},{9,10},{10,1... | collective-permute-start | bytes 1474568 | tf_op jit(solution)/shard_map/ppermute | solution.py:41
  (63 other events, 1265.9 us)

commit v3 on v2

--- a/solution.py
+++ b/solution.py
@@ -441,11 +441,13 @@
     return start[:, :1].astype(jnp.int32), (start == transposed(start)) & (s_row <= t_col)
 
 
-def attn_forward(x_ref, qkv_ref, attn_ref):
+def attn_forward(x_ref, qkv_ref, attn_ref, kept_ref):
     first, keep = links(x_ref[...].astype(F32))
-    low, _, _, _, _, values, probs, _ = attn_common(
+    low, cosine, sine, q_rot, keys, values, probs, _ = attn_common(
         qkv_ref[:, :128], qkv_ref[:, 128:], first, keep
     )
+    for i, value in enumerate((cosine, sine, q_rot, keys, values, *probs)):
+        kept_ref[:, i * 128 : (i + 1) * 128] = value
     out = [quick(p, values, NN) for p in probs]
     attn_ref[...] = jnp.where(low, out[0], out[1]).astype(BF)
 
@@ -471,12 +473,12 @@
     d_attn_ref[...] = d_mix[:, inner:]
 
 
-def branch_back_attn(x_ref, qkv_ref, d_attn_ref, d_qkv_ref):
-    start = x_ref[...].astype(F32)
-    rows = start.shape[0]
-    first, keep = links(start)
-    q, kv = qkv_ref[:, :128], qkv_ref[:, 128:]
-    low, cosine, sine, q_rot, keys, values, probs, picks = attn_common(q, kv, first, keep)
+def branch_back_attn(kept_ref, d_attn_ref, d_qkv_ref):
+    rows = kept_ref.shape[0]
+    kept = [kept_ref[:, i * 128 : (i + 1) * 128] for i in range(7)]
+    cosine, sine, q_rot, keys, values, *probs = kept
+    low = lax.broadcasted_iota(jnp.int32, (rows, 128), 1) < HD
+    picks = [low, ~low]
     d_attn = d_attn_ref[...]
     d_q = []
     d_k = jnp.zeros((rows, 128), F32)
@@ -718,10 +720,10 @@
         parts_a, tok_held = tie((parts_a, first[-2]))
         own_a = jnp.concatenate(parts_a, 0)
         halves_a = [own_a, flip(own_a, 1)]
-        tok_blocks, first = first, jnp.concatenate(first, 0)
+        tok_blocks = first
     else:
         tok_held = first[-2]
-        tok_blocks, first = first, jnp.concatenate(first, 0)
+        tok_blocks = first
         full_a = lax.all_gather(sh_a, "fsdp", axis=0, tiled=True)
         halves_a = [full_a[: width // 2], full_a[width // 2 :]]
 
@@ -759,10 +761,9 @@
     gm = gm.reshape(1, my_inner)
     g_in_row = g_in.reshape(1, width)
     count = n * rows
-    normed, proj, y, gated, square = pl.pallas_call(
+    normed, proj, y, gated, square, first = pl.pallas_call(
         functools.partial(branch_forward, sizes, n),
         grid=(n,),
-        scratch_shapes=[pltpu.VMEM((rows, first.shape[1]), BF)],
         in_specs=[fixed_spec(a) for a in tok_blocks]
         + [pl.BlockSpec((a.shape[0], span), lambda i: (0, 0)) for a in halves_a]
         + [fixed_spec(a) for a in (g_in_row, conv_p, head_p)],
@@ -772,6 +773,7 @@
             row_spec(rows, my_inner),
             row_spec(rows, my_inner),
             row_spec(1, 1, rows),
+            row_spec(rows, width + 128),
         ],
         out_shape=[
             out_of((count, width), BF),
@@ -779,17 +781,18 @@
             out_of((count, my_inner), F32),
             out_of((count, my_inner), F32),
             out_of((n, 1, rows), F32),
+            out_of((count, width + 128), BF),
         ],
     )(*tok_blocks, *halves_a, g_in_row, conv_p, head_p)
     square = peer_scalar_sum(square.reshape(n, rows))
     start_spec = pl.BlockSpec((rows, 128), lambda i: (i, width // 128))
     qkv_spec = pl.BlockSpec((rows, 256), lambda i: (i, o // 256))
-    attn = pl.pallas_call(
+    attn, kept = pl.pallas_call(
         attn_forward,
         grid=(n,),
         in_specs=[start_spec, qkv_spec],
-        out_specs=row_spec(rows, qc),
-        out_shape=out_of((count, qc), BF),
+        out_specs=[row_spec(rows, qc), row_spec(rows, 7 * 128)],
+        out_shape=[out_of((count, qc), BF), out_of((count, 7 * 128), F32)],
     )(first, proj)
     scale_rows = lax.rsqrt(square / inner + norm_eps).reshape(n, 1, rows)
     shapes = rows_out(n, rows, width)
@@ -827,12 +830,13 @@
     d_mixed_n, grad_g_ff = rms_back(mixed, f_scale, g_ff, add_up(d_hidden))
     d_mixed = cotangent.astype(F32) + d_mixed_n
     dm_blocks = peer_blocks(d_mixed.astype(BF))
-    dm_blocks, grad_c = tie((dm_blocks, grad_c))
     if cube:
         grad_c = add_up(grad_c).astype(BF)
     else:
         grad_c = lax.psum_scatter(grad_c, "fsdp", scatter_dimension=0, tiled=True)
-    c_blocks = peer_direct(grad_c)
+    c_blocks = [grad_c]
+    for _ in range(1, n):
+        c_blocks.append(next_peer(c_blocks[-1]))
     out_parts = partial_rows(n, act, halves_b, 2 * my_hidden, 3 * my_hidden)
     out_parts = peer_send(out_parts)
     d_scaled, d_attn, m_inner, grad_gm, dm_all = pl.pallas_call(
@@ -848,13 +852,13 @@
     d_qkv = pl.pallas_call(
         branch_back_attn,
         grid=(n,),
-        in_specs=[start_spec, qkv_spec, row_spec(rows, qc)],
+        in_specs=[row_spec(rows, 7 * 128), row_spec(rows, qc)],
         out_specs=row_spec(rows, 256),
         out_shape=out_of((count, 256), BF),
         cost_estimate=pl.CostEstimate(
             flops=30 * count * rows * 128, bytes_accessed=count * 5000, transcendentals=count * 512
         ),
-    )(first, proj, d_attn)
+    )(kept, d_attn)
     m_inner = peer_scalar_sum(m_inner.reshape(n, rows)).reshape(n, 1, rows)
     m_inner, d_qkv = tie((m_inner, d_qkv))
     d_proj, g_conv, g_head, g_skip = pl.pallas_call(
@@ -936,11 +940,6 @@
             grads(a_pairs, 0, width), "fsdp", scatter_dimension=0, tiled=True
         )
     output = (mixed + add_up(out_parts)).astype(BF)
-    d_tok_n, _ = rms_back(tok32, rms_scale(tok32), g_in, add_up(d_normed))
-    grad_tokens = (d_mixed + d_tok_n).astype(BF)
-    if cube:
-        output, grad_tokens = reorder([output, grad_tokens], back=True)
-
     a_blocks = [grad_a, next_peer(grad_a)]
     while len(a_blocks) < n:
         a_blocks[-1], flat = tie((a_blocks[-1], flat))
@@ -948,15 +947,18 @@
         if len(a_blocks) == 3:
             flat = sum_fsdp(sum_level(flat), 1, 4)
     flat = sum_fsdp(flat, 4)
+    a_blocks[2], d_normed = tie((a_blocks[2], d_normed))
+    d_tok_n, _ = rms_back(tok32, rms_scale(tok32), g_in, add_up(d_normed))
+    grad_tokens = (d_mixed + d_tok_n).astype(BF)
+    if cube:
+        output, grad_tokens = reorder([output, grad_tokens], True)
+
 
     def kv_of(owner):
         return owner * my_q // per_kv
 
     grad_gate, grad_up, grad_down = lay(
-        c_blocks,
-        [("slice", i * my_hidden, my_hidden, i, 0) for i in range(3)],
-        [hidden] * 3,
-        kv_of,
+        c_blocks, [("slice", i * my_hidden, my_hidden, i, 0) for i in range(3)], [hidden] * 3, kv_of
     )
     grad_in, grad_q, grad_k, grad_v, grad_out, grad_o = lay(
         a_blocks,

time: 399 us -> 411 us (1.030)
  the two profiles are of different devices: /device:TPU:0 before, /device:TPU:8 now
where the time goes in v3:
time: 411 us; the launch traced here: 410 us
  waiting for transfers between devices  211 us (51%)
  Pallas kernels  86.4 us (21%)
  starting transfers between devices  67.8 us (16%)
  local copies, waits for them, and re-layouts  27.1 us (7%)
  other arithmetic  15.6 us (4%)
    ppermute x12, waiting for transfers between devices, peer_send(): lax.ppermute(blocks[k], 'dp', [(i, (i - k) % n) for i in range(n)])  87.3 us
    ppermute x15, waiting for transfers between devices, next_peer(): return lax.ppermute(x, 'dp', [(i, (i + 1) % n) for i in range(n)])  58 us
    ppermute x16, waiting for transfers between devices, flip(): return lax.ppermute(x, 'fsdp', [(i, i ^ bits) for i in range(size)])  46.7 us
    pallas_call x4, Pallas kernels, grads(): pl.pallas_call(functools.partial(grad_kernel, len(pairs), add is not None...  17.6 us
    ppermute x15, starting transfers between devices, next_peer(): return lax.ppermute(x, 'dp', [(i, (i + 1) % n) for i in range(n)])  17 us
    ppermute x16, starting transfers between devices, flip(): return lax.ppermute(x, 'fsdp', [(i, i ^ bits) for i in range(size)])  15.3 us
    ppermute x12, starting transfers between devices, peer_send(): lax.ppermute(blocks[k], 'dp', [(i, (i - k) % n) for i in range(n)])  14.8 us
    ppermute x3, waiting for transfers between devices, sum_dp(): lax.ppermute(v, 'dp', [(i, i ^ m) for i in range(n)])  13.9 us
  transfers between devices with their start and end apart: 58, of which 33 were waited for; matrix products, arithmetic and copies ran while one was open for 7% of the time, Pallas kernels for 13%

profile of v3, /device:TPU:8, one launch (start us, length us, event | category | flops | bytes accessed | tf_op | source)
XLA Modules:
  0.0 409.9 jit_solution(4906520420634352949)
XLA Ops:
  6.6 3.1 shard_map.358
  9.8 2.5 collective-permute-start.5
  15.4 9.7 %collective-permute-done.5 = bf16[128,1920]{1,0:T(8,128)(2,1)S(1)} collective-permute-done((bf16[128,1920]{1,0:T(8,128)(2,1)}, bf16[128,1920]{1,0:T(8,128)(2,1)S(1)}, u32[]{:S(2)}, u32[]{:S(2)}) %collective-permute-start.5) | collective-permute-done | bytes 491552 | tf_op jit(solution)/shard_map/ppermute | solution.py:60
  25.1 9.1 %collective-permute-done.4 = bf16[128,1920]{1,0:T(8,128)(2,1)S(1)} collective-permute-done((bf16[128,1920]{1,0:T(8,128)(2,1)}, bf16[128,1920]{1,0:T(8,128)(2,1)S(1)}, u32[]{:S(2)}, u32[]{:S(2)}) %collective-permute-start.4) | collective-permute-done | bytes 491552 | tf_op jit(solution)/shard_map/ppermute | solution.py:60
  36.2 2.6 collective-permute-start.14
  47.1 15.0 %collective-permute-done.2.refs_3_ = bf16[128,1152]{1,0:T(8,128)(2,1)S(1)} collective-permute-done((bf16[128,1152]{1,0:T(8,128)(2,1)}, bf16[128,1152]{1,0:T(8,128)(2,1)S(1)}, u32[]{:S(2)}, u32[]{:S(2)}) %collective-permute-start.2) | collective-permute-done | bytes 294944 | tf_op jit(solution)/shard_map/ppermute | solution.py:41
  66.1 9.5 %shard_map.359 = (bf16[512,1024]{1,0:T(8,128)(2,1)}, f32[512,1408]{1,0:T(8,128)}, f32[512,384]{1,0:T(8,128)}, f32[512,384]{1,0:T(8,128)}, f32[4,1,128]{2,1,0:T(1,128)}, /*index=5*/bf16[512,1152]{1,0:T(8,128)(2,1)}) custom-call(bf16[128,1152]{1,0:T(8,128)(2,1)} %copy-done.9, bf16[128,1152]{1,0:T(8,128)(2,1)} %copy-done.18, ...), custom_call_target="tpu_custom_call" | custom-call | tf_op jit(solution)/shard_map/pallas_call | solution.py:764
  76.7 6.0 %shard_map.360 = (bf16[512,128]{1,0:T(8,128)(2,1)}, f32[512,896]{1,0:T(8,128)}) custom-call(bf16[512,1152]{1,0:T(8,128)(2,1)} %get-tuple-element.135.x_ref.refs_0_, f32[512,1408]{1,0:T(8,128)} %get-tuple-element.136.qkv_ref.refs_1_), custom_call_target="tpu_custom_call" | custom-call | tf_op jit(solution)/shard_map/pallas_call | solution.py:790
  92.7 4.4 %shard_map.361 = (bf16[512,512]{1,0:T(8,128)(2,1)}, f32[128,1024]{1,0:T(8,128)}, bf16[128,1024]{1,0:T(8,128)(2,1)}, bf16[128,1024]{1,0:T(8,128)(2,1)}, bf16[128,1024]{1,0:T(8,128)(2,1)}) custom-call(f32[512,384]{1,0:T(8,128)} %get-tuple-element.133.gated_ref.refs_6_.refs_3_, f32[4,1,128]{2,1,0:T(1,128)} %add_rsqrt_fusion.scale_ref.refs_7_.refs_5_, ...), custom_call_target="tpu_custom_call" | custom-call | tf_op jit(solution)/shard_map/pallas_call | solution.py:799
  99.2 2.7 collective-permute-start.11
  103.1 12.8 %collective-permute-done.10 = bf16[128,1024]{1,0:T(8,128)(2,1)S(1)} collective-permute-done((bf16[128,1024]{1,0:T(8,128)(2,1)}, bf16[128,1024]{1,0:T(8,128)(2,1)S(1)}, u32[]{:S(2)}, u32[]{:S(2)}) %collective-permute-start.10) | collective-permute-done | bytes 262176 | tf_op jit(solution)/shard_map/ppermute | solution.py:252
  115.9 2.8 collective-permute-done.11
  118.8 5.4 %collective-permute-done.12 = bf16[128,1024]{1,0:T(8,128)(2,1)S(1)} collective-permute-done((bf16[128,1024]{1,0:T(8,128)(2,1)}, bf16[128,1024]{1,0:T(8,128)(2,1)S(1)}, u32[]{:S(2)}, u32[]{:S(2)}) %collective-permute-start.12) | collective-permute-done | bytes 262176 | tf_op jit(solution)/shard_map/ppermute | solution.py:252
  124.7 7.4 %collective-permute-done.16.refs_1_ = bf16[128,1024]{1,0:T(8,128)(2,1)S(1)} collective-permute-done((bf16[128,1024]{1,0:T(8,128)(2,1)S(1)}, bf16[128,1024]{1,0:T(8,128)(2,1)S(1)}, u32[]{:S(2)}, u32[]{:S(2)}) %collective-permute-start.16) | collective-permute-done | bytes 262176 | tf_op jit(solution)/shard_map/ppermute | solution.py:41
  133.4 5.3 %collective-permute-done.17.refs_2_ = bf16[128,1024]{1,0:T(8,128)(2,1)S(1)} collective-permute-done((bf16[128,1024]{1,0:T(8,128)(2,1)S(1)}, bf16[128,1024]{1,0:T(8,128)(2,1)S(1)}, u32[]{:S(2)}, u32[]{:S(2)}) %collective-permute-start.17) | collective-permute-done | bytes 262176 | tf_op jit(solution)/shard_map/ppermute | solution.py:41
  145.2 6.9 %shard_map.362 = (bf16[512,512]{1,0:T(8,128)(2,1)}, bf16[512,1024]{1,0:T(8,128)(2,1)}, bf16[512,1024]{1,0:T(8,128)(2,1)}, f32[128,1024]{1,0:T(8,128)}, bf16[128,...) custom-call(bf16[128,1024]{1,0:T(8,128)(2,1)} %copy-done.10, bf16[128,1024]{1,0:T(8,128)(2,1)} %copy-done.26, ...), custom_call_target="tpu_custom_call" | custom-call | tf_op jit(solution)/shard_map/pallas_call | solution.py:816
  152.0 3.9 shard_map.363
  156.5 4.9 %collective-permute-start.24 = (bf16[128,1024]{1,0:T(8,128)(2,1)}, bf16[128,1024]{1,0:T(8,128)(2,1)S(1)}, u32[]{:S(2)}, u32[]{:S(2)}) collective-permute-start(bf16[128,1024]{1,0:T(8,128)(2,1)} %get-tuple-element.157), channel_id=1, source_target_pairs={{0,2},{1,3},{2,0},{3,1},{4,6},{5,7},{6,4},{7,5},{8,10},{9,11},{10,... | collective-permute-start | bytes 786440 | tf_op jit(solution)/shard_map/ppermute | solution.py:252
  162.6 4.3 %shard_map.364 = (bf16[128,1536]{1,0:T(8,128)(2,1)}, bf16[128,1536]{1,0:T(8,128)(2,1)}, bf16[128,1536]{1,0:T(8,128)(2,1)}, bf16[128,1536]{1,0:T(8,128)(2,1)}) custom-call(bf16[512,1024]{1,0:T(8,128)(2,1)} %get-tuple-element.159.refs_0_, bf16[512,1024]{1,0:T(8,128)(2,1)} %copy-done.1, bf16[512,1024]{1,0:T(8,128)(2,1)} %get-tuple-element.160.refs_2_, ...), custom_call_target="tpu_custom_call" | custom-call | flops 805306368 | bytes 4194304 | tf_op jit(solution)/shard_map/pallas_call | solution.py:116
  166.9 13.1 %collective-permute-done.24 = bf16[128,1024]{1,0:T(8,128)(2,1)S(1)} collective-permute-done((bf16[128,1024]{1,0:T(8,128)(2,1)}, bf16[128,1024]{1,0:T(8,128)(2,1)S(1)}, u32[]{:S(2)}, u32[]{:S(2)}) %collective-permute-start.24) | collective-permute-done | bytes 262176 | tf_op jit(solution)/shard_map/ppermute | solution.py:252
  179.9 4.4 %collective-permute-done.25 = bf16[128,1024]{1,0:T(8,128)(2,1)S(1)} collective-permute-done((bf16[128,1024]{1,0:T(8,128)(2,1)}, bf16[128,1024]{1,0:T(8,128)(2,1)S(1)}, u32[]{:S(2)}, u32[]{:S(2)}) %collective-permute-start.25) | collective-permute-done | bytes 262176 | tf_op jit(solution)/shard_map/ppermute | solution.py:252
  187.6 7.8 %collective-permute-done.27.refs_1_ = bf16[128,1024]{1,0:T(8,128)(2,1)S(1)} collective-permute-done((bf16[128,1024]{1,0:T(8,128)(2,1)S(1)}, bf16[128,1024]{1,0:T(8,128)(2,1)S(1)}, u32[]{:S(2)}, u32[]{:S(2)}) %collective-permute-start.27) | collective-permute-done | bytes 262176 | tf_op jit(solution)/shard_map/ppermute | solution.py:41
  195.7 6.7 %collective-permute-done.28.refs_2_ = bf16[128,1024]{1,0:T(8,128)(2,1)S(1)} collective-permute-done((bf16[128,1024]{1,0:T(8,128)(2,1)S(1)}, bf16[128,1024]{1,0:T(8,128)(2,1)S(1)}, u32[]{:S(2)}, u32[]{:S(2)}) %collective-permute-start.28) | collective-permute-done | bytes 262176 | tf_op jit(solution)/shard_map/ppermute | solution.py:41
  202.9 5.8 %collective-permute-done.29.refs_3_ = bf16[128,1024]{1,0:T(8,128)(2,1)S(1)} collective-permute-done((bf16[128,1024]{1,0:T(8,128)(2,1)S(1)}, bf16[128,1024]{1,0:T(8,128)(2,1)S(1)}, u32[]{:S(2)}, u32[]{:S(2)}) %collective-permute-start.29) | collective-permute-done | bytes 262176 | tf_op jit(solution)/shard_map/ppermute | solution.py:41
  209.5 4.7 %shard_map.365 = (f32[512,384]{1,0:T(8,128)}, f32[512,128]{1,0:T(8,128)}, f32[4,1,128]{2,1,0:T(1,128)}, f32[1,384]{1,0:T(1,128)}, bf16[512,1024]{1,0:T(8,128)(2,1)}) custom-call(bf16[128,1024]{1,0:T(8,128)(2,1)} %copy-done.11, bf16[128,1024]{1,0:T(8,128)(2,1)} %copy-done.30, bf16[128,1024]{1,0:T(8,128)(2,1)} %copy-done.31, bf16[128,1024]{1,0:T(8,128)(2,1)} %copy-done.32, ...), custom_call_target="tpu_custom_call" | custom-call | tf_op jit(solution)/shard_map/pallas_call | solution.py:842
  214.8 4.9 %collective-permute-start.31 = (f32[4,128]{1,0:T(4,128)}, f32[4,128]{1,0:T(4,128)S(1)}, u32[]{:S(2)}, u32[]{:S(2)}) collective-permute-start(f32[4,128]{1,0:T(4,128)} %bitcast.107), channel_id=1, source_target_pairs={{0,2},{1,3},{2,0},{3,1},{4,6},{5,7},{6,4},{7,5},{8,10},{9,11},{10,... | collective-permute-start | bytes 6152 | tf_op jit(solution)/shard_map/ppermute | solution.py:261
  219.7 5.5 %shard_map.366.refs_7_ = bf16[512,256]{1,0:T(8,128)(2,1)} custom-call(f32[512,896]{1,0:T(8,128)} %get-tuple-element.172.kept_ref, f32[512,128]{1,0:T(8,128)} %get-tuple-element.173.d_attn_ref), custom_call_target="tpu_custom_call" | custom-call | flops 251658240 | bytes 2560000 | tf_op jit(solution)/shard_map/pallas_call | solution.py:852
  225.9 8.8 %shard_map.367 = (bf16[512,1408]{1,0:T(8,128)(2,1)}, f32[8,640]{1,0:T(8,128)}, f32[8,128]{1,0:T(8,128)}, f32[1,384]{1,0:T(1,128)}) custom-call(bf16[512,1152]{1,0:T(8,128)(2,1)} %get-tuple-element.135.x_ref.refs_0_, f32[512,1408]{1,0:T(8,128)} %get-tuple-element.136.qkv_ref.refs_1_, f32[512,384]{1,0:T(8,128)} %get-tuple-element.147.refs_2_, ...), custom_call_target="tpu_custom_call" | custom-call | tf_op jit(solution)/shard_map/pallas_call | solution.py:864
  234.7 4.5 %shard_map.370 = bf16[512,1920]{1,0:T(8,128)(2,1)} custom-call(bf16[512,1024]{1,0:T(8,128)(2,1)} %get-tuple-element.177.refs_0_, bf16[512,1024]{1,0:T(8,128)(2,1)} %get-tuple-element.179.refs_1_, bf16[512,512]{1,0:T(8,128)(2,1)} %get-tuple-element.178.refs_2_, bf16[512,1408]{1,0:T(8,128)(2,1)} %get-tuple-element.180.left_ref.refs_3_), custom_call_target="tpu_custom_call" | custom-call | flops 1006632960 | bytes 4980736 | tf_op jit(solution)/shard_map/pallas_call | solution.py:116
  243.0 8.5 %collective-permute-done.33 = bf16[128,1536]{1,0:T(8,128)(2,1)S(1)} collective-permute-done((bf16[128,1536]{1,0:T(8,128)(2,1)}, bf16[128,1536]{1,0:T(8,128)(2,1)S(1)}, u32[]{:S(2)}, u32[]{:S(2)}) %collective-permute-start.33) | collective-permute-done | bytes 393248 | tf_op jit(solution)/shard_map/ppermute | solution.py:60
  251.8 7.9 %collective-permute-done.35 = bf16[128,1536]{1,0:T(8,128)(2,1)S(1)} collective-permute-done((bf16[128,1536]{1,0:T(8,128)(2,1)S(1)}, bf16[128,1536]{1,0:T(8,128)(2,1)S(1)}, u32[]{:S(2)}, u32[]{:S(2)}) %collective-permute-start.35) | collective-permute-done | bytes 393248 | tf_op jit(solution)/shard_map/ppermute | solution.py:60
  262.7 7.9 %collective-permute-done.36.refs_1_ = bf16[128,1536]{1,0:T(8,128)(2,1)} collective-permute-done((bf16[128,1536]{1,0:T(8,128)(2,1)S(1)}, bf16[128,1536]{1,0:T(8,128)(2,1)}, u32[]{:S(2)}, u32[]{:S(2)}) %collective-permute-start.36) | collective-permute-done | bytes 393248 | tf_op jit(solution)/shard_map/ppermute | solution.py:41
  273.6 4.9 %shard_map.371 = (bf16[128,1920]{1,0:T(8,128)(2,1)}, bf16[128,1920]{1,0:T(8,128)(2,1)}, bf16[128,1920]{1,0:T(8,128)(2,1)}, bf16[128,1920]{1,0:T(8,128)(2,1)}) custom-call(bf16[512,1024]{1,0:T(8,128)(2,1)} %get-tuple-element.177.refs_0_, bf16[512,1024]{1,0:T(8,128)(2,1)} %get-tuple-element.179.refs_1_, bf16[512,512]{1,0:T(8,128)(2,1)} %get-tuple-element.178.refs_2_, ...), custom_call_target="tpu_custom_call" | custom-call | flops 1006632960 | bytes 4980736 | tf_op jit(solution)/shard_map/pallas_call | solution.py:116
  284.1 5.8 %shard_map.368 = (f32[1,1024]{1,0:T(1,128)}, f32[128,1024]{1,0:T(8,128)}, bf16[128,1024]{1,0:T(8,128)(2,1)}, bf16[128,1024]{1,0:T(8,128)(2,1)}, bf16[128,1024]{1,0:T(8,128)(2,1)}) custom-call(bf16[512,1408]{1,0:T(8,128)(2,1)} %get-tuple-element.180.left_ref.refs_3_, bf16[512,1152]{1,0:T(8,128)(2,1)} %get-tuple-element.135.x_ref.refs_0_, ...), custom_call_target="tpu_custom_call" | custom-call | tf_op jit(solution)/shard_map/pallas_call | solution.py:896
  292.8 8.7 %collective-permute-done.44 = bf16[128,1920]{1,0:T(8,128)(2,1)S(1)} collective-permute-done((bf16[128,1920]{1,0:T(8,128)(2,1)}, bf16[128,1920]{1,0:T(8,128)(2,1)S(1)}, u32[]{:S(2)}, u32[]{:S(2)}) %collective-permute-start.44) | collective-permute-done | bytes 491552 | tf_op jit(solution)/shard_map/ppermute | solution.py:60
  303.5 3.7 collective-permute-start.38
  309.9 2.7 collective-permute-start.47
  312.6 3.7 shard_map.369
  316.4 13.9 %collective-permute-done.49 = f32[104,128]{1,0:T(8,128)S(1)} collective-permute-done((f32[104,128]{1,0:T(8,128)S(1)}, f32[104,128]{1,0:T(8,128)S(1)}, u32[]{:S(2)}, u32[]{:S(2)}) %collective-permute-start.49) | collective-permute-done | bytes 53280 | tf_op jit(solution)/shard_map/ppermute | solution.py:275
  331.6 2.4 collective-permute-start.41
  334.9 11.8 %collective-permute-done.39 = bf16[128,1024]{1,0:T(8,128)(2,1)S(1)} collective-permute-done((bf16[128,1024]{1,0:T(8,128)(2,1)}, bf16[128,1024]{1,0:T(8,128)(2,1)S(1)}, u32[]{:S(2)}, u32[]{:S(2)}) %collective-permute-start.39) | collective-permute-done | bytes 262176 | tf_op jit(solution)/shard_map/ppermute | solution.py:252
  346.6 7.5 %collective-permute-done.40 = bf16[128,1024]{1,0:T(8,128)(2,1)S(1)} collective-permute-done((bf16[128,1024]{1,0:T(8,128)(2,1)}, bf16[128,1024]{1,0:T(8,128)(2,1)S(1)}, u32[]{:S(2)}, u32[]{:S(2)}) %collective-permute-start.40) | collective-permute-done | bytes 262176 | tf_op jit(solution)/shard_map/ppermute | solution.py:252
  354.2 7.8 %collective-permute-done.41 = bf16[128,1024]{1,0:T(8,128)(2,1)S(1)} collective-permute-done((bf16[128,1024]{1,0:T(8,128)(2,1)}, bf16[128,1024]{1,0:T(8,128)(2,1)S(1)}, u32[]{:S(2)}, u32[]{:S(2)}) %collective-permute-start.41) | collective-permute-done | bytes 262176 | tf_op jit(solution)/shard_map/ppermute | solution.py:252
  367.8 3.2 shard_map.374
  373.8 12.2 %collective-permute-done.54 = bf16[128,1024]{1,0:T(8,128)(2,1)S(1)} collective-permute-done((bf16[128,1024]{1,0:T(8,128)(2,1)}, bf16[128,1024]{1,0:T(8,128)(2,1)S(1)}, u32[]{:S(2)}, u32[]{:S(2)}) %collective-permute-start.54) | collective-permute-done | bytes 262176 | tf_op jit(solution)/shard_map/ppermute | solution.py:252
  386.0 9.5 %collective-permute-done.55 = bf16[128,1024]{1,0:T(8,128)(2,1)S(1)} collective-permute-done((bf16[128,1024]{1,0:T(8,128)(2,1)}, bf16[128,1024]{1,0:T(8,128)(2,1)S(1)}, u32[]{:S(2)}, u32[]{:S(2)}) %collective-permute-start.55) | collective-permute-done | bytes 262176 | tf_op jit(solution)/shard_map/ppermute | solution.py:252
  403.9 3.3 shard_map.373
  407.2 2.7 copy.61
  (308 shorter events, 95.8 us)
Async XLA Ops:
  5.0 8.8 %collective-permute-start = (bf16[128,1152]{1,0:T(8,128)(2,1)S(1)}, bf16[128,1152]{1,0:T(8,128)(2,1)S(1)}, u32[]{:S(2)}, u32[]{:S(2)}) collective-permute-start(bf16[128,1152]{1,0:T(8,128)(2,1)S(1)} %pad_maximum_fusion.refs_0_), channel_id=1, source_target_pairs={{0,1},{1,2},{2,3},{3,0},{4,5},{5,6},{6,7},{7,4},{8,9},{9,10},{10,1... | collective-permute-start | bytes 884744 | tf_op jit(solution)/shard_map/ppermute | solution.py:41
  9.8 15.3 %collective-permute-start.5 = (bf16[128,1920]{1,0:T(8,128)(2,1)}, bf16[128,1920]{1,0:T(8,128)(2,1)S(1)}, u32[]{:S(2)}, u32[]{:S(2)}) collective-permute-start(bf16[128,1920]{1,0:T(8,128)(2,1)} %get-tuple-element.128), channel_id=1, source_target_pairs={{0,24},{4,28},{8,16},{12,20},{16,8},{20,12},{24,0},{28,4},{1,25},{... | collective-permute-start | bytes 1474568 | tf_op jit(solution)/shard_map/ppermute | solution.py:60
  12.3 21.9 %collective-permute-start.4 = (bf16[128,1920]{1,0:T(8,128)(2,1)}, bf16[128,1920]{1,0:T(8,128)(2,1)S(1)}, u32[]{:S(2)}, u32[]{:S(2)}) collective-permute-start(bf16[128,1920]{1,0:T(8,128)(2,1)} %get-tuple-element.128), channel_id=1, source_target_pairs={{0,16},{4,20},{8,24},{12,28},{16,0},{20,4},{24,8},{28,12},{1,17},{... | collective-permute-start | bytes 1474568 | tf_op jit(solution)/shard_map/ppermute | solution.py:60
  12.9 21.5 %collective-permute-start.3 = (bf16[128,1920]{1,0:T(8,128)(2,1)}, bf16[128,1920]{1,0:T(8,128)(2,1)S(1)}, u32[]{:S(2)}, u32[]{:S(2)}) collective-permute-start(bf16[128,1920]{1,0:T(8,128)(2,1)} %get-tuple-element.128), channel_id=1, source_target_pairs={{0,8},{4,12},{8,0},{12,4},{16,24},{20,28},{24,16},{28,20},{1,9},{5... | collective-permute-start | bytes 1474568 | tf_op jit(solution)/shard_map/ppermute | solution.py:60
  13.8 20.5 %collective-permute-start.1 = (bf16[128,1152]{1,0:T(8,128)(2,1)S(1)}, bf16[128,1152]{1,0:T(8,128)(2,1)}, u32[]{:S(2)}, u32[]{:S(2)}) collective-permute-start(bf16[128,1152]{1,0:T(8,128)(2,1)S(1)} %collective-permute-done.refs_1_), channel_id=1, source_target_pairs={{0,1},{1,2},{2,3},{3,0},{4,5},{5,6},{6,7},{7,4},{8,9},{9,10},{10,1... | collective-permute-start | bytes 884744 | tf_op jit(solution)/shard_map/ppermute | solution.py:41
  35.6 28.8 %collective-permute-start.6 = (bf16[512,1920]{1,0:T(8,128)(2,1)S(1)}, bf16[512,1920]{1,0:T(8,128)(2,1)}, u32[]{:S(2)}, u32[]{:S(2)}) collective-permute-start(bf16[512,1920]{1,0:T(8,128)(2,1)S(1)} %constant_dynamic-update-slice_fusion.refs_4_.w0_ref), channel_id=1, source_target_pairs={{0,4},{4,0},{8,12},{12,8},{16,20},{20,16},{24,28},{28,24},{1,5},{5... | collective-permute-start | bytes 5898248 | tf_op jit(solution)/shard_map/ppermute | solution.py:60
  35.7 61.5 %collective-permute-start.15 = (bf16[128,1024]{1,0:T(8,128)(2,1)}, bf16[128,1024]{1,0:T(8,128)(2,1)}, u32[]{:S(2)}, u32[]{:S(2)}) collective-permute-start(bf16[128,1024]{1,0:T(8,128)(2,1)} %get-tuple-element.149), channel_id=1, source_target_pairs={{0,3},{1,0},{2,1},{3,2},{4,7},{5,4},{6,5},{7,6},{8,11},{9,8},{10,9... | collective-permute-start | bytes 786440 | tf_op jit(solution)/shard_map/ppermute | solution.py:54
  36.2 66.9 %collective-permute-start.14 = (bf16[128,1024]{1,0:T(8,128)(2,1)}, bf16[128,1024]{1,0:T(8,128)(2,1)}, u32[]{:S(2)}, u32[]{:S(2)}) collective-permute-start(bf16[128,1024]{1,0:T(8,128)(2,1)} %get-tuple-element.149), channel_id=1, source_target_pairs={{0,2},{1,3},{2,0},{3,1},{4,6},{5,7},{6,4},{7,5},{8,10},{9,11},{10,... | collective-permute-start | bytes 786440 | tf_op jit(solution)/shard_map/ppermute | solution.py:54
  41.3 34.3 %collective-permute-start.19 = (bf16[128,1536]{1,0:T(8,128)(2,1)}, bf16[128,1536]{1,0:T(8,128)(2,1)}, u32[]{:S(2)}, u32[]{:S(2)}) collective-permute-start(bf16[128,1536]{1,0:T(8,128)(2,1)} %get-tuple-element.154), channel_id=1, source_target_pairs={{0,8},{4,12},{8,0},{12,4},{16,24},{20,28},{24,16},{28,20},{1,9},{5... | collective-permute-start | bytes 1179656 | tf_op jit(solution)/shard_map/ppermute | solution.py:60
  44.2 17.8 %collective-permute-start.2 = (bf16[128,1152]{1,0:T(8,128)(2,1)}, bf16[128,1152]{1,0:T(8,128)(2,1)S(1)}, u32[]{:S(2)}, u32[]{:S(2)}) collective-permute-start(bf16[128,1152]{1,0:T(8,128)(2,1)} %collective-permute-done.1.refs_2_), channel_id=1, source_target_pairs={{0,1},{1,2},{2,3},{3,0},{4,5},{5,6},{6,7},{7,4},{8,9},{9,10},{10,1... | collective-permute-start | bytes 884744 | tf_op jit(solution)/shard_map/ppermute | solution.py:41
  62.0 41.1 %collective-permute-start.13 = (bf16[128,1024]{1,0:T(8,128)(2,1)}, bf16[128,1024]{1,0:T(8,128)(2,1)}, u32[]{:S(2)}, u32[]{:S(2)}) collective-permute-start(bf16[128,1024]{1,0:T(8,128)(2,1)} %get-tuple-element.149), channel_id=1, source_target_pairs={{0,1},{1,2},{2,3},{3,0},{4,5},{5,6},{6,7},{7,4},{8,9},{9,10},{10,1... | collective-permute-start | bytes 786440 | tf_op jit(solution)/shard_map/ppermute | solution.py:54
  64.4 34.8 %collective-permute-start.21 = (bf16[128,1536]{1,0:T(8,128)(2,1)}, bf16[128,1536]{1,0:T(8,128)(2,1)}, u32[]{:S(2)}, u32[]{:S(2)}) collective-permute-start(bf16[128,1536]{1,0:T(8,128)(2,1)} %get-tuple-element.154), channel_id=1, source_target_pairs={{0,24},{4,28},{8,16},{12,20},{16,8},{20,12},{24,0},{28,4},{1,25},{... | collective-permute-start | bytes 1179656 | tf_op jit(solution)/shard_map/ppermute | solution.py:60
  75.6 7.1 %collective-permute-start.7 = (f32[4,128]{1,0:T(4,128)}, f32[4,128]{1,0:T(4,128)S(1)}, u32[]{:S(2)}, u32[]{:S(2)}) collective-permute-start(f32[4,128]{1,0:T(4,128)} %bitcast.102), channel_id=1, source_target_pairs={{0,3},{1,0},{2,1},{3,2},{4,7},{5,4},{6,5},{7,6},{8,11},{9,8},{10,9... | collective-permute-start | bytes 6152 | tf_op jit(solution)/shard_map/ppermute | solution.py:261
  90.8 11.1 %collective-permute-start.20 = (bf16[128,1536]{1,0:T(8,128)(2,1)}, bf16[128,1536]{1,0:T(8,128)(2,1)S(1)}, u32[]{:S(2)}, u32[]{:S(2)}) collective-permute-start(bf16[128,1536]{1,0:T(8,128)(2,1)} %get-tuple-element.154), channel_id=1, source_target_pairs={{0,16},{4,20},{8,24},{12,28},{16,0},{20,4},{24,8},{28,12},{1,17},{... | collective-permute-start | bytes 1179656 | tf_op jit(solution)/shard_map/ppermute | solution.py:60
  97.2 18.8 %collective-permute-start.10 = (bf16[128,1024]{1,0:T(8,128)(2,1)}, bf16[128,1024]{1,0:T(8,128)(2,1)S(1)}, u32[]{:S(2)}, u32[]{:S(2)}) collective-permute-start(bf16[128,1024]{1,0:T(8,128)(2,1)} %get-tuple-element.139), channel_id=1, source_target_pairs={{0,1},{1,2},{2,3},{3,0},{4,5},{5,6},{6,7},{7,4},{8,9},{9,10},{10,1... | collective-permute-start | bytes 786440 | tf_op jit(solution)/shard_map/ppermute | solution.py:252
  99.2 19.5 %collective-permute-start.11 = (bf16[128,1024]{1,0:T(8,128)(2,1)}, bf16[128,1024]{1,0:T(8,128)(2,1)S(1)}, u32[]{:S(2)}, u32[]{:S(2)}) collective-permute-start(bf16[128,1024]{1,0:T(8,128)(2,1)} %get-tuple-element.140), channel_id=1, source_target_pairs={{0,2},{1,3},{2,0},{3,1},{4,6},{5,7},{6,4},{7,5},{8,10},{9,11},{10,... | collective-permute-start | bytes 786440 | tf_op jit(solution)/shard_map/ppermute | solution.py:252
  101.9 22.2 %collective-permute-start.12 = (bf16[128,1024]{1,0:T(8,128)(2,1)}, bf16[128,1024]{1,0:T(8,128)(2,1)S(1)}, u32[]{:S(2)}, u32[]{:S(2)}) collective-permute-start(bf16[128,1024]{1,0:T(8,128)(2,1)} %get-tuple-element.141), channel_id=1, source_target_pairs={{0,3},{1,0},{2,1},{3,2},{4,7},{5,4},{6,5},{7,6},{8,11},{9,8},{10,9... | collective-permute-start | bytes 786440 | tf_op jit(solution)/shard_map/ppermute | solution.py:252
  103.0 39.1 %collective-permute-start.22 = (bf16[512,1536]{1,0:T(8,128)(2,1)S(1)}, bf16[512,1536]{1,0:T(8,128)(2,1)S(1)}, u32[]{:S(2)}, u32[]{:S(2)}) collective-permute-start(bf16[512,1536]{1,0:T(8,128)(2,1)S(1)} %constant_dynamic-update-slice_fusion.8.refs_5_.w0_ref), channel_id=1, source_target_pairs={{0,4},{4,0},{8,12},{12,8},{16,20},{20,16},{24,28},{28,24},{1,5},{5... | collective-permute-start | bytes 4718600 | tf_op jit(solution)/shard_map/ppermute | solution.py:60
  124.7 7.5 %collective-permute-start.16 = (bf16[128,1024]{1,0:T(8,128)(2,1)S(1)}, bf16[128,1024]{1,0:T(8,128)(2,1)S(1)}, u32[]{:S(2)}, u32[]{:S(2)}) collective-permute-start(bf16[128,1024]{1,0:T(8,128)(2,1)S(1)} %multiply_convert_fusion.refs_0_), channel_id=1, source_target_pairs={{0,1},{1,2},{2,3},{3,0},{4,5},{5,6},{6,7},{7,4},{8,9},{9,10},{10,1... | collective-permute-start | bytes 786440 | tf_op jit(solution)/shard_map/ppermute | solution.py:41
  155.9 11.0 %collective-permute-start.23 = (bf16[128,1024]{1,0:T(8,128)(2,1)}, bf16[128,1024]{1,0:T(8,128)(2,1)}, u32[]{:S(2)}, u32[]{:S(2)}) collective-permute-start(bf16[128,1024]{1,0:T(8,128)(2,1)} %get-tuple-element.156), channel_id=1, source_target_pairs={{0,1},{1,2},{2,3},{3,0},{4,5},{5,6},{6,7},{7,4},{8,9},{9,10},{10,1... | collective-permute-start | bytes 786440 | tf_op jit(solution)/shard_map/ppermute | solution.py:252
  156.5 23.5 %collective-permute-start.24 = (bf16[128,1024]{1,0:T(8,128)(2,1)}, bf16[128,1024]{1,0:T(8,128)(2,1)S(1)}, u32[]{:S(2)}, u32[]{:S(2)}) collective-permute-start(bf16[128,1024]{1,0:T(8,128)(2,1)} %get-tuple-element.157), channel_id=1, source_target_pairs={{0,2},{1,3},{2,0},{3,1},{4,6},{5,7},{6,4},{7,5},{8,10},{9,11},{10,... | collective-permute-start | bytes 786440 | tf_op jit(solution)/shard_map/ppermute | solution.py:252
  161.4 22.9 %collective-permute-start.25 = (bf16[128,1024]{1,0:T(8,128)(2,1)}, bf16[128,1024]{1,0:T(8,128)(2,1)S(1)}, u32[]{:S(2)}, u32[]{:S(2)}) collective-permute-start(bf16[128,1024]{1,0:T(8,128)(2,1)} %get-tuple-element.158), channel_id=1, source_target_pairs={{0,3},{1,0},{2,1},{3,2},{4,7},{5,4},{6,5},{7,6},{8,11},{9,8},{10,9... | collective-permute-start | bytes 786440 | tf_op jit(solution)/shard_map/ppermute | solution.py:252
  187.6 7.9 %collective-permute-start.27 = (bf16[128,1024]{1,0:T(8,128)(2,1)S(1)}, bf16[128,1024]{1,0:T(8,128)(2,1)S(1)}, u32[]{:S(2)}, u32[]{:S(2)}) collective-permute-start(bf16[128,1024]{1,0:T(8,128)(2,1)S(1)} %fusion.11.refs_0_), channel_id=1, source_target_pairs={{0,1},{1,2},{2,3},{3,0},{4,5},{5,6},{6,7},{7,4},{8,9},{9,10},{10,1... | collective-permute-start | bytes 786440 | tf_op jit(solution)/shard_map/ppermute | solution.py:41
  195.4 6.9 %collective-permute-start.28 = (bf16[128,1024]{1,0:T(8,128)(2,1)S(1)}, bf16[128,1024]{1,0:T(8,128)(2,1)S(1)}, u32[]{:S(2)}, u32[]{:S(2)}) collective-permute-start(bf16[128,1024]{1,0:T(8,128)(2,1)S(1)} %collective-permute-done.27.refs_1_), channel_id=1, source_target_pairs={{0,1},{1,2},{2,3},{3,0},{4,5},{5,6},{6,7},{7,4},{8,9},{9,10},{10,1... | collective-permute-start | bytes 786440 | tf_op jit(solution)/shard_map/ppermute | solution.py:41
  214.2 11.0 %collective-permute-start.32 = (f32[4,128]{1,0:T(4,128)}, f32[4,128]{1,0:T(4,128)S(1)}, u32[]{:S(2)}, u32[]{:S(2)}) collective-permute-start(f32[4,128]{1,0:T(4,128)} %bitcast.106), channel_id=1, source_target_pairs={{0,1},{1,2},{2,3},{3,0},{4,5},{5,6},{6,7},{7,4},{8,9},{9,10},{10,1... | collective-permute-start | bytes 6152 | tf_op jit(solution)/shard_map/ppermute | solution.py:261
  214.8 10.4 %collective-permute-start.31 = (f32[4,128]{1,0:T(4,128)}, f32[4,128]{1,0:T(4,128)S(1)}, u32[]{:S(2)}, u32[]{:S(2)}) collective-permute-start(f32[4,128]{1,0:T(4,128)} %bitcast.107), channel_id=1, source_target_pairs={{0,2},{1,3},{2,0},{3,1},{4,6},{5,7},{6,4},{7,5},{8,10},{9,11},{10,... | collective-permute-start | bytes 6152 | tf_op jit(solution)/shard_map/ppermute | solution.py:261
  239.2 34.4 %collective-permute-start.42 = (bf16[512,1920]{1,0:T(8,128)(2,1)}, bf16[512,1920]{1,0:T(8,128)(2,1)}, u32[]{:S(2)}, u32[]{:S(2)}) collective-permute-start(bf16[512,1920]{1,0:T(8,128)(2,1)} %shard_map.370), channel_id=1, source_target_pairs={{0,4},{4,0},{8,12},{12,8},{16,20},{20,16},{24,28},{28,24},{1,5},{5... | collective-permute-start | bytes 5898248 | tf_op jit(solution)/shard_map/ppermute | solution.py:60
  239.3 12.3 %collective-permute-start.33 = (bf16[128,1536]{1,0:T(8,128)(2,1)}, bf16[128,1536]{1,0:T(8,128)(2,1)S(1)}, u32[]{:S(2)}, u32[]{:S(2)}) collective-permute-start(bf16[128,1536]{1,0:T(8,128)(2,1)} %get-tuple-element.163), channel_id=1, source_target_pairs={{0,8},{4,12},{8,0},{12,4},{16,24},{20,28},{24,16},{28,20},{1,9},{5... | collective-permute-start | bytes 1179656 | tf_op jit(solution)/shard_map/ppermute | solution.py:60
  239.9 11.9 %collective-permute-start.34 = (bf16[128,1536]{1,0:T(8,128)(2,1)}, bf16[128,1536]{1,0:T(8,128)(2,1)S(1)}, u32[]{:S(2)}, u32[]{:S(2)}) collective-permute-start(bf16[128,1536]{1,0:T(8,128)(2,1)} %get-tuple-element.164), channel_id=1, source_target_pairs={{0,16},{4,20},{8,24},{12,28},{16,0},{20,4},{24,8},{28,12},{1,17},{... | collective-permute-start | bytes 1179656 | tf_op jit(solution)/shard_map/ppermute | solution.py:60
  241.3 18.4 %collective-permute-start.35 = (bf16[128,1536]{1,0:T(8,128)(2,1)S(1)}, bf16[128,1536]{1,0:T(8,128)(2,1)S(1)}, u32[]{:S(2)}, u32[]{:S(2)}) collective-permute-start(bf16[128,1536]{1,0:T(8,128)(2,1)S(1)} %copy-done.55), channel_id=1, source_target_pairs={{0,24},{4,28},{8,16},{12,20},{16,8},{20,12},{24,0},{28,4},{1,25},{... | collective-permute-start | bytes 1179656 | tf_op jit(solution)/shard_map/ppermute | solution.py:60
  259.9 10.7 %collective-permute-start.36 = (bf16[128,1536]{1,0:T(8,128)(2,1)S(1)}, bf16[128,1536]{1,0:T(8,128)(2,1)}, u32[]{:S(2)}, u32[]{:S(2)}) collective-permute-start(bf16[128,1536]{1,0:T(8,128)(2,1)S(1)} %add_convert_fusion.1.refs_0_), channel_id=1, source_target_pairs={{0,1},{1,2},{2,3},{3,0},{4,5},{5,6},{6,7},{7,4},{8,9},{9,10},{10,1... | collective-permute-start | bytes 1179656 | tf_op jit(solution)/shard_map/ppermute | solution.py:41
  270.6 32.9 %collective-permute-start.37 = (bf16[128,1536]{1,0:T(8,128)(2,1)}, bf16[128,1536]{1,0:T(8,128)(2,1)}, u32[]{:S(2)}, u32[]{:S(2)}) collective-permute-start(bf16[128,1536]{1,0:T(8,128)(2,1)} %collective-permute-done.36.refs_1_), channel_id=1, source_target_pairs={{0,1},{1,2},{2,3},{3,0},{4,5},{5,6},{6,7},{7,4},{8,9},{9,10},{10,1... | collective-permute-start | bytes 1179656 | tf_op jit(solution)/shard_map/ppermute | solution.py:41
  278.5 14.3 %collective-permute-start.43 = (bf16[128,1920]{1,0:T(8,128)(2,1)}, bf16[128,1920]{1,0:T(8,128)(2,1)S(1)}, u32[]{:S(2)}, u32[]{:S(2)}) collective-permute-start(bf16[128,1920]{1,0:T(8,128)(2,1)} %get-tuple-element.190), channel_id=1, source_target_pairs={{0,8},{4,12},{8,0},{12,4},{16,24},{20,28},{24,16},{28,20},{1,9},{5... | collective-permute-start | bytes 1474568 | tf_op jit(solution)/shard_map/ppermute | solution.py:60
  279.8 21.7 %collective-permute-start.44 = (bf16[128,1920]{1,0:T(8,128)(2,1)}, bf16[128,1920]{1,0:T(8,128)(2,1)S(1)}, u32[]{:S(2)}, u32[]{:S(2)}) collective-permute-start(bf16[128,1920]{1,0:T(8,128)(2,1)} %get-tuple-element.191), channel_id=1, source_target_pairs={{0,16},{4,20},{8,24},{12,28},{16,0},{20,4},{24,8},{28,12},{1,17},{... | collective-permute-start | bytes 1474568 | tf_op jit(solution)/shard_map/ppermute | solution.py:60
  280.4 21.2 %collective-permute-start.45 = (bf16[128,1920]{1,0:T(8,128)(2,1)}, bf16[128,1920]{1,0:T(8,128)(2,1)}, u32[]{:S(2)}, u32[]{:S(2)}) collective-permute-start(bf16[128,1920]{1,0:T(8,128)(2,1)} %get-tuple-element.192), channel_id=1, source_target_pairs={{0,24},{4,28},{8,16},{12,20},{16,8},{20,12},{24,0},{28,4},{1,25},{... | collective-permute-start | bytes 1474568 | tf_op jit(solution)/shard_map/ppermute | solution.py:60
  302.9 31.2 %collective-permute-start.46 = (bf16[128,1920]{1,0:T(8,128)(2,1)S(1)}, bf16[128,1920]{1,0:T(8,128)(2,1)}, u32[]{:S(2)}, u32[]{:S(2)}) collective-permute-start(bf16[128,1920]{1,0:T(8,128)(2,1)S(1)} %add_convert_fusion.refs_0_), channel_id=1, source_target_pairs={{0,1},{1,2},{2,3},{3,0},{4,5},{5,6},{6,7},{7,4},{8,9},{9,10},{10,1... | collective-permute-start | bytes 1474568 | tf_op jit(solution)/shard_map/ppermute | solution.py:41
  303.5 58.5 %collective-permute-start.38 = (bf16[128,1536]{1,0:T(8,128)(2,1)}, bf16[128,1536]{1,0:T(8,128)(2,1)S(1)}, u32[]{:S(2)}, u32[]{:S(2)}) collective-permute-start(bf16[128,1536]{1,0:T(8,128)(2,1)} %collective-permute-done.37.refs_2_), channel_id=1, source_target_pairs={{0,1},{1,2},{2,3},{3,0},{4,5},{5,6},{6,7},{7,4},{8,9},{9,10},{10,1... | collective-permute-start | bytes 1179656 | tf_op jit(solution)/shard_map/ppermute | solution.py:41
  309.1 21.2 %collective-permute-start.49 = (f32[104,128]{1,0:T(8,128)S(1)}, f32[104,128]{1,0:T(8,128)S(1)}, u32[]{:S(2)}, u32[]{:S(2)}) collective-permute-start(f32[104,128]{1,0:T(8,128)S(1)} %pad.27), channel_id=1, source_target_pairs={{0,3},{1,2},{2,1},{3,0},{4,7},{5,6},{6,5},{7,4},{8,11},{9,10},{10,... | collective-permute-start | bytes 159752 | tf_op jit(solution)/shard_map/ppermute | solution.py:275
  309.4 20.9 %collective-permute-start.48 = (f32[104,128]{1,0:T(8,128)S(1)}, f32[104,128]{1,0:T(8,128)S(1)}, u32[]{:S(2)}, u32[]{:S(2)}) collective-permute-start(f32[104,128]{1,0:T(8,128)S(1)} %pad.27), channel_id=1, source_target_pairs={{0,2},{1,3},{2,0},{3,1},{4,6},{5,7},{6,4},{7,5},{8,10},{9,11},{10,... | collective-permute-start | bytes 159752 | tf_op jit(solution)/shard_map/ppermute | solution.py:275
  309.9 20.5 %collective-permute-start.47 = (f32[104,128]{1,0:T(8,128)S(1)}, f32[104,128]{1,0:T(8,128)S(1)}, u32[]{:S(2)}, u32[]{:S(2)}) collective-permute-start(f32[104,128]{1,0:T(8,128)S(1)} %pad.27), channel_id=1, source_target_pairs={{0,1},{1,0},{2,3},{3,2},{4,5},{5,4},{6,7},{7,6},{8,9},{9,8},{10,11... | collective-permute-start | bytes 159752 | tf_op jit(solution)/shard_map/ppermute | solution.py:275
  330.3 16.3 %collective-permute-start.39 = (bf16[128,1024]{1,0:T(8,128)(2,1)}, bf16[128,1024]{1,0:T(8,128)(2,1)S(1)}, u32[]{:S(2)}, u32[]{:S(2)}) collective-permute-start(bf16[128,1024]{1,0:T(8,128)(2,1)} %get-tuple-element.186), channel_id=1, source_target_pairs={{0,1},{1,2},{2,3},{3,0},{4,5},{5,6},{6,7},{7,4},{8,9},{9,10},{10,1... | collective-permute-start | bytes 786440 | tf_op jit(solution)/shard_map/ppermute | solution.py:252
  330.3 23.8 %collective-permute-start.40 = (bf16[128,1024]{1,0:T(8,128)(2,1)}, bf16[128,1024]{1,0:T(8,128)(2,1)S(1)}, u32[]{:S(2)}, u32[]{:S(2)}) collective-permute-start(bf16[128,1024]{1,0:T(8,128)(2,1)} %get-tuple-element.187), channel_id=1, source_target_pairs={{0,2},{1,3},{2,0},{3,1},{4,6},{5,7},{6,4},{7,5},{8,10},{9,11},{10,... | collective-permute-start | bytes 786440 | tf_op jit(solution)/shard_map/ppermute | solution.py:252
  331.6 30.4 %collective-permute-start.41 = (bf16[128,1024]{1,0:T(8,128)(2,1)}, bf16[128,1024]{1,0:T(8,128)(2,1)S(1)}, u32[]{:S(2)}, u32[]{:S(2)}) collective-permute-start(bf16[128,1024]{1,0:T(8,128)(2,1)} %get-tuple-element.188), channel_id=1, source_target_pairs={{0,3},{1,0},{2,1},{3,2},{4,7},{5,4},{6,5},{7,6},{8,11},{9,8},{10,9... | collective-permute-start | bytes 786440 | tf_op jit(solution)/shard_map/ppermute | solution.py:252
  334.0 38.3 %collective-permute-start.50 = (bf16[128,1920]{1,0:T(8,128)(2,1)}, bf16[128,1920]{1,0:T(8,128)(2,1)}, u32[]{:S(2)}, u32[]{:S(2)}) collective-permute-start(bf16[128,1920]{1,0:T(8,128)(2,1)} %collective-permute-done.46.refs_1_), channel_id=1, source_target_pairs={{0,1},{1,2},{2,3},{3,0},{4,5},{5,6},{6,7},{7,4},{8,9},{9,10},{10,1... | collective-permute-start | bytes 1474568 | tf_op jit(solution)/shard_map/ppermute | solution.py:41
  362.0 11.8 %collective-permute-start.53 = (bf16[128,1024]{1,0:T(8,128)(2,1)}, bf16[128,1024]{1,0:T(8,128)(2,1)S(1)}, u32[]{:S(2)}, u32[]{:S(2)}) collective-permute-start(bf16[128,1024]{1,0:T(8,128)(2,1)} %get-tuple-element.209), channel_id=1, source_target_pairs={{0,1},{1,2},{2,3},{3,0},{4,5},{5,6},{6,7},{7,4},{8,9},{9,10},{10,1... | collective-permute-start | bytes 786440 | tf_op jit(solution)/shard_map/ppermute | solution.py:252
  362.1 23.9 %collective-permute-start.54 = (bf16[128,1024]{1,0:T(8,128)(2,1)}, bf16[128,1024]{1,0:T(8,128)(2,1)S(1)}, u32[]{:S(2)}, u32[]{:S(2)}) collective-permute-start(bf16[128,1024]{1,0:T(8,128)(2,1)} %get-tuple-element.210), channel_id=1, source_target_pairs={{0,2},{1,3},{2,0},{3,1},{4,6},{5,7},{6,4},{7,5},{8,10},{9,11},{10,... | collective-permute-start | bytes 786440 | tf_op jit(solution)/shard_map/ppermute | solution.py:252
  362.2 33.3 %collective-permute-start.55 = (bf16[128,1024]{1,0:T(8,128)(2,1)}, bf16[128,1024]{1,0:T(8,128)(2,1)S(1)}, u32[]{:S(2)}, u32[]{:S(2)}) collective-permute-start(bf16[128,1024]{1,0:T(8,128)(2,1)} %get-tuple-element.211), channel_id=1, source_target_pairs={{0,3},{1,0},{2,1},{3,2},{4,7},{5,4},{6,5},{7,6},{8,11},{9,8},{10,9... | collective-permute-start | bytes 786440 | tf_op jit(solution)/shard_map/ppermute | solution.py:252
  372.3 31.6 %collective-permute-start.56 = (bf16[128,1920]{1,0:T(8,128)(2,1)}, bf16[128,1920]{1,0:T(8,128)(2,1)}, u32[]{:S(2)}, u32[]{:S(2)}) collective-permute-start(bf16[128,1920]{1,0:T(8,128)(2,1)} %collective-permute-done.50.refs_2_), channel_id=1, source_target_pairs={{0,1},{1,2},{2,3},{3,0},{4,5},{5,6},{6,7},{7,4},{8,9},{9,10},{10,1... | collective-permute-start | bytes 1474568 | tf_op jit(solution)/shard_map/ppermute | solution.py:41
  (69 other events, 1234.1 us)
